TPU v7x, 32 devices: a whole 2x2x4 slice. The times are simulated.
32 devices in a mesh: rep: 8 (over y, x, core), shard: 4 (over z).
Axes of the slice: x: 2, y: 2, z: 4, core: 2. Of those that a mesh axis runs over, the one named last changes fastest.
Arguments:
- tokens: bfloat16 [8, 1024, 2048], P('rep', 'shard'), may hold values from -6 to 6
- segments: int32 [8, 1024], P('rep'), may hold values from 0 to 15, as said below
- positions: int32 [8, 1024], P('rep', 'shard'), may hold values from 0 to 1023, as said below
- norm_gain: bfloat16 [2048], P('shard'), may hold values from 0.5 to 1.5
- norm_shift: bfloat16 [2048], P('shard'), may hold values from -1.75 to 1.75
- inproj_weight: bfloat16 [6144, 2048], P('shard'), may hold values from -0.125 to 0.125
- inproj_bias: bfloat16 [6144], P('shard'), may hold values from -3 to 3
- outproj_weight: bfloat16 [2048, 2048], P('shard'), may hold values from -0.75 to 0.75
- outproj_bias: bfloat16 [2048], P('shard'), may hold values from -3 to 3
- expand_weight: bfloat16 [8192, 2048], P('shard'), may hold values from -0.125 to 0.125
- expand_bias: bfloat16 [8192], P('shard'), may hold values from -3 to 3
- shrink_weight: bfloat16 [2048, 8192], P('shard'), may hold values from -0.0625 to 0.0625
- shrink_bias: bfloat16 [2048], P('shard'), may hold values from -3 to 3
- out_grad: bfloat16 [8, 1024, 2048], P('rep', 'shard'), may hold values from -6 to 6
Outputs:
- block_output: bfloat16 [8, 1024, 2048], P('rep', 'shard')
- token_grad: float32 [8, 1024, 2048], P('rep', 'shard')
- grad_gain: float32 [2048], P('shard')
- grad_shift: float32 [2048], P('shard')
- grad_inproj: float32 [6144, 2048], P('shard')
- grad_inbias: float32 [6144], P('shard')
- grad_outproj: float32 [2048, 2048], P('shard')
- grad_outbias: float32 [2048], P('shard')
- grad_expand: float32 [8192, 2048], P('shard')
- grad_expbias: float32 [8192], P('shard')
- grad_shrink: float32 [2048, 8192], P('shard')
- grad_shrbias: float32 [2048], P('shard')
Inputs may be any that keep to these rules, and one draw needn't show every extreme that they name: `segments`: along each row the document numbers start at 0 and never fall; a document starts only at a multiple of 64 positions. `positions`: each token's offset from the first token of its document.
All inputs are finite; a program needn't handle non-finite values.
Results may differ from a plain program's by a relative error of at most 0.011.
Values may be sent and summed in bfloat16 or wider, within the bound.
No kernel may reach another device: no remote copies, remote signals or barrier semaphores. Data moves between devices by JAX's collectives and lax.ppermute only.
A program may use at most 640 MiB of HBM per device.

v0:
```python
import math

import jax
import jax.numpy as jnp
from jax import lax
from jax.sharding import PartitionSpec as P

HEAD_DIM = 64
ROT = 32


def project(values, weight):
    return lax.dot_general(
        values, weight, (((1,), (1,)), ((), ())), preferred_element_type=jnp.float32
    )


def gelu_tanh(values):
    return (
        0.5
        * values
        * (
            1.0
            + jnp.tanh(math.sqrt(2.0 / math.pi) * (values + 0.044715 * values * values * values))
        )
    )


def rotate(values, cosine, sine):
    rot_half = ROT // 2
    first_part = values[..., :rot_half]
    second_part = values[..., rot_half:ROT]
    return jnp.concatenate(
        [
            first_part * cosine - second_part * sine,
            second_part * cosine + first_part * sine,
            values[..., ROT:],
        ],
        -1,
    )


def split_heads(values, group_size):
    rows_here, span, head_count, head_size = values.shape
    grouped = values.reshape(rows_here, span, head_count // group_size, group_size, head_size)
    return jnp.transpose(grouped, (2, 0, 1, 3, 4))


def join_heads(values):
    group_count, rows_here, span, group_size, head_size = values.shape
    return jnp.transpose(values, (1, 2, 0, 3, 4)).reshape(
        rows_here, span, group_count * group_size * head_size
    )


def local(
    tokens,
    segments,
    positions,
    norm_gain,
    norm_shift,
    inproj_weight,
    inproj_bias,
    outproj_weight,
    outproj_bias,
    expand_weight,
    expand_bias,
    shrink_weight,
    shrink_bias,
    out_grad,
):
    batch_rows, local_span, model_width = tokens.shape
    token_count = batch_rows * local_span
    head_count = model_width // HEAD_DIM
    group_size = math.gcd(head_count, 8)
    score_scale = HEAD_DIM ** (-0.5)
    gathered = (
        lax.all_gather(norm_gain, "shard", axis=0, tiled=True),
        lax.all_gather(norm_shift, "shard", axis=0, tiled=True),
        lax.all_gather(inproj_weight, "shard", axis=0, tiled=True),
        lax.all_gather(inproj_bias, "shard", axis=0, tiled=True),
        lax.all_gather(outproj_weight, "shard", axis=0, tiled=True),
        lax.all_gather(outproj_bias, "shard", axis=0, tiled=True),
        lax.all_gather(expand_weight, "shard", axis=0, tiled=True),
        lax.all_gather(expand_bias, "shard", axis=0, tiled=True),
        lax.all_gather(shrink_weight, "shard", axis=0, tiled=True),
        lax.all_gather(shrink_bias, "shard", axis=0, tiled=True),
    )
    (
        gain_broadcast,
        shift_broadcast,
        inproj_full,
        inbias_full,
        outproj_full,
        outbias_full,
        expand_full,
        expbias_full,
        shrink_full,
        shrbias_full,
    ) = gathered
    residual = tokens.reshape(token_count, model_width).astype(jnp.float32)
    row_mean = jnp.mean(residual, -1, keepdims=True)
    centered_rows = residual - row_mean
    row_var = jnp.mean(centered_rows * centered_rows, -1, keepdims=True)
    inverse_deviation = lax.rsqrt(row_var + 1e-05)
    standardized_input = centered_rows * inverse_deviation
    normalized_rows = (
        standardized_input * gain_broadcast.astype(jnp.float32)
        + shift_broadcast.astype(jnp.float32)
    ).astype(jnp.bfloat16)
    mixed = project(normalized_rows, inproj_full) + inbias_full.astype(jnp.float32)
    head_shape = (batch_rows, local_span, head_count, HEAD_DIM)
    queries = mixed[:, :model_width].reshape(head_shape)
    key_part = mixed[:, model_width : 2 * model_width].reshape(head_shape)
    v_low = mixed[:, 2 * model_width :].astype(jnp.bfloat16)
    inverse_freq = 10000.0 ** (-jnp.arange(ROT // 2).astype(jnp.float32) * 2.0 / ROT)
    angle = positions.astype(jnp.float32)[:, :, None, None] * inverse_freq[None, None, None, :]
    cosine = jnp.cos(angle)
    sine = jnp.sin(angle)
    q_rot = rotate(queries, cosine, sine).astype(jnp.bfloat16)
    k_rot = rotate(key_part, cosine, sine).astype(jnp.bfloat16)
    key_all, value_all = (
        lax.all_gather(
            k_rot.reshape(batch_rows, local_span, model_width), "shard", axis=1, tiled=True
        ),
        lax.all_gather(
            v_low.reshape(batch_rows, local_span, model_width), "shard", axis=1, tiled=True
        ),
    )
    length = key_all.shape[1]
    key_groups = split_heads(key_all.reshape(batch_rows, length, head_count, HEAD_DIM), group_size)
    value_groups = split_heads(
        value_all.reshape(batch_rows, length, head_count, HEAD_DIM), group_size
    )
    query_groups = split_heads(q_rot, group_size)
    first_pos = lax.axis_index("shard") * local_span
    query_places = first_pos + jnp.arange(local_span)
    key_places = jnp.arange(length)
    query_segments = lax.dynamic_slice_in_dim(segments, first_pos, local_span, 1)
    allowed = (key_places[None, None, :] <= query_places[None, :, None]) & (
        segments[:, None, :] == query_segments[:, :, None]
    )

    def scores_of(query_block, key_block):
        raw_scores = (
            jnp.einsum(
                "rqhd,rkhd->rhqk", query_block, key_block, preferred_element_type=jnp.float32
            )
            * score_scale
        )
        return jnp.where(allowed[:, None], raw_scores, -1e30)

    def attend_group(packed):
        query_block, key_block, value_block = packed
        scores = scores_of(query_block, key_block)
        row_max = jnp.max(scores, -1, keepdims=True)
        log_block = row_max + jnp.log(jnp.sum(jnp.exp(scores - row_max), -1, keepdims=True))
        probs = jnp.exp(scores - log_block)
        out_block = jnp.einsum(
            "rhqk,rkhd->rqhd",
            probs.astype(jnp.bfloat16),
            value_block,
            preferred_element_type=jnp.float32,
        )
        return (out_block, log_block)

    attended_groups, log_total = lax.map(attend_group, (query_groups, key_groups, value_groups))
    attended = join_heads(attended_groups).reshape(token_count, model_width).astype(jnp.bfloat16)
    expanded = project(normalized_rows, expand_full) + expbias_full.astype(jnp.float32)
    hidden = gelu_tanh(expanded).astype(jnp.bfloat16)
    branches = (
        project(attended, outproj_full)
        + outbias_full.astype(jnp.float32)
        + project(hidden, shrink_full)
        + shrbias_full.astype(jnp.float32)
    )
    block_output = (
        (residual + branches).reshape(batch_rows, local_span, model_width).astype(jnp.bfloat16)
    )
    gain_back, inproj_back, outproj_back, expand_back, shrink_back = (
        lax.all_gather(norm_gain, "shard", axis=0, tiled=True),
        lax.all_gather(inproj_weight, "shard", axis=0, tiled=True),
        lax.all_gather(outproj_weight, "shard", axis=0, tiled=True),
        lax.all_gather(expand_weight, "shard", axis=0, tiled=True),
        lax.all_gather(shrink_weight, "shard", axis=0, tiled=True),
    )
    grad_rows = out_grad.reshape(token_count, model_width)
    d_att = jnp.dot(grad_rows, outproj_back, preferred_element_type=jnp.float32).astype(
        jnp.bfloat16
    )
    d_hidden = jnp.dot(grad_rows, shrink_back, preferred_element_type=jnp.float32)
    gelu_grad = jax.vjp(gelu_tanh, expanded)[1](d_hidden)[0]
    d_up = gelu_grad.astype(jnp.bfloat16)
    d_att_groups = split_heads(d_att.reshape(head_shape), group_size)

    def backward_group(packed):
        query_block, key_block, value_block, grad_block, log_block = packed
        probs = jnp.exp(scores_of(query_block, key_block) - log_block)
        d_probs = jnp.einsum(
            "rqhd,rkhd->rhqk", grad_block, value_block, preferred_element_type=jnp.float32
        )
        row_delta = jnp.sum(probs * d_probs, -1, keepdims=True)
        d_scores = (probs * (d_probs - row_delta)).astype(jnp.bfloat16)
        query_terms = (
            jnp.einsum("rhqk,rkhd->rqhd", d_scores, key_block, preferred_element_type=jnp.float32)
            * score_scale
        )
        key_block_terms = (
            jnp.einsum("rhqk,rqhd->rkhd", d_scores, query_block, preferred_element_type=jnp.float32)
            * score_scale
        )
        value_block_terms = jnp.einsum(
            "rhqk,rqhd->rkhd",
            probs.astype(jnp.bfloat16),
            grad_block,
            preferred_element_type=jnp.float32,
        )
        return (query_terms, key_block_terms, value_block_terms)

    query_parts, key_parts, value_parts = lax.map(
        backward_group, (query_groups, key_groups, value_groups, d_att_groups, log_total)
    )
    d_query = join_heads(query_parts).reshape(head_shape)
    key_terms = join_heads(key_parts)
    value_terms = join_heads(value_parts)
    d_key, d_value = (
        lax.psum_scatter(key_terms, "shard", scatter_dimension=1, tiled=True),
        lax.psum_scatter(value_terms, "shard", scatter_dimension=1, tiled=True),
    )
    d_query = rotate(d_query, cosine, -sine).reshape(token_count, model_width)
    d_key = rotate(d_key.reshape(head_shape), cosine, -sine).reshape(token_count, model_width)
    d_mixed = jnp.concatenate(
        [d_query, d_key, d_value.reshape(token_count, model_width)], 1
    ).astype(jnp.bfloat16)
    normalized_gradient = jnp.dot(
        d_mixed, inproj_back, preferred_element_type=jnp.float32
    ) + jnp.dot(d_up, expand_back, preferred_element_type=jnp.float32)
    standardized_gradient = normalized_gradient * gain_back.astype(jnp.float32)
    token_grad = grad_rows.astype(jnp.float32) + inverse_deviation * (
        standardized_gradient
        - jnp.mean(standardized_gradient, -1, keepdims=True)
        - standardized_input
        * jnp.mean(standardized_gradient * standardized_input, -1, keepdims=True)
    )
    token_grad = token_grad.reshape(batch_rows, local_span, model_width)
    small_sums = (
        lax.psum_scatter(
            jnp.sum(normalized_gradient * standardized_input, 0),
            "shard",
            scatter_dimension=0,
            tiled=True,
        ),
        lax.psum_scatter(jnp.sum(normalized_gradient, 0), "shard", scatter_dimension=0, tiled=True),
        lax.psum_scatter(
            jnp.sum(d_mixed, 0, dtype=jnp.float32), "shard", scatter_dimension=0, tiled=True
        ),
        lax.psum_scatter(
            jnp.sum(grad_rows, 0, dtype=jnp.float32), "shard", scatter_dimension=0, tiled=True
        ),
        lax.psum_scatter(
            jnp.sum(d_up, 0, dtype=jnp.float32), "shard", scatter_dimension=0, tiled=True
        ),
    )

    def owned(outputs, inputs):
        return lax.psum_scatter(
            lax.dot_general(
                outputs, inputs, (((0,), (0,)), ((), ())), preferred_element_type=jnp.float32
            ),
            "shard",
            scatter_dimension=0,
            tiled=True,
        )

    inproj_part = owned(d_mixed, normalized_rows)
    outproj_part = owned(grad_rows, attended)
    expand_part = owned(d_up, normalized_rows)
    shrink_part = owned(grad_rows, hidden)
    totals = lax.psum(
        (
            small_sums[0],
            small_sums[1],
            inproj_part,
            small_sums[2],
            outproj_part,
            small_sums[3],
            expand_part,
            small_sums[4],
            shrink_part,
        ),
        "rep",
    )
    shrink_bias_grad = totals[5]
    return (
        block_output,
        token_grad,
        totals[0],
        totals[1],
        totals[2],
        totals[3],
        totals[4],
        totals[5],
        totals[6],
        totals[7],
        totals[8],
        shrink_bias_grad,
    )


def solution(mesh):
    in_specs = (
        P("rep", "shard", None),
        P("rep", None),
        P("rep", "shard"),
        P("shard"),
        P("shard"),
        P("shard", None),
        P("shard"),
        P("shard", None),
        P("shard"),
        P("shard", None),
        P("shard"),
        P("shard", None),
        P("shard"),
        P("rep", "shard", None),
    )
    out_specs = (
        P("rep", "shard", None),
        P("rep", "shard", None),
        P("shard"),
        P("shard"),
        P("shard", None),
        P("shard"),
        P("shard", None),
        P("shard"),
        P("shard", None),
        P("shard"),
        P("shard", None),
        P("shard"),
    )
    return jax.shard_map(local, mesh=mesh, in_specs=in_specs, out_specs=out_specs, check_vma=False)
```

profile of v0, /device:TPU:0, one launch (start us, length us, event | category | flops | bytes accessed | tf_op | source)
XLA Modules:
  0.0 6256.9 jit_solution(7079234838396761159)
XLA Ops:
  8.8 13.6 all-gather.2
  22.5 12.1 all-gather.1
  34.6 33.8 all-gather.3
  69.1 368.8 %all-gather.13.cloned.1.call-done = bf16[6144,2048]{1,0:T(8,128)(2,1)} async-done(((bf16[1536,2048]{1,0:T(8,128)(2,1)}), bf16[6144,2048]{1,0:T(8,128)(2,1)}) %all-gather.13.cloned.1.call-update) | async-done | bytes 25165840 | tf_op jit(solution)/shard_map/all_gather | solution.py:80
  437.9 14.3 convolution_add_fusion.1
  452.2 2.7 slice.101
  455.8 4.0 fusion.95
  459.7 2.9 copy.58
  466.6 2.5 subtract_convert_fusion.2
  471.7 115.6 %all-gather.17.cloned.1.call-done = bf16[2048,2048]{1,0:T(8,128)(2,1)} async-done(((bf16[512,2048]{1,0:T(8,128)(2,1)}), bf16[2048,2048]{1,0:T(8,128)(2,1)}) %all-gather.17.cloned.1.call-update) | async-done | bytes 8388624 | tf_op jit(solution)/shard_map/all_gather | solution.py:82
  587.3 6.7 convolution_convert_fusion
  598.0 70.4 %all-gather.23.cloned.1.call-done = bf16[1024,2048]{1,0:T(8,128)(2,1)} async-done(((bf16[256,2048]{1,0:T(8,128)(2,1)}), bf16[1024,2048]{1,0:T(8,128)(2,1)}) %all-gather.23.cloned.1.call-update) | async-done | bytes 4194320 | tf_op jit(solution)/shard_map/all_gather | solution.py:126
  668.4 6.4 copy.53
  674.8 74.7 %all-gather.15.cloned.1.call-done = bf16[1,1024,2048]{1,2,0:T(8,128)(2,1)} async-done(((bf16[1,256,2048]{1,2,0:T(8,128)(2,1)}), bf16[1,1024,2048]{1,2,0:T(8,128)(2,1)}) %all-gather.15.cloned.1.call-update) | async-done | bytes 4194320 | tf_op jit(solution)/shard_map/all_gather | solution.py:123
  749.5 35.1 while.30
  749.8 2.8 fusion.142
  754.8 3.4 fusion.143
  758.6 2.8 fusion.142
  763.6 3.4 fusion.143
  767.3 2.8 fusion.142
  772.4 3.4 fusion.143
  776.1 2.8 fusion.142
  781.2 3.4 fusion.143
  785.6 75.3 %while.31 = (s32[]{:T(128)}, f32[4,1,256,8,64]{2,4,3,1,0:T(8,128)}, f32[4,1,1024,8,64]{2,4,3,1,0:T(8,128)}, f32[4,1,1024,8,64]{2,4,3,1,0:T(8,128)}, bf16[4,1,102...) while((s32[]{:T(128)}, f32[4,1,256,8,64]{2,4,3,1,0:T(8,128)}, ...), condition=%wide.region_8.9_spmd.clone.clone, body=%wide.region_6.8_spmd.clone.sunk.clone | while | flops 1375074304 | bytes 72944768 | solution.py:220
  788.6 3.6 bitcast_dynamic-update-slice_fusion.11
  792.2 4.5 multiply_reduce_fusion.4
  799.0 3.4 fusion.154
  807.4 3.6 bitcast_dynamic-update-slice_fusion.11
  811.0 4.5 multiply_reduce_fusion.4
  817.8 3.4 fusion.154
  826.2 3.6 bitcast_dynamic-update-slice_fusion.11
  829.7 4.5 multiply_reduce_fusion.4
  836.6 3.4 fusion.154
  845.0 3.6 bitcast_dynamic-update-slice_fusion.11
  848.5 4.5 multiply_reduce_fusion.4
  855.3 3.4 fusion.154
  863.8 8.5 convolution_bitcast_fusion.1
  873.9 130.0 %reduce-scatter.9.cloned.1.call-done = f32[1,256,2048]{1,2,0:T(8,128)} async-done(((f32[1,1024,2048]{1,2,0:T(8,128)}), f32[1,256,2048]{1,2,0:T(8,128)}) %reduce-scatter.9.cloned.1.call-update) | async-done | bytes 2097168 | tf_op jit(solution)/shard_map/reduce_scatter | solution.py:227
  1008.7 143.3 %reduce-scatter.11.cloned.1.call-done = f32[1,256,2048]{1,2,0:T(8,128)} async-done(((f32[1,1024,2048]{1,2,0:T(8,128)}), f32[1,256,2048]{1,2,0:T(8,128)}) %reduce-scatter.11.cloned.1.call-update) | async-done | bytes 2097168 | tf_op jit(solution)/shard_map/reduce_scatter | solution.py:228
  1153.7 29.6 fusion.88
  1184.0 38.9 all_gather.50
  1222.9 492.8 %all-gather.19.cloned.1.call-done = bf16[8192,2048]{1,0:T(8,128)(2,1)} async-done(((bf16[2048,2048]{1,0:T(8,128)(2,1)}), bf16[8192,2048]{1,0:T(8,128)(2,1)}) %all-gather.19.cloned.1.call-update) | async-done | bytes 33554448 | tf_op jit(solution)/shard_map/all_gather | solution.py:84
  1715.8 23.1 convolution_add_fusion
  1738.9 28.2 convolution_bitcast_fusion
  1767.2 509.8 %all-gather.21.cloned.1.call-done = bf16[2048,8192]{1,0:T(8,128)(2,1)} async-done(((bf16[512,8192]{1,0:T(8,128)(2,1)}), bf16[2048,8192]{1,0:T(8,128)(2,1)}) %all-gather.21.cloned.1.call-update) | async-done | bytes 33554448 | tf_op jit(solution)/shard_map/all_gather | solution.py:86
  2277.0 24.1 convert_reduce_fusion
  2301.0 25.6 fusion.90
  2326.8 13.5 fusion.89
  2340.2 18.4 fusion.77
  2360.3 3.0 convert_reduce_fusion.2
  2363.4 195.2 %reduce-scatter.15.cloned.1.call-done = f32[512,2048]{0,1:T(8,128)} async-done(((f32[2048,2048]{0,1:T(8,128)}), f32[512,2048]{0,1:T(8,128)}) %reduce-scatter.15.cloned.1.call-update) | async-done | bytes 4194320 | tf_op jit(solution)/shard_map/reduce_scatter | solution.py:266
  2558.6 823.6 %reduce-scatter.13.cloned.1.call-done = f32[1536,2048]{1,0:T(8,128)} async-done(((f32[6144,2048]{1,0:T(8,128)}), f32[1536,2048]{1,0:T(8,128)}) %reduce-scatter.13.cloned.1.call-update) | async-done | bytes 12582928 | tf_op jit(solution)/shard_map/reduce_scatter | solution.py:266
  3382.2 1099.2 %reduce-scatter.17.cloned.1.call-done = f32[512,8192]{0,1:T(8,128)} async-done(((f32[2048,8192]{0,1:T(8,128)}), f32[512,8192]{0,1:T(8,128)}) %reduce-scatter.17.cloned.1.call-update) | async-done | bytes 16777232 | tf_op jit(solution)/shard_map/reduce_scatter | solution.py:266
  4481.4 1098.4 %reduce-scatter.19.cloned.1.call-done = f32[2048,2048]{1,0:T(8,128)} async-done(((f32[8192,2048]{1,0:T(8,128)}), f32[2048,2048]{1,0:T(8,128)}) %reduce-scatter.19.cloned.1.call-update) | async-done | bytes 16777232
  5583.0 12.6 all-gather.5
  5595.6 11.9 all-gather.4
  5607.6 7.1 convolution_add_fusion.4
  5614.7 18.9 fusion.71
  5637.3 24.7 all-reduce.6
  5662.0 541.4 %all-reduce.12.cloned.1.call-done = (f32[1536,2048]{1,0:T(8,128)}, f32[512,2048]{0,1:T(8,128)}, f32[2048,2048]{1,0:T(8,128)}, f32[512,8192]{0,1:T(8,128)}) async-done(((f32[1536,2048]{1,0:T(8,128)}, f32[512,2048]{0,1:T(8,128)}, f32[2048,2048]{1,0:T(8,128)}, f32[512,8192]{0,1:T(8,128)}), (f32[1536,2048]{1,0:T(8,128)}, f32[512,2048]{0,1:T(8,128)}, f32[2048,2048]{1,0:T(8,128)}, ...) | async-done | bytes 50331664 | tf_op jit(solution)/shard_map/psum | solution.py:279
  6203.4 5.3 copy.64
  6208.7 17.4 copy.65
  6226.7 11.5 copy.105
  6238.3 11.8 copy.106
  (167 shorter events, 72.3 us)
Async XLA Ops:
  7.2 1.6 copy-start.24
  7.2 1.6 copy-start.25
  7.2 27.4 copy-start.22
  7.2 61.2 copy-start
  7.2 430.7 %all-gather.13.cloned.1.call-start = ((), (), s32[]{:S(2)}) async-start(), calls=%async_computation.6 | async-start | bytes 31457280 | tf_op jit(solution)/shard_map/all_gather | solution.py:80
  8.0 579.4 %all-gather.17.cloned.1.call-start = ((), (), s32[]{:S(2)}) async-start(), calls=%async_computation.8 | async-start | bytes 10485760 | tf_op jit(solution)/shard_map/all_gather | solution.py:82
  8.7 659.7 %all-gather.23.cloned.1.call-start = ((), (), s32[]{:S(2)}) async-start(), calls=%async_computation.16 | async-start | bytes 5242880 | tf_op jit(solution)/shard_map/all_gather | solution.py:126
  22.4 429.7 %copy-start.14 = (f32[4,1,512]{2,1,0:T(1,128)}, f32[4,1,512]{2,1,0:T(1,128)S(1)}, u32[]{:S(2)}) copy-start(f32[4,1,512]{2,1,0:T(1,128)S(1)} %convert_element_type.135) | copy-start | bytes 24580
  34.6 417.6 %copy-start.12 = (f32[4,1,512]{2,1,0:T(1,128)}, f32[4,1,512]{2,1,0:T(1,128)S(1)}, u32[]{:S(2)}) copy-start(f32[4,1,512]{2,1,0:T(1,128)S(1)} %convert_element_type.134) | copy-start | bytes 24580
  68.7 383.5 %copy-start.17 = (f32[256]{0:T(256)}, f32[256]{0:T(256)S(1)}, u32[]{:S(2)}) copy-start(f32[256]{0:T(256)S(1)} %broadcast_multiply_fusion.2) | copy-start | bytes 3076
  69.1 383.1 %copy-start.19 = (f32[256]{0:T(256)}, f32[256]{0:T(256)S(1)}, u32[]{:S(2)}) copy-start(f32[256]{0:T(256)S(1)} %add_rsqrt_fusion) | copy-start | bytes 3076
  437.9 17.1 copy-start.28
  455.0 294.5 %all-gather.15.cloned.1.call-start = ((), (), s32[]{:S(2)}) async-start(), calls=%async_computation.7 | async-start | bytes 5242880 | tf_op jit(solution)/shard_map/all_gather | solution.py:123
  455.8 10.8 copy-start.10
  462.6 9.0 copy-start.9
  462.6 124.7 %copy-start.2 = (bf16[1,256,2048]{2,1,0:T(8,128)(2,1)S(1)}, bf16[1,256,2048]{2,1,0:T(8,128)(2,1)}, u32[]{:S(2)}) copy-start(bf16[1,256,2048]{2,1,0:T(8,128)(2,1)} %param.31) | copy-start | bytes 3145732
  471.3 532.6 %reduce-scatter.9.cloned.1.call-start = ((), (), s32[]{:S(2)}) async-start(), calls=%async_computation.11 | async-start | bytes 10485760 | tf_op jit(solution)/shard_map/reduce_scatter | solution.py:227
  784.6 1.0 copy-start.6
  860.9 291.0 %reduce-scatter.11.cloned.1.call-start = ((), (), s32[]{:S(2)}) async-start(), calls=%async_computation.12 | async-start | bytes 10485760 | tf_op jit(solution)/shard_map/reduce_scatter | solution.py:228
  861.5 854.2 %all-gather.19.cloned.1.call-start = ((), (), s32[]{:S(2)}) async-start(), calls=%async_computation.9 | async-start | bytes 41943040 | tf_op jit(solution)/shard_map/all_gather | solution.py:84
  862.3 1.2 copy-start.3
  862.3 1.5 copy-start.7
  862.3 1414.7 %all-gather.21.cloned.1.call-start = ((), (), s32[]{:S(2)}) async-start(), calls=%async_computation.10 | async-start | bytes 41943040 | tf_op jit(solution)/shard_map/all_gather | solution.py:86
  863.0 1695.5 %reduce-scatter.15.cloned.1.call-start = ((), (), s32[]{:S(2)}) async-start(), calls=%async_computation.14 | async-start | bytes 20971520 | tf_op jit(solution)/shard_map/reduce_scatter | solution.py:266
  872.3 132.9 %copy-start.11 = (f32[256,16]{0,1:T(8,128)S(1)}, f32[256,16]{0,1:T(8,128)}, u32[]{:S(2)}) copy-start(f32[256,16]{0,1:T(8,128)} %copy-done.10) | copy-start | bytes 49156
  872.3 132.9 %copy-start.16 = (f32[256,16]{0,1:T(8,128)S(1)}, f32[256,16]{0,1:T(8,128)}, u32[]{:S(2)}) copy-start(f32[256,16]{0,1:T(8,128)} %get-tuple-element.321) | copy-start | bytes 49156
  872.4 2509.8 %reduce-scatter.13.cloned.1.call-start = ((), (), s32[]{:S(2)}) async-start(), calls=%async_computation.13 | async-start | bytes 62914560 | tf_op jit(solution)/shard_map/reduce_scatter | solution.py:266
  872.4 281.2 %copy-start.1 = (bf16[1,256,2048]{2,1,0:T(8,128)(2,1)S(1)}, bf16[1,256,2048]{2,1,0:T(8,128)(2,1)}, u32[]{:S(2)}) copy-start(bf16[1,256,2048]{2,1,0:T(8,128)(2,1)} %param.18) | copy-start | bytes 3145732
  872.4 281.2 %copy-start.13 = (f32[4,1,512]{2,1,0:T(1,128)S(1)}, f32[4,1,512]{2,1,0:T(1,128)}, u32[]{:S(2)}) copy-start(f32[4,1,512]{2,1,0:T(1,128)} %copy-done.12) | copy-start | bytes 24580
  872.4 281.2 %copy-start.15 = (f32[4,1,512]{2,1,0:T(1,128)S(1)}, f32[4,1,512]{2,1,0:T(1,128)}, u32[]{:S(2)}) copy-start(f32[4,1,512]{2,1,0:T(1,128)} %copy-done.14) | copy-start | bytes 24580
  872.4 281.2 %copy-start.18 = (f32[256]{0:T(256)S(1)}, f32[256]{0:T(256)}, u32[]{:S(2)}) copy-start(f32[256]{0:T(256)} %copy-done.17) | copy-start | bytes 3076
  872.5 281.2 %copy-start.20 = (f32[256]{0:T(256)S(1)}, f32[256]{0:T(256)}, u32[]{:S(2)}) copy-start(f32[256]{0:T(256)} %copy-done.19) | copy-start | bytes 3076
  1183.3 0.7 copy-start.21
  1183.3 3298.0 %reduce-scatter.17.cloned.1.call-start = ((), (), s32[]{:S(2)}) async-start(), calls=%async_computation.15 | async-start | bytes 83886080 | tf_op jit(solution)/shard_map/reduce_scatter | solution.py:266
  1767.1 3812.6 %reduce-scatter.19.cloned.1.call-start = ((), (), s32[]{:S(2)}) async-start(), calls=%async_computation.17 | async-start | bytes 83886080
  2326.7 3306.9 %all-reduce.14.cloned.1.call-start = ((), (), s32[]{:S(2)}) async-start(), calls=%async_computation.19 | async-start | bytes 163840
  2340.2 18.4 copy-start.4
  2340.2 18.4 copy-start.5
  2363.3 3840.1 %all-reduce.12.cloned.1.call-start = ((), (), s32[]{:S(2)}) async-start(), calls=%async_computation.18 | async-start | bytes 100663296 | tf_op jit(solution)/shard_map/psum | solution.py:279
  5579.8 0.7 copy-start.29
  5579.8 3.2 copy-start.26
  5579.8 3.2 copy-start.27
  5579.8 27.8 copy-start.8
  5662.0 564.2 %copy-start.23 = (f32[512]{0:T(512)}, f32[512]{0:T(512)S(1)}, u32[]{:S(2)}) copy-start(f32[512]{0:T(512)S(1)} %get-tuple-element.615) | copy-start | bytes 6148
Sparse Core Ops, SparseCore 0:
  9.6 428.2 all-gather.12
  439.5 147.7 all-gather.16
  589.5 78.9 all-gather.22
  670.4 79.0 all-gather.14
  861.1 142.7 reduce-scatter.8
  1006.7 145.2 reduce-scatter.10
  1153.5 562.2 all-gather.18
  1717.3 559.5 all-gather.20
  2279.9 278.6 reduce-scatter.14
  2560.8 821.3 reduce-scatter.12
  3384.6 1096.7 reduce-scatter.16
  4483.6 1096.1 reduce-scatter.18
  5583.6 36.1 all-reduce.13
  5623.9 579.4 all-reduce.11
where the time goes:
time: 6260 us
  waiting for transfers between devices  5670 us (91%)
  matrix products  308 us (5%)
  blocking collectives  148 us (2%)
  local copies, waits for them, and re-layouts  79.6 us (1%)
    reduce_scatter x3, waiting for transfers between devices, owned(): lax.psum_scatter(lax.dot_general(outputs, inputs, (((0,), (0,)), ((), ())...  2120 us
    unnamed x16, waiting for transfers between devices  1100 us
    psum x1, waiting for transfers between devices, local(): lax.psum((small_sums[0], small_sums[1], inproj_part, small_sums[2], outpr...  541 us
    all_gather x1, waiting for transfers between devices, local(): lax.all_gather(shrink_weight, 'shard', axis=0, tiled=True)  510 us
    all_gather x1, waiting for transfers between devices, local(): lax.all_gather(expand_weight, 'shard', axis=0, tiled=True)  493 us
    all_gather x1, waiting for transfers between devices, local(): lax.all_gather(inproj_weight, 'shard', axis=0, tiled=True)  369 us
    reduce_scatter x1, waiting for transfers between devices, local(): lax.psum_scatter(value_terms, 'shard', scatter_dimension=1, tiled=True)  143 us
    reduce_scatter x1, waiting for transfers between devices, local(): lax.psum_scatter(key_terms, 'shard', scatter_dimension=1, tiled=True)  130 us
  transfers between devices with their start and end apart: 14, of which 13 were waited for; matrix products, arithmetic and copies ran while one was open for 4% of the time, Pallas kernels for 0%

commit v1 on v0

v1 whole, which is shorter than its diff:
```python
import functools
import math

import jax
import jax.numpy as jnp
import numpy as np
from jax import lax
from jax.experimental import pallas as pl
from jax.experimental.pallas import tpu as pltpu
from jax.sharding import PartitionSpec as P


HEAD_DIM = 64
ROT = 32
PAIR = 2 * HEAD_DIM
NEG = -1e30
F32 = jnp.float32
BF16 = jnp.bfloat16


def nt(a, b):
    return lax.dot_general(a, b, (((1,), (1,)), ((), ())), preferred_element_type=F32)


def nn(a, b):
    return lax.dot_general(a, b, (((1,), (0,)), ((), ())), preferred_element_type=F32)


def tn(a, b):
    return lax.dot_general(a, b, (((0,), (0,)), ((), ())), preferred_element_type=F32)


def gelu_parts(values):
    c = math.sqrt(2.0 / math.pi)
    square = values * values
    t = jnp.tanh(c * (values + 0.044715 * square * values))
    half = 0.5 * (1.0 + t)
    slope = half + 0.5 * values * (1.0 - t * t) * (c * (1.0 + 3.0 * 0.044715 * square))
    return values * half, slope


def rotate_pair(x, cosine, sine_low, sine_high):
    quarter = ROT // 2
    up = pltpu.roll(x, PAIR - quarter, 1)
    down = pltpu.roll(x, quarter, 1)
    return x * cosine + up * sine_low + down * sine_high


def allowed_mask(seg_col, seg_row, first_key, keys, first_query, queries):
    same = seg_col == seg_row
    kpos = first_key + lax.broadcasted_iota(jnp.int32, (keys, queries), 0)
    qpos = first_query + lax.broadcasted_iota(jnp.int32, (keys, queries), 1)
    return same & (kpos <= qpos)


def attend_kernel(blk, q_ref, k_ref, v_ref, cos_ref, slo_ref, shi_ref, segc_ref, segr_ref,
                  o_ref, q_out, k_out, v_out, lse_ref):
    length = q_ref.shape[0]
    cosine, slo, shi = cos_ref[...], slo_ref[...], shi_ref[...]
    q_low = (rotate_pair(q_ref[...], cosine, slo, shi).astype(BF16)) * jnp.asarray(HEAD_DIM**-0.5, BF16)
    k_low = rotate_pair(k_ref[...], cosine, slo, shi).astype(BF16)
    v_low = v_ref[...].astype(BF16)
    q_out[...] = q_low
    k_out[...] = k_low
    v_out[...] = v_low
    lane = lax.broadcasted_iota(jnp.int32, (1, PAIR), 1)
    v_t = v_low.T
    for b in range(length // blk):
        rows = slice(b * blk, (b + 1) * blk)
        keys = (b + 1) * blk
        mask = allowed_mask(segc_ref[:keys, :1], segr_ref[:1, rows], 0, keys, b * blk, blk)
        outs = []
        for h in range(2):
            mine = (lane < HEAD_DIM) if h == 0 else (lane >= HEAD_DIM)
            qh = jnp.where(mine, q_low[rows], jnp.zeros((), BF16))
            s = jnp.where(mask, nt(k_low[:keys], qh), NEG)
            top = jnp.max(s, axis=0, keepdims=True)
            e = jnp.exp(s - top)
            total = jnp.sum(e, axis=0, keepdims=True)
            p = (e * (1.0 / total)).astype(BF16)
            lse_ref[0, h : h + 1, rows] = top + jnp.log(total)
            outs.append(nn(v_t[h * HEAD_DIM : (h + 1) * HEAD_DIM, :keys], p))
        o_ref[rows, :] = jnp.concatenate(outs, 0).T.astype(BF16)


def attend(mixed, tables, seg_col, seg_row, blk):
    length, wide = mixed.shape
    heads_wide = wide // 3
    pairs = heads_wide // PAIR
    col = lambda off: pl.BlockSpec((length, PAIR), lambda p: (0, off + p))
    fixed = lambda shape: pl.BlockSpec(shape, lambda p: (0, 0))
    return pl.pallas_call(
        functools.partial(attend_kernel, blk),
        grid=(pairs,),
        in_specs=[col(0), col(pairs), col(2 * pairs)]
        + [fixed((length, PAIR))] * 3
        + [fixed((length, 1)), fixed((1, length))],
        out_specs=[col(0)] * 4 + [pl.BlockSpec((1, 2, length), lambda p: (p, 0, 0))],
        out_shape=[jax.ShapeDtypeStruct((length, heads_wide), BF16)] * 4
        + [jax.ShapeDtypeStruct((pairs, 2, length), F32)],
        compiler_params=pltpu.CompilerParams(vmem_limit_bytes=56 << 20),
        name="attend",
    )(mixed, mixed, mixed, *tables, seg_col, seg_row)


def attend_back_kernel(blk, q_ref, k_ref, v_ref, g_ref, lse_ref, cos_ref, slo_ref, shi_ref,
                       segc_ref, segr_ref, dq_ref, dk_ref, dv_ref, dk_acc, dv_acc):
    length = q_ref.shape[0]
    q_low, k_low, v_low, g_low = q_ref[...], k_ref[...], v_ref[...], g_ref[...]
    lane = lax.broadcasted_iota(jnp.int32, (1, PAIR), 1)
    k_t = k_low.T
    zero = jnp.zeros((), BF16)
    cosine, slo, shi = cos_ref[...], slo_ref[...], shi_ref[...]
    first = lane < HEAD_DIM
    count = length // blk
    for b in reversed(range(count)):
        rows = slice(b * blk, (b + 1) * blk)
        keys = (b + 1) * blk
        mask = allowed_mask(segc_ref[:keys, :1], segr_ref[:1, rows], 0, keys, b * blk, blk)
        dq_t, dk_h, dv_h = [], [], []
        for h in range(2):
            mine = first if h == 0 else jnp.logical_not(first)
            qh = jnp.where(mine, q_low[rows], zero)
            gh = jnp.where(mine, g_low[rows], zero)
            s = jnp.where(mask, nt(k_low[:keys], qh), NEG)
            p = jnp.exp(s - lse_ref[0, h : h + 1, rows])
            dp = nt(v_low[:keys], gh)
            delta = jnp.sum(p * dp, axis=0, keepdims=True)
            ds = (p * (dp - delta)).astype(BF16)
            dq_t.append(nn(k_t[h * HEAD_DIM : (h + 1) * HEAD_DIM, :keys], ds))
            dk_h.append(nn(ds, q_low[rows]))
            dv_h.append(nn(p.astype(BF16), g_low[rows]))
        dk_new = jnp.where(first, dk_h[0], dk_h[1])
        dv_new = jnp.where(first, dv_h[0], dv_h[1])
        if b == count - 1:
            dk_acc[...] = dk_new
            dv_acc[...] = dv_new
        else:
            dk_acc[:keys] += dk_new
            dv_acc[:keys] += dv_new
        dq = jnp.concatenate(dq_t, 0).T * (HEAD_DIM**-0.5)
        dq_ref[rows, :] = rotate_pair(dq, cosine[rows], -slo[rows], -shi[rows]).astype(BF16)
    dk_ref[...] = rotate_pair(dk_acc[...], cosine, -slo, -shi).astype(BF16)
    dv_ref[...] = dv_acc[...].astype(BF16)


def attend_back(q, k, v, g, lse, tables, seg_col, seg_row, blk):
    length, heads_wide = q.shape
    pairs = heads_wide // PAIR
    col = pl.BlockSpec((length, PAIR), lambda p: (0, p))
    fixed = lambda shape: pl.BlockSpec(shape, lambda p: (0, 0))
    return pl.pallas_call(
        functools.partial(attend_back_kernel, blk),
        grid=(pairs,),
        in_specs=[col] * 4
        + [pl.BlockSpec((1, 2, length), lambda p: (p, 0, 0))]
        + [fixed((length, PAIR))] * 3
        + [fixed((length, 1)), fixed((1, length))],
        out_specs=[col] * 3,
        out_shape=[jax.ShapeDtypeStruct((length, heads_wide), BF16)] * 3,
        scratch_shapes=[pltpu.VMEM((length, PAIR), F32)] * 2,
        compiler_params=pltpu.CompilerParams(vmem_limit_bytes=56 << 20),
        name="attend_back",
    )(q, k, v, g, lse, *tables, seg_col, seg_row)


def pick(x, index, axis=0):
    return lax.dynamic_index_in_dim(x, index, axis, keepdims=False)


def shift(x, offset, count):
    return lax.ppermute(x, "shard", [(i, (i + offset) % count) for i in range(count)])


def gather_row(x, count, me):
    half = x.shape[0] // 2
    out = jnp.zeros((count,) + x.shape, x.dtype)
    out = lax.dynamic_update_slice(out, x[None], (me, 0, 0))
    fore = aft = x
    for step in range(1, count // 2):
        fore = shift(fore, 1, count)
        aft = shift(aft, -1, count)
        out = lax.dynamic_update_slice(out, fore[None], ((me - step) % count, 0, 0))
        out = lax.dynamic_update_slice(out, aft[None], ((me + step) % count, 0, 0))
    far = (me + count // 2) % count
    fore = shift(fore[:half], 1, count)
    aft = shift(aft[half:], -1, count)
    out = lax.dynamic_update_slice(out, fore[None], (far, 0, 0))
    out = lax.dynamic_update_slice(out, aft[None], (far, half, 0))
    return out.reshape(count * x.shape[0], x.shape[1])


def scatter_row(x, count, me):
    x = x.reshape(count, x.shape[0] // count, x.shape[1])
    half = x.shape[1] // 2

    def block(step):
        return pick(x, (me + step) % count)

    far = block(count // 2)
    fore = shift(far[:half], 1, count)
    aft = shift(far[half:], -1, count)
    for step in range(count // 2 - 1, 0, -1):
        ahead, behind = block(step).astype(F32), block(-step).astype(F32)
        if fore.shape[0] == half:
            ahead = jnp.concatenate([ahead[:half] + fore.astype(F32), ahead[half:]], 0)
            behind = jnp.concatenate([behind[:half], behind[half:] + aft.astype(F32)], 0)
        else:
            ahead = ahead + fore.astype(F32)
            behind = behind + aft.astype(F32)
        fore = shift(ahead.astype(BF16), 1, count)
        aft = shift(behind.astype(BF16), -1, count)
    return block(0).astype(F32) + fore.astype(F32) + aft.astype(F32)


def scatter_direct(x, count, me):
    x = x.reshape(count, x.shape[0] // count, x.shape[1])
    out = pick(x, me).astype(F32)
    for step in range(1, count):
        out = out + shift(pick(x, (me + step) % count), step, count).astype(F32)
    return out


def gather_small(x, count, me):
    out = lax.dynamic_update_slice(jnp.zeros((count,) + x.shape, x.dtype), x[None], (me, 0))
    for step in range(1, count):
        out = lax.dynamic_update_slice(out, shift(x, step, count)[None], ((me - step) % count, 0))
    return out


def swap_blocks(x, axis, count, me):
    out = jnp.zeros(x.shape, x.dtype)

    def put(out, block, place):
        start = [0] * x.ndim
        start[axis] = place
        return lax.dynamic_update_slice(out, jnp.expand_dims(block, axis), start)

    out = put(out, pick(x, me, axis), me)
    for step in range(1, count):
        block = shift(pick(x, (me + step) % count, axis), step, count)
        out = put(out, block, (me - step) % count)
    return out


def flip(x, mask, reps):
    return lax.ppermute(x, "rep", [(i, i ^ mask) for i in range(reps)])


def reduce_chips(x, rep, reps):
    lead, rows, cols = x.shape
    chips = reps // 2
    x = x.reshape(lead, chips, rows // chips, cols)
    mine = rep >> 1
    arrived = [flip(pick(x, mine ^ mask, 1), 2 * mask, reps) for mask in range(1, chips)]

    def total():
        out = pick(x, mine, 1).astype(F32)
        for term in arrived:
            out = out + term.astype(F32)
        return out.astype(BF16)

    return total


def spread(x, reps):
    own = [x] + [flip(x, 2 * mask, reps) for mask in range(1, reps // 2)]
    return own + [flip(piece, 1, reps) for piece in own]


def assemble(pieces, rep, wide):
    chips = len(pieces) // 2
    lead, rows, cols = pieces[0].shape
    tile = max(8, rows // 2)
    tiles = rows // tile
    groups, width = (1, 2 * cols * lead) if wide else (lead, 2 * cols)

    def kernel(place_ref, *refs):
        out = refs[-1]
        for i in range(chips):

            @pl.when(pl.program_id(0) == i)
            def _(i=i):
                for side, ref in ((place_ref[1], refs[i]), (1 - place_ref[1], refs[chips + i])):
                    for l in range(lead):
                        at = pl.multiple_of(side * cols + (l * 2 * cols if wide else 0), 128)
                        out[0 if wide else l, 0, :, pl.ds(at, cols)] = ref[l].astype(F32)

    def source(i):
        return pl.BlockSpec(
            (lead, tile, cols),
            lambda p, t, place: (0, jnp.where(p == i, t, jnp.where(p < i, 0, tiles - 1)), 0),
        )

    out = pl.pallas_call(
        kernel,
        grid_spec=pltpu.PrefetchScalarGridSpec(
            num_scalar_prefetch=1,
            grid=(chips, tiles),
            in_specs=[source(i) for i in range(chips)] * 2,
            out_specs=pl.BlockSpec(
                (groups, 1, tile, width), lambda p, t, place: (0, place[0] ^ p, t, 0)
            ),
        ),
        out_shape=jax.ShapeDtypeStruct((groups, chips, rows, width), F32),
        compiler_params=pltpu.CompilerParams(vmem_limit_bytes=48 << 20),
        name="assemble",
    )(jnp.stack([rep >> 1, rep & 1]), *pieces)
    return out.reshape(groups * chips * rows, width)


def hold(*xs):
    return lax.optimization_barrier(xs)


def local(
    tokens,
    segments,
    positions,
    norm_gain,
    norm_shift,
    inproj_weight,
    inproj_bias,
    outproj_weight,
    outproj_bias,
    expand_weight,
    expand_bias,
    shrink_weight,
    shrink_bias,
    out_grad,
):
    span, width = tokens.shape[1:]
    count = lax.axis_size("shard")
    reps = lax.axis_size("rep")
    bits = reps.bit_length() - 1
    me = lax.axis_index("shard")
    rep = lax.axis_index("rep")
    core = rep & 1
    length = span * count
    part = width // count
    inner = expand_weight.shape[0]
    sub = part // reps

    kind_of = np.zeros((count, 3), np.int32)
    forward = [[(s, (3 * s + j) % count) for s in range(count)] for j in range(3)]
    for s in range(count):
        for j in range(3):
            kind_of[(3 * s + j) % count, j] = (3 * s + j) // count
    round_of = np.argsort(kind_of, 1).astype(np.int32)

    down = jnp.concatenate(
        [
            lax.dynamic_slice_in_dim(shrink_weight, rep * sub, sub, 0).reshape(sub, count, inner),
            lax.dynamic_slice_in_dim(outproj_weight, rep * sub, sub, 0).reshape(sub, count, part),
        ],
        2,
    )
    down = swap_blocks(jnp.transpose(down, (1, 0, 2)), 0, count, me)

    packed = jnp.concatenate([norm_gain, norm_shift, outproj_bias, shrink_bias, inproj_bias])
    packed = gather_small(packed, count, me)
    gain, shift_all, outbias, shrbias = (
        packed[:, i * part : (i + 1) * part].reshape(width).astype(F32) for i in range(4)
    )
    inbias = packed[:, 4 * part :].reshape(3, count, part)
    inbias = pick(inbias, me, 1).reshape(3 * part).astype(F32)

    grad_own = out_grad.reshape(span, width)
    grads = gather_row(grad_own, count, me)

    residual = tokens.reshape(span, width).astype(F32)
    row_mean = jnp.mean(residual, -1, keepdims=True)
    centered = residual - row_mean
    row_var = jnp.mean(centered * centered, -1, keepdims=True)
    inv_std = lax.rsqrt(row_var + 1e-05)
    xhat = centered * inv_std
    normed_own = (xhat * gain + shift_all).astype(BF16)
    normed = gather_row(normed_own, count, me)

    down = lax.all_gather(down, "rep", axis=1, tiled=True).reshape(width, inner + part)
    shrink_w, out_w = down[:, :inner], down[:, inner:]

    seg = segments.reshape(length)
    starts = jnp.sum((seg[None, :] < seg[:, None]).astype(jnp.int32), 1)
    place = (jnp.arange(length, dtype=jnp.int32) - starts).astype(F32)
    inverse_freq = 10000.0 ** (-jnp.arange(ROT // 2).astype(F32) * 2.0 / ROT)
    angle = place[:, None] * inverse_freq[None, :]
    cosine, sine = jnp.cos(angle), jnp.sin(angle)
    quiet = jnp.zeros_like(sine)
    rest = jnp.zeros((length, HEAD_DIM - ROT), F32)
    tables = (
        jnp.concatenate([cosine, cosine, rest + 1.0] * 2, 1),
        jnp.concatenate([-sine, quiet, rest] * 2, 1),
        jnp.concatenate([quiet, sine, rest] * 2, 1),
    )
    seg_col, seg_row = seg[:, None], seg[None, :]
    blk = min(256, length)
    back = [[(b, a) for a, b in pairs] for pairs in forward]

    def col_half(x, which):
        wide = x.shape[1] // 2
        return lax.dynamic_slice_in_dim(x, which * wide, wide, 1)

    def low_term(outputs, inputs, extra=None):
        out = tn(outputs, inputs)
        return (out if extra is None else out + extra.astype(F32)).astype(BF16)

    normed_mine, normed_other = col_half(normed, core), col_half(normed, 1 - core)
    expanded = nt(normed, expand_weight) + expand_bias.astype(F32)
    hidden, slope = gelu_parts(expanded)
    hidden = hidden.astype(BF16)
    hidden_mine, hidden_other = col_half(hidden, core), col_half(hidden, 1 - core)

    slices = lax.dynamic_slice_in_dim(inproj_weight.reshape(3, part, width), rep * sub, sub, 1)
    grads, slices = hold(grads, slices)
    arrived = jnp.stack([lax.ppermute(slices[j], "shard", forward[j]) for j in range(3)])
    my_rounds = pick(jnp.asarray(round_of), me)
    arrived = jnp.stack([pick(arrived, my_rounds[k]) for k in range(3)])
    in_w = lax.all_gather(arrived, "rep", axis=1, tiled=True).reshape(3 * part, width)

    blocks = inner // part
    shr_send = low_term(grads, hidden_other)
    shr_arrived = flip(shr_send, 1, reps)
    grads_1, shr_send = hold(grads, shr_send)
    d_up = (nn(grads_1, shrink_w) * slope).astype(BF16)
    grads_2, d_up = hold(grads_1, d_up)
    shr_sum = low_term(grads_2, hidden_mine, shr_arrived)
    shr_total = reduce_chips(shr_sum.reshape(count, part, inner // 2), rep, reps)
    d_up, shr_sum = hold(d_up, shr_sum)
    exp_send = low_term(d_up, normed_other)
    exp_arrived = flip(exp_send, 1, reps)
    grads_3, exp_send = hold(grads_2, exp_send)
    d_att = nn(grads_3, out_w).astype(BF16)
    d_up_1, d_att = hold(d_up, d_att)
    exp_sum = low_term(d_up_1, normed_mine, exp_arrived)
    exp_total = reduce_chips(exp_sum.reshape(blocks, part, width // 2), rep, reps)

    normed_1, exp_sum = hold(normed, exp_sum)
    mixed = nt(normed_1, in_w) + inbias
    attended, q_low, k_low, v_low, lse = attend(mixed, tables, seg_col, seg_row, blk)
    grads_4, attended = hold(grads_3, attended)
    g_out = tn(grads_4, attended).astype(BF16)
    hidden_1, g_out = hold(hidden, g_out)
    g_out = lax.psum_scatter(
        g_out.reshape(count, part, part), "rep", scatter_dimension=1, tiled=True
    )
    g_shr = shr_total()
    g_shr = swap_blocks(g_shr, 0, count, me)
    branches = (nt(hidden_1, shrink_w) + nt(attended, out_w)).astype(BF16)
    branches_sum = scatter_direct(branches, count, me)
    shr_pieces = spread(g_shr, reps)
    g_exp = exp_total()
    exp_pieces = spread(g_exp, reps)

    d_att, branches, g_exp = hold(d_att, branches, g_exp)
    d_q, d_k, d_v = attend_back(q_low, k_low, v_low, d_att, lse, tables, seg_col, seg_row, blk)
    d_mixed = jnp.concatenate([d_q, d_k, d_v], 1)
    g_out, d_mixed = hold(g_out, d_mixed)
    in_send = low_term(d_mixed, normed_other)
    in_arrived = flip(in_send, 1, reps)
    g_out = jnp.transpose(swap_blocks(g_out, 0, count, me), (1, 0, 2)).reshape(sub, width)
    in_sum = low_term(d_mixed, normed_mine, in_arrived)
    in_total = reduce_chips(in_sum.reshape(3, part, width // 2), rep, reps)
    d_up_3, in_sum = hold(d_up_1, in_sum)
    d_normed = (nn(d_up_3, expand_weight) + nn(d_mixed, in_w)).astype(BF16)
    d_normed = scatter_row(d_normed, count, me)
    g_out = lax.all_gather(g_out, "rep", axis=0, tiled=True).astype(F32)

    g_shr = assemble(shr_pieces, rep, True)
    kinds = pick(jnp.asarray(kind_of), me)
    g_in = in_total()
    g_in = jnp.stack([lax.ppermute(pick(g_in, kinds[j]), "shard", back[j]) for j in range(3)])
    in_pieces = spread(g_in, reps)
    g_exp = assemble(exp_pieces, rep, False)
    g_in = assemble(in_pieces, rep, False)
    block_output = (residual + (branches_sum + (outbias + shrbias))).astype(BF16)

    d_hat = d_normed * gain
    token_grad = grad_own.astype(F32) + inv_std * (
        d_hat
        - jnp.mean(d_hat, -1, keepdims=True)
        - xhat * jnp.mean(d_hat * xhat, -1, keepdims=True)
    )

    b_out = jnp.sum(lax.dynamic_slice_in_dim(grads, me * part, part, 1), 0, dtype=F32)
    b_exp = jnp.sum(d_up, 0, dtype=F32)
    b_in = jnp.sum(d_mixed, 0, dtype=F32)
    sums = jnp.concatenate([b_out, b_exp, b_in])
    for bit in range(bits):
        sums = sums + flip(sums, 1 << bit, reps)
    b_out, b_exp, b_in = sums[:part], sums[part : part + inner], sums[part + inner :]
    b_in = b_in.reshape(3, part)
    b_in = jnp.concatenate([lax.ppermute(pick(b_in, kinds[j]), "shard", back[j]) for j in range(3)])
    both = jnp.stack([jnp.sum(d_normed * xhat, 0), jnp.sum(d_normed, 0)])
    both = jnp.sum(swap_blocks(both.reshape(2, count, part), 1, count, me), 1)
    for bit in range(bits):
        both = both + flip(both, 1 << bit, reps)

    return (
        block_output[None],
        token_grad[None],
        both[0],
        both[1],
        g_in,
        b_in,
        g_out,
        b_out,
        g_exp,
        b_exp,
        g_shr,
        b_out,
    )


def solution(mesh):
    in_specs = (
        P("rep", "shard", None),
        P("rep", None),
        P("rep", "shard"),
        P("shard"),
        P("shard"),
        P("shard", None),
        P("shard"),
        P("shard", None),
        P("shard"),
        P("shard", None),
        P("shard"),
        P("shard", None),
        P("shard"),
        P("rep", "shard", None),
    )
    out_specs = (
        P("rep", "shard", None),
        P("rep", "shard", None),
        P("shard"),
        P("shard"),
        P("shard", None),
        P("shard"),
        P("shard", None),
        P("shard"),
        P("shard", None),
        P("shard"),
        P("shard", None),
        P("shard"),
    )

    return jax.shard_map(local, mesh=mesh, in_specs=in_specs, out_specs=out_specs, check_vma=False)
```

time: 6260 us -> 827 us (0.13)
  the two profiles are of different devices: /device:TPU:0 before, /device:TPU:25 now
where the time goes in v1:
time: 827 us; the launch traced here: 817 us
  waiting for transfers between devices  330 us (40%)
  matrix products  152 us (18%)
  starting transfers between devices  124 us (15%)
  Pallas kernels  78.4 us (9%)
  local copies, waits for them, and re-layouts  66.2 us (8%)
  other arithmetic  39.2 us (5%)
  between operations  27.4 us (3%)
    ppermute x30, waiting for transfers between devices, shift(): lax.ppermute(x, 'shard', [(i, (i + offset) % count) for i in range(count)])  158 us
    ppermute x39, waiting for transfers between devices, flip(): return lax.ppermute(x, 'rep', [(i, i ^ mask) for i in range(reps)])  112 us
    ppermute x39, starting transfers between devices, flip(): return lax.ppermute(x, 'rep', [(i, i ^ mask) for i in range(reps)])  61.2 us
    ppermute x3, waiting for transfers between devices, local(): lax.ppermute(pick(b_in, kinds[j]), 'shard', back[j])  60.1 us
    dot_general x7, matrix products, tn(): lax.dot_general(a, b, (((0,), (0,)), ((), ())), preferred_element_type=F32)  57.7 us
    dot_general x4, matrix products, nt(): lax.dot_general(a, b, (((1,), (1,)), ((), ())), preferred_element_type=F32)  47.7 us
    dot_general x4, matrix products, nn(): lax.dot_general(a, b, (((1,), (0,)), ((), ())), preferred_element_type=F32)  46.1 us
    ppermute x30, starting transfers between devices, shift(): lax.ppermute(x, 'shard', [(i, (i + offset) % count) for i in range(count)])  44.2 us
  transfers between devices with their start and end apart: 82, of which 23 were waited for; matrix products, arithmetic and copies ran while one was open for 29% of the time, Pallas kernels for 8%

profile of v1, /device:TPU:25, one launch (start us, length us, event | category | flops | bytes accessed | tf_op | source)
XLA Modules:
  0.0 817.0 jit_solution(3641167637685222010)
XLA Ops:
  13.9 2.7 constant_dynamic-slice_fusion.13
  20.8 5.6 collective-permute-done.11
  27.4 20.0 %collective-permute-done.12 = bf16[64,2560]{1,0:T(8,128)(2,1)} collective-permute-done((bf16[64,2560]{1,0:T(8,128)(2,1)}, bf16[64,2560]{1,0:T(8,128)(2,1)}, u32[]{:S(2)}, u32[]{:S(2)}) %collective-permute-start.12) | collective-permute-done | bytes 327712 | tf_op jit(solution)/shard_map/ppermute | solution.py:172
  58.5 2.6 broadcast.82.clone
  69.9 3.4 collective-permute-start.3
  74.3 3.8 collective-permute-done.7
  79.2 3.4 collective-permute-start.9
  82.6 17.8 %collective-permute-done.8 = bf16[256,2048]{1,0:T(8,128)(2,1)} collective-permute-done((bf16[256,2048]{1,0:T(8,128)(2,1)S(1)}, bf16[256,2048]{1,0:T(8,128)(2,1)}, u32[]{:S(2)}, u32[]{:S(2)}) %collective-permute-start.8) | collective-permute-done | bytes 1048608 | tf_op jit(solution)/shard_map/ppermute | solution.py:172
  103.2 2.5 bitcast_dynamic-update-slice_fusion.1
  108.0 14.9 %collective-permute-done.3 = bf16[256,2048]{1,0:T(8,128)(2,1)S(1)} collective-permute-done((bf16[256,2048]{1,0:T(8,128)(2,1)S(1)}, bf16[256,2048]{1,0:T(8,128)(2,1)S(1)}, u32[]{:S(2)}, u32[]{:S(2)}) %collective-permute-start.3) | collective-permute-done | bytes 1048608 | tf_op jit(solution)/shard_map/ppermute | solution.py:172
  122.9 3.5 collective-permute-start.5
  126.4 18.9 %collective-permute-done.4 = bf16[256,2048]{1,0:T(8,128)(2,1)S(1)} collective-permute-done((bf16[256,2048]{1,0:T(8,128)(2,1)S(1)}, bf16[256,2048]{1,0:T(8,128)(2,1)S(1)}, u32[]{:S(2)}, u32[]{:S(2)}) %collective-permute-start.4) | collective-permute-done | bytes 1048608 | tf_op jit(solution)/shard_map/ppermute | solution.py:172
  147.3 9.2 %collective-permute-done.9 = bf16[128,2048]{1,0:T(8,128)(2,1)S(1)} collective-permute-done((bf16[128,2048]{1,0:T(8,128)(2,1)S(1)}, bf16[128,2048]{1,0:T(8,128)(2,1)S(1)}, u32[]{:S(2)}, u32[]{:S(2)}) %collective-permute-start.9) | collective-permute-done | bytes 524320 | tf_op jit(solution)/shard_map/ppermute | solution.py:172
  157.4 21.6 %collective-permute-done.5 = bf16[128,2048]{1,0:T(8,128)(2,1)S(1)} collective-permute-done((bf16[128,2048]{1,0:T(8,128)(2,1)S(1)}, bf16[128,2048]{1,0:T(8,128)(2,1)S(1)}, u32[]{:S(2)}, u32[]{:S(2)}) %collective-permute-start.5) | collective-permute-done | bytes 524320 | tf_op jit(solution)/shard_map/ppermute | solution.py:172
  179.1 11.2 %collective-permute-done.6 = bf16[128,2048]{1,0:T(8,128)(2,1)S(1)} collective-permute-done((bf16[128,2048]{1,0:T(8,128)(2,1)S(1)}, bf16[128,2048]{1,0:T(8,128)(2,1)S(1)}, u32[]{:S(2)}, u32[]{:S(2)}) %collective-permute-start.6) | collective-permute-done | bytes 524320 | tf_op jit(solution)/shard_map/ppermute | solution.py:172
  191.9 4.3 collective-permute-start.17
  196.1 3.3 collective-permute-start.16
  199.4 12.7 %multiply_convert_fusion.1 = (bf16[1024,2048]{1,0:T(8,128)(2,1)S(1)}, f32[1024,2048]{1,0:T(8,128)}) fusion(f32[2048]{0:T(1024)S(1)} %convert_element_type.243, bf16[1024,2048]{1,0:T(8,128)(2,1)S(1)} %bitcast.255, bf16[2048,2048]{1,0:T(8,128)(2,1)S(1)} %bitcast.308), kind=kOutput, calls=%fused_computation.9 | convolution fusion | flops 8610906112 | bytes 25174016 | tf_op jit(solution)/shard_map/dot_general | solution.py:22
  212.1 9.9 %convolution_convert_fusion.2 = bf16[2048,1024]{1,0:T(8,128)(2,1)} fusion(bf16[1024,2048]{1,0:T(8,128)(2,1)} %bitcast.11, bf16[1024,2048]{1,0:T(8,128)(2,1)S(1)} %get-tuple-element.50, s32[]{:T(128)S(6)} %select_n.251), kind=kOutput, calls=%fused_computation.21 | convolution fusion | flops 4297064448 | bytes 10485764 | tf_op jit(solution)/shard_map/dot_general | solution.py:30
  222.1 2.9 collective-permute-start.14
  226.6 17.6 %multiply_convert_fusion = bf16[1024,2048]{1,0:T(8,128)(2,1)S(1)} fusion(f32[1024,2048]{1,0:T(8,128)} %get-tuple-element.131, bf16[1024,2048]{1,0:T(8,128)(2,1)} %bitcast.11, bf16[2048,2560]{1,0:T(8,128)(2,1)} %bitcast.303, f32[2048]{0:T(1024)S(1)} %convert_element_type.243), kind=kOutput, calls=%fused_computation.8 | convolution fusion | flops 8629780480 | bytes 25174016 | tf_op jit(solution)/shard_map/dot_general | solution.py:26
  244.3 10.6 %add_convert_fusion.3 = bf16[2048,1024]{1,0:T(8,128)(2,1)} fusion(bf16[2048,1024]{1,0:T(8,128)(2,1)} %collective-permute-done.14, bf16[1024,2048]{1,0:T(8,128)(2,1)} %bitcast.11, bf16[1024,2048]{1,0:T(8,128)(2,1)S(1)} %copy-done.57, s32[]{:T(128)S(6)} %select_n.254), kind=kOutput, calls=%fused_computation.7 | convolution fusion | flops 4301258752 | bytes 14680068 | tf_op jit(solution)/shard_map/dot_general | solution.py:30
  254.9 6.4 convolution_convert_fusion.1
  270.5 6.3 fusion.58.g_ref
  280.9 8.0 add_convert_fusion.2
  288.9 11.7 %convolution_add_fusion.q_ref.k_ref.v_ref = f32[1024,1536]{1,0:T(8,128)} fusion(bf16[1024,2048]{1,0:T(8,128)(2,1)} %bitcast.256, bf16[1536,2048]{1,0:T(8,128)(2,1)} %bitcast.311, f32[1536]{0:T(1024)S(1)} %reshape.250), kind=kOutput, calls=%fused_computation.17 | convolution fusion | flops 6444023808 | bytes 16783360 | tf_op jit(solution)/shard_map/dot_general | solution.py:22
  300.6 22.7 %attend.1 = (bf16[1024,512]{1,0:T(8,128)(2,1)}, bf16[1024,512]{1,0:T(8,128)(2,1)}, bf16[1024,512]{1,0:T(8,128)(2,1)}, bf16[1024,512]{1,0:T(8,128)(2,1)}, f32[4,2,1024]{2,1,0:T(2,128)}) custom-call(f32[1024,1536]{1,0:T(8,128)} %convolution_add_fusion.q_ref.k_ref.v_ref, f32[1024,1536]{1,0:T(8,128)} %convolution_add_fusion.q_ref.k_ref.v_ref, ...), custom_call_target="tpu_custom_call" | custom-call | tf_op jit(solution)/shard_map/attend/pallas_call | solution.py:92
  323.4 6.3 convolution_convert_fusion.3
  329.7 7.5 fusion.47
  340.3 15.8 %add_convert_fusion.1 = bf16[1024,2048]{1,0:T(8,128)(2,1)} fusion(f32[1024,2048]{1,0:T(8,128)} %fusion.47, bf16[1024,2048]{1,0:T(8,128)(2,1)S(1)} %copy-done.58, bf16[2048,2560]{1,0:T(8,128)(2,1)} %bitcast.306), kind=kOutput, calls=%fused_computation.5 | convolution fusion | flops 8594128896 | bytes 25165824 | tf_op jit(solution)/shard_map/dot_general | solution.py:22
  356.0 11.8 %collective-permute-done.24 = bf16[4,128,1024]{2,1,0:T(8,128)(2,1)S(1)} collective-permute-done((bf16[4,128,1024]{2,1,0:T(8,128)(2,1)S(1)}, bf16[4,128,1024]{2,1,0:T(8,128)(2,1)S(1)}, u32[]{:S(2)}, u32[]{:S(2)}) %collective-permute-start.24) | collective-permute-done | bytes 1048608 | tf_op jit(solution)/shard_map/ppermute | solution.py:247
  368.1 26.4 %collective-permute-done.23 = bf16[4,128,1024]{2,1,0:T(8,128)(2,1)S(1)} collective-permute-done((bf16[4,128,1024]{2,1,0:T(8,128)(2,1)S(1)}, bf16[4,128,1024]{2,1,0:T(8,128)(2,1)S(1)}, u32[]{:S(2)}, u32[]{:S(2)}) %collective-permute-start.23) | collective-permute-done | bytes 1048608 | tf_op jit(solution)/shard_map/ppermute | solution.py:247
  395.4 25.5 %attend_back.1 = (bf16[1024,512]{1,0:T(8,128)(2,1)}, bf16[1024,512]{1,0:T(8,128)(2,1)}, bf16[1024,512]{1,0:T(8,128)(2,1)}) custom-call(bf16[1024,512]{1,0:T(8,128)(2,1)} %get-tuple-element.52.q_ref, bf16[1024,512]{1,0:T(8,128)(2,1)} %get-tuple-element.53.k_ref, bf16[1024,512]{1,0:T(8,128)(2,1)} %get-tuple-element.54.v_ref, bf16[1024,512]{1,0:T(8,128)(2,1)} %fusion.58.g_ref, ...), custom_call_target="tpu_custom_call" | custom-call | tf_op jit(solution)/shard_map/attend_back/pallas_call | solution.py:152
  420.9 3.3 pad_maximum_fusion
  424.2 7.7 convolution_convert_fusion
  434.0 2.8 fusion.34
  439.3 6.5 collective-permute-done.68
  445.8 15.5 %collective-permute-done.69 = bf16[128,1024]{1,0:T(8,128)(2,1)S(1)} collective-permute-done((bf16[128,1024]{1,0:T(8,128)(2,1)S(1)}, bf16[128,1024]{1,0:T(8,128)(2,1)S(1)}, u32[]{:S(2)}, u32[]{:S(2)}) %collective-permute-start.69) | collective-permute-done | bytes 262176 | tf_op jit(solution)/shard_map/ppermute | solution.py:172
  467.0 18.7 %collective-permute-done.71.refs_1_ = bf16[4,128,1024]{2,1,0:T(8,128)(2,1)S(1)} collective-permute-done((bf16[4,128,1024]{2,1,0:T(8,128)(2,1)S(1)}, bf16[4,128,1024]{2,1,0:T(8,128)(2,1)S(1)}, u32[]{:S(2)}, u32[]{:S(2)}) %collective-permute-start.71) | collective-permute-done | bytes 1048608 | tf_op jit(solution)/shard_map/ppermute | solution.py:247
  488.3 8.8 %add_convert_fusion.4 = bf16[1536,1024]{1,0:T(8,128)(2,1)} fusion(bf16[1536,1024]{1,0:T(8,128)(2,1)} %collective-permute-done.25, bf16[1024,1536]{1,0:T(8,128)(2,1)} %pad_maximum_fusion, bf16[1024,2048]{1,0:T(8,128)(2,1)} %bitcast.258, s32[]{:T(128)S(6)} %select_n.254), kind=kOutput, calls=%fused_computation.16 | convolution fusion | flops 3225944064 | bytes 11534340 | tf_op jit(solution)/shard_map/dot_general | solution.py:30
  497.1 11.3 %fusion.78 = f32[1024,2048]{1,0:T(8,128)} fusion(bf16[1024,2048]{1,0:T(8,128)(2,1)S(1)} %copy-done.20, bf16[2048,2048]{1,0:T(8,128)(2,1)S(1)} %bitcast.310), kind=kOutput, calls=%fused_computation.197 | convolution fusion | flops 8589934592 | bytes 20971520 | tf_op jit(solution)/shard_map/dot_general | solution.py:26
  508.4 10.8 %add_convert_fusion = bf16[1024,2048]{1,0:T(8,128)(2,1)S(1)} fusion(f32[1024,2048]{1,0:T(8,128)} %fusion.78, bf16[1024,1536]{1,0:T(8,128)(2,1)S(1)} %copy-done.15, bf16[1536,2048]{1,0:T(8,128)(2,1)} %bitcast.312), kind=kOutput, calls=%fused_computation.4 | convolution fusion | flops 6446645248 | bytes 22020096 | tf_op jit(solution)/shard_map/dot_general | solution.py:26
  540.1 10.2 %collective-permute-done.28 = bf16[128,2048]{1,0:T(8,128)(2,1)} collective-permute-done((bf16[128,2048]{1,0:T(8,128)(2,1)}, bf16[128,2048]{1,0:T(8,128)(2,1)}, u32[]{:S(2)}, u32[]{:S(2)}) %collective-permute-start.28) | collective-permute-done | bytes 524320 | tf_op jit(solution)/shard_map/ppermute | solution.py:172
  560.3 11.4 %collective-permute-done.58.refs_1_ = bf16[4,128,1024]{2,1,0:T(8,128)(2,1)S(1)} collective-permute-done((bf16[4,128,1024]{2,1,0:T(8,128)(2,1)S(1)}, bf16[4,128,1024]{2,1,0:T(8,128)(2,1)S(1)}, u32[]{:S(2)}, u32[]{:S(2)}) %collective-permute-start.58) | collective-permute-done | bytes 1048608 | tf_op jit(solution)/shard_map/ppermute | solution.py:247
  572.0 22.7 %collective-permute-done.60.refs_3_ = bf16[4,128,1024]{2,1,0:T(8,128)(2,1)S(1)} collective-permute-done((bf16[4,128,1024]{2,1,0:T(8,128)(2,1)S(1)}, bf16[4,128,1024]{2,1,0:T(8,128)(2,1)S(1)}, u32[]{:S(2)}, u32[]{:S(2)}) %collective-permute-start.60) | collective-permute-done | bytes 1048608 | tf_op jit(solution)/shard_map/ppermute | solution.py:247
  597.0 15.0 %collective-permute-done.50 = f32[4096]{0:T(1024)S(1)} collective-permute-done((f32[4096]{0:T(1024)S(1)}, f32[4096]{0:T(1024)S(1)}, u32[]{:S(2)}, u32[]{:S(2)}) %collective-permute-start.50) | collective-permute-done | bytes 16416 | tf_op jit(solution)/shard_map/ppermute | solution.py:247
  615.8 3.0 collective-permute-start.21
  619.5 6.0 collective-permute-done.37
  625.5 4.2 collective-permute-start.61
  637.3 3.4 fusion.57
  640.7 2.9 collective-permute-done.27
  643.6 20.1 %collective-permute-start.64 = (bf16[4,128,1024]{2,1,0:T(8,128)(2,1)}, bf16[4,128,1024]{2,1,0:T(8,128)(2,1)}, u32[]{:S(2)}, u32[]{:S(2)}) collective-permute-start(bf16[4,128,1024]{2,1,0:T(8,128)(2,1)} %copy-done.10), channel_id=1, source_target_pairs={{0,4},{4,0},{8,12},{12,8},{16,20},{20,16},{24,28},{28,24},{1,5},{5... | collective-permute-start | bytes 3145736 | tf_op jit(solution)/shard_map/ppermute | solution.py:247
  663.6 4.4 fusion.25
  668.8 2.6 collective-permute-start.31
  674.0 4.1 collective-permute-start.40
  682.9 2.7 collective-permute-start.20
  685.6 5.5 collective-permute-start.19
  695.5 37.6 %collective-permute-done.53 = f32[512]{0:T(512)S(1)} collective-permute-done((f32[512]{0:T(512)S(1)}, f32[512]{0:T(512)S(1)}, u32[]{:S(2)}, u32[]{:S(2)}) %collective-permute-start.53) | collective-permute-done | bytes 2080 | tf_op jit(solution)/shard_map/ppermute | solution.py:493
  734.1 22.5 %collective-permute-done.52 = f32[512]{0:T(512)S(1)} collective-permute-done((f32[512]{0:T(512)S(1)}, f32[512]{0:T(512)S(1)}, u32[]{:S(2)}, u32[]{:S(2)}) %collective-permute-start.52) | collective-permute-done | bytes 2080 | tf_op jit(solution)/shard_map/ppermute | solution.py:493
  762.1 11.3 %assemble.5 = f32[1,4,128,8192]{3,2,1,0:T(8,128)} custom-call(s32[2]{0:T(128)S(1)} %pad_add_fusion.place_ref, bf16[4,128,1024]{2,1,0:T(8,128)(2,1)S(1)} %bitcast_dynamic-update-slice_fusion.12.refs_0_, bf16[4,128,1024]{2,1,0:T(8,128)(2,1)S(1)} %copy-done.3, bf16[4,128,1024]{2,1,0:T(8,128)(2,1)} %collective-permute-done.72.refs_2_, ...), custom_call_target="tpu_custom_call" | custom-call | tf_op jit(solution)/shard_map/assemble/pallas_call | solution.py:295
  773.4 10.0 %assemble.4 = f32[4,4,128,2048]{3,2,1,0:T(8,128)} custom-call(s32[2]{0:T(128)S(1)} %pad_add_fusion.place_ref, bf16[4,128,1024]{2,1,0:T(8,128)(2,1)S(1)} %fusion.38.refs_0_, bf16[4,128,1024]{2,1,0:T(8,128)(2,1)S(1)} %copy-done.7, bf16[4,128,1024]{2,1,0:T(8,128)(2,1)S(1)} %copy-done.9, bf16[4,128,1024]{2,1,0:T(8,128)(2,1)S(1)} %copy-done.11, ...), custom_call_target="tpu_custom_call" | custom-call | tf_op jit(solution)/shard_map/assemble/pallas_call | solution.py:295
  784.6 4.3 convert_element_type.294
  793.6 5.3 fusion.24
  800.4 9.0 %assemble.3 = f32[3,4,128,2048]{3,2,1,0:T(8,128)} custom-call(s32[2]{0:T(128)S(1)} %pad_add_fusion.place_ref, bf16[3,128,1024]{2,1,0:T(8,128)(2,1)S(1)} %pad_maximum_fusion.5.refs_0_, bf16[3,128,1024]{2,1,0:T(8,128)(2,1)} %collective-permute-done.42.refs_1_, bf16[3,128,1024]{2,1,0:T(8,128)(2,1)} %collective-permute-done.43.refs_2_, ...), custom_call_target="tpu_custom_call" | custom-call | tf_op jit(solution)/shard_map/assemble/pallas_call | solution.py:295
  (402 shorter events, 135.7 us)
Async XLA Ops:
  7.2 219.4 %all-gather.4.cloned.1.call-start = ((), (), s32[]{:S(2)}) async-start(), calls=%async_computation.1 | async-start | bytes 11796480 | tf_op jit(solution)/shard_map/all_gather | solution.py:380
  18.3 29.1 %collective-permute-start.12 = (bf16[64,2560]{1,0:T(8,128)(2,1)}, bf16[64,2560]{1,0:T(8,128)(2,1)}, u32[]{:S(2)}, u32[]{:S(2)}) collective-permute-start(bf16[64,2560]{1,0:T(8,128)(2,1)} %bitcast.247), channel_id=1, source_target_pairs={{0,2},{1,3},{2,0},{3,1},{4,6},{5,7},{6,4},{7,5},{8,10},{9,11},{10,... | collective-permute-start | bytes 983048 | tf_op jit(solution)/shard_map/ppermute | solution.py:172
  20.4 28.0 %collective-permute-start.13 = (bf16[64,2560]{1,0:T(8,128)(2,1)}, bf16[64,2560]{1,0:T(8,128)(2,1)}, u32[]{:S(2)}, u32[]{:S(2)}) collective-permute-start(bf16[64,2560]{1,0:T(8,128)(2,1)} %bitcast.246), channel_id=1, source_target_pairs={{0,3},{1,0},{2,1},{3,2},{4,7},{5,4},{6,5},{7,6},{8,11},{9,8},{10,9... | collective-permute-start | bytes 983048 | tf_op jit(solution)/shard_map/ppermute | solution.py:172
  50.5 238.5 %all-gather.6.cloned.1.call-start = ((), (), s32[]{:S(2)}) async-start(), calls=%async_computation.2 | async-start | bytes 7077888 | tf_op jit(solution)/shard_map/all_gather | solution.py:419
  51.5 17.3 %collective-permute-start = (bf16[3584]{0:T(1024)(128)(2,1)S(1)}, bf16[3584]{0:T(1024)(128)(2,1)S(1)}, u32[]{:S(2)}, u32[]{:S(2)}) collective-permute-start(bf16[3584]{0:T(1024)(128)(2,1)S(1)} %constant_dynamic-update-slice_fusion.5), channel_id=1, source_target_pairs={{0,1},{1,2},{2,3},{3,0},{4,5},{5,6},{6,7},{7,4},{8,9},{9,10},{10,1... | collective-permute-start | bytes 21512 | tf_op jit(solution)/shard_map/ppermute | solution.py:172
  51.5 17.5 %collective-permute-start.1 = (bf16[3584]{0:T(1024)(128)(2,1)S(1)}, bf16[3584]{0:T(1024)(128)(2,1)S(1)}, u32[]{:S(2)}, u32[]{:S(2)}) collective-permute-start(bf16[3584]{0:T(1024)(128)(2,1)S(1)} %constant_dynamic-update-slice_fusion.5), channel_id=1, source_target_pairs={{0,2},{1,3},{2,0},{3,1},{4,6},{5,7},{6,4},{7,5},{8,10},{9,11},{10,... | collective-permute-start | bytes 21512 | tf_op jit(solution)/shard_map/ppermute | solution.py:172
  52.7 16.5 %collective-permute-start.2 = (bf16[3584]{0:T(1024)(128)(2,1)S(1)}, bf16[3584]{0:T(1024)(128)(2,1)S(1)}, u32[]{:S(2)}, u32[]{:S(2)}) collective-permute-start(bf16[3584]{0:T(1024)(128)(2,1)S(1)} %constant_dynamic-update-slice_fusion.5), channel_id=1, source_target_pairs={{0,3},{1,0},{2,1},{3,2},{4,7},{5,4},{6,5},{7,6},{8,11},{9,8},{10,9... | collective-permute-start | bytes 21512 | tf_op jit(solution)/shard_map/ppermute | solution.py:172
  54.1 24.0 %collective-permute-start.7 = (bf16[256,2048]{1,0:T(8,128)(2,1)S(1)}, bf16[256,2048]{1,0:T(8,128)(2,1)}, u32[]{:S(2)}, u32[]{:S(2)}) collective-permute-start(bf16[256,2048]{1,0:T(8,128)(2,1)S(1)} %bitcast.270), channel_id=1, source_target_pairs={{0,1},{1,2},{2,3},{3,0},{4,5},{5,6},{6,7},{7,4},{8,9},{9,10},{10,1... | collective-permute-start | bytes 3145736 | tf_op jit(solution)/shard_map/ppermute | solution.py:172
  55.9 44.4 %collective-permute-start.8 = (bf16[256,2048]{1,0:T(8,128)(2,1)S(1)}, bf16[256,2048]{1,0:T(8,128)(2,1)}, u32[]{:S(2)}, u32[]{:S(2)}) collective-permute-start(bf16[256,2048]{1,0:T(8,128)(2,1)S(1)} %bitcast.271), channel_id=1, source_target_pairs={{0,3},{1,0},{2,1},{3,2},{4,7},{5,4},{6,5},{7,6},{8,11},{9,8},{10,9... | collective-permute-start | bytes 3145736 | tf_op jit(solution)/shard_map/ppermute | solution.py:172
  69.9 53.0 %collective-permute-start.3 = (bf16[256,2048]{1,0:T(8,128)(2,1)S(1)}, bf16[256,2048]{1,0:T(8,128)(2,1)S(1)}, u32[]{:S(2)}, u32[]{:S(2)}) collective-permute-start(bf16[256,2048]{1,0:T(8,128)(2,1)S(1)} %fusion.19), channel_id=1, source_target_pairs={{0,1},{1,2},{2,3},{3,0},{4,5},{5,6},{6,7},{7,4},{8,9},{9,10},{10,1... | collective-permute-start | bytes 3145736 | tf_op jit(solution)/shard_map/ppermute | solution.py:172
  73.2 72.0 %collective-permute-start.4 = (bf16[256,2048]{1,0:T(8,128)(2,1)S(1)}, bf16[256,2048]{1,0:T(8,128)(2,1)S(1)}, u32[]{:S(2)}, u32[]{:S(2)}) collective-permute-start(bf16[256,2048]{1,0:T(8,128)(2,1)S(1)} %fusion.19), channel_id=1, source_target_pairs={{0,3},{1,0},{2,1},{3,2},{4,7},{5,4},{6,5},{7,6},{8,11},{9,8},{10,9... | collective-permute-start | bytes 3145736 | tf_op jit(solution)/shard_map/ppermute | solution.py:172
  79.2 77.4 %collective-permute-start.9 = (bf16[128,2048]{1,0:T(8,128)(2,1)S(1)}, bf16[128,2048]{1,0:T(8,128)(2,1)S(1)}, u32[]{:S(2)}, u32[]{:S(2)}) collective-permute-start(bf16[128,2048]{1,0:T(8,128)(2,1)S(1)} %slice.184), channel_id=1, source_target_pairs={{0,1},{1,2},{2,3},{3,0},{4,5},{5,6},{6,7},{7,4},{8,9},{9,10},{10,1... | collective-permute-start | bytes 1572872 | tf_op jit(solution)/shard_map/ppermute | solution.py:172
  101.5 77.6 %collective-permute-start.10 = (bf16[128,2048]{1,0:T(8,128)(2,1)S(1)}, bf16[128,2048]{1,0:T(8,128)(2,1)S(1)}, u32[]{:S(2)}, u32[]{:S(2)}) collective-permute-start(bf16[128,2048]{1,0:T(8,128)(2,1)S(1)} %slice.185), channel_id=1, source_target_pairs={{0,3},{1,0},{2,1},{3,2},{4,7},{5,4},{6,5},{7,6},{8,11},{9,8},{10,9... | collective-permute-start | bytes 1572872 | tf_op jit(solution)/shard_map/ppermute | solution.py:172
  122.9 56.1 %collective-permute-start.5 = (bf16[128,2048]{1,0:T(8,128)(2,1)S(1)}, bf16[128,2048]{1,0:T(8,128)(2,1)S(1)}, u32[]{:S(2)}, u32[]{:S(2)}) collective-permute-start(bf16[128,2048]{1,0:T(8,128)(2,1)S(1)} %slice.182), channel_id=1, source_target_pairs={{0,1},{1,2},{2,3},{3,0},{4,5},{5,6},{6,7},{7,4},{8,9},{9,10},{10,1... | collective-permute-start | bytes 1572872 | tf_op jit(solution)/shard_map/ppermute | solution.py:172
  145.3 44.9 %collective-permute-start.6 = (bf16[128,2048]{1,0:T(8,128)(2,1)S(1)}, bf16[128,2048]{1,0:T(8,128)(2,1)S(1)}, u32[]{:S(2)}, u32[]{:S(2)}) collective-permute-start(bf16[128,2048]{1,0:T(8,128)(2,1)S(1)} %slice.183), channel_id=1, source_target_pairs={{0,3},{1,0},{2,1},{3,2},{4,7},{5,4},{6,5},{7,6},{8,11},{9,8},{10,9... | collective-permute-start | bytes 1572872 | tf_op jit(solution)/shard_map/ppermute | solution.py:172
  191.2 33.8 %collective-permute-start.18 = (bf16[64,2048]{1,0:T(8,128)(2,1)S(1)}, bf16[64,2048]{1,0:T(8,128)(2,1)S(1)}, u32[]{:S(2)}, u32[]{:S(2)}) collective-permute-start(bf16[64,2048]{1,0:T(8,128)(2,1)S(1)} %get-tuple-element.104), channel_id=1, source_target_pairs={{0,2},{1,1},{2,0},{3,3},{4,6},{5,5},{6,4},{7,7},{8,10},{9,9},{10,8... | collective-permute-start | bytes 786440 | tf_op jit(solution)/shard_map/ppermute | solution.py:416
  191.9 33.1 %collective-permute-start.17 = (bf16[64,2048]{1,0:T(8,128)(2,1)S(1)}, bf16[64,2048]{1,0:T(8,128)(2,1)S(1)}, u32[]{:S(2)}, u32[]{:S(2)}) collective-permute-start(bf16[64,2048]{1,0:T(8,128)(2,1)S(1)} %get-tuple-element.105), channel_id=1, source_target_pairs={{0,1},{1,0},{2,3},{3,2},{4,5},{5,4},{6,7},{7,6},{8,9},{9,8},{10,11... | collective-permute-start | bytes 786440 | tf_op jit(solution)/shard_map/ppermute | solution.py:416
  196.1 28.8 %collective-permute-start.16 = (bf16[64,2048]{1,0:T(8,128)(2,1)S(1)}, bf16[64,2048]{1,0:T(8,128)(2,1)S(1)}, u32[]{:S(2)}, u32[]{:S(2)}) collective-permute-start(bf16[64,2048]{1,0:T(8,128)(2,1)S(1)} %get-tuple-element.103), channel_id=1, source_target_pairs={{0,0},{1,3},{2,2},{3,1},{4,4},{5,7},{6,6},{7,5},{8,8},{9,11},{10,1... | collective-permute-start | bytes 786440 | tf_op jit(solution)/shard_map/ppermute | solution.py:416
  222.1 22.2 %collective-permute-start.14 = (bf16[2048,1024]{1,0:T(8,128)(2,1)}, bf16[2048,1024]{1,0:T(8,128)(2,1)}, u32[]{:S(2)}, u32[]{:S(2)}) collective-permute-start(bf16[2048,1024]{1,0:T(8,128)(2,1)} %convolution_convert_fusion.2), channel_id=1, source_target_pairs={{0,4},{4,0},{8,12},{12,8},{16,20},{20,16},{24,28},{28,24},{1,5},{5... | collective-permute-start | bytes 12582920 | tf_op jit(solution)/shard_map/ppermute | solution.py:247
  226.1 198.1 %reduce-scatter.2.cloned.1.call-start = ((), (), s32[]{:S(2)}) async-start(), calls=%async_computation.3 | async-start | bytes 2359296 | tf_op jit(solution)/shard_map/reduce_scatter | solution.py:444
  261.4 19.5 %collective-permute-start.15 = (bf16[2048,1024]{1,0:T(8,128)(2,1)}, bf16[2048,1024]{1,0:T(8,128)(2,1)}, u32[]{:S(2)}, u32[]{:S(2)}) collective-permute-start(bf16[2048,1024]{1,0:T(8,128)(2,1)} %convolution_convert_fusion.1), channel_id=1, source_target_pairs={{0,4},{4,0},{8,12},{12,8},{16,20},{20,16},{24,28},{28,24},{1,5},{5... | collective-permute-start | bytes 12582920 | tf_op jit(solution)/shard_map/ppermute | solution.py:247
  278.5 155.5 %collective-permute-start.67 = (bf16[4,128,1024]{2,1,0:T(8,128)(2,1)}, bf16[4,128,1024]{2,1,0:T(8,128)(2,1)S(1)}, u32[]{:S(2)}, u32[]{:S(2)}) collective-permute-start(bf16[4,128,1024]{2,1,0:T(8,128)(2,1)} %get-tuple-element.70), channel_id=1, source_target_pairs={{0,24},{4,28},{8,16},{12,20},{16,8},{20,12},{24,0},{28,4},{1,25},{... | collective-permute-start | bytes 3145736 | tf_op jit(solution)/shard_map/ppermute | solution.py:247
  280.6 153.3 %collective-permute-start.66 = (bf16[4,128,1024]{2,1,0:T(8,128)(2,1)}, bf16[4,128,1024]{2,1,0:T(8,128)(2,1)}, u32[]{:S(2)}, u32[]{:S(2)}) collective-permute-start(bf16[4,128,1024]{2,1,0:T(8,128)(2,1)} %get-tuple-element.71), channel_id=1, source_target_pairs={{0,16},{4,20},{8,24},{12,28},{16,0},{20,4},{24,8},{28,12},{1,17},{... | collective-permute-start | bytes 3145736 | tf_op jit(solution)/shard_map/ppermute | solution.py:247
  329.7 454.9 %all-gather.8.cloned.1.call-start = ((), (), s32[]{:S(2)}) async-start(), calls=%async_computation.4 | async-start | bytes 2359296 | tf_op jit(solution)/shard_map/all_gather | solution.py:467
  337.6 30.2 %collective-permute-start.24 = (bf16[4,128,1024]{2,1,0:T(8,128)(2,1)S(1)}, bf16[4,128,1024]{2,1,0:T(8,128)(2,1)S(1)}, u32[]{:S(2)}, u32[]{:S(2)}) collective-permute-start(bf16[4,128,1024]{2,1,0:T(8,128)(2,1)S(1)} %get-tuple-element.79), channel_id=1, source_target_pairs={{0,24},{4,28},{8,16},{12,20},{16,8},{20,12},{24,0},{28,4},{1,25},{... | collective-permute-start | bytes 3145736 | tf_op jit(solution)/shard_map/ppermute | solution.py:247
  338.8 55.7 %collective-permute-start.23 = (bf16[4,128,1024]{2,1,0:T(8,128)(2,1)S(1)}, bf16[4,128,1024]{2,1,0:T(8,128)(2,1)S(1)}, u32[]{:S(2)}, u32[]{:S(2)}) collective-permute-start(bf16[4,128,1024]{2,1,0:T(8,128)(2,1)S(1)} %get-tuple-element.80), channel_id=1, source_target_pairs={{0,16},{4,20},{8,24},{12,28},{16,0},{20,4},{24,8},{28,12},{1,17},{... | collective-permute-start | bytes 3145736 | tf_op jit(solution)/shard_map/ppermute | solution.py:247
  339.1 55.4 %collective-permute-start.22 = (bf16[4,128,1024]{2,1,0:T(8,128)(2,1)S(1)}, bf16[4,128,1024]{2,1,0:T(8,128)(2,1)S(1)}, u32[]{:S(2)}, u32[]{:S(2)}) collective-permute-start(bf16[4,128,1024]{2,1,0:T(8,128)(2,1)S(1)} %get-tuple-element.78), channel_id=1, source_target_pairs={{0,8},{4,12},{8,0},{12,4},{16,24},{20,28},{24,16},{28,20},{1,9},{5... | collective-permute-start | bytes 3145736 | tf_op jit(solution)/shard_map/ppermute | solution.py:247
  367.8 66.2 %collective-permute-start.65 = (bf16[4,128,1024]{2,1,0:T(8,128)(2,1)S(1)}, bf16[4,128,1024]{2,1,0:T(8,128)(2,1)}, u32[]{:S(2)}, u32[]{:S(2)}) collective-permute-start(bf16[4,128,1024]{2,1,0:T(8,128)(2,1)S(1)} %get-tuple-element.69), channel_id=1, source_target_pairs={{0,8},{4,12},{8,0},{12,4},{16,24},{20,28},{24,16},{28,20},{1,9},{5... | collective-permute-start | bytes 3145736 | tf_op jit(solution)/shard_map/ppermute | solution.py:247
  431.9 56.3 %collective-permute-start.25 = (bf16[1536,1024]{1,0:T(8,128)(2,1)}, bf16[1536,1024]{1,0:T(8,128)(2,1)}, u32[]{:S(2)}, u32[]{:S(2)}) collective-permute-start(bf16[1536,1024]{1,0:T(8,128)(2,1)} %convolution_convert_fusion), channel_id=1, source_target_pairs={{0,4},{4,0},{8,12},{12,8},{16,20},{20,16},{24,28},{28,24},{1,5},{5... | collective-permute-start | bytes 9437192 | tf_op jit(solution)/shard_map/ppermute | solution.py:247
  437.0 24.3 %collective-permute-start.69 = (bf16[128,1024]{1,0:T(8,128)(2,1)S(1)}, bf16[128,1024]{1,0:T(8,128)(2,1)S(1)}, u32[]{:S(2)}, u32[]{:S(2)}) collective-permute-start(bf16[128,1024]{1,0:T(8,128)(2,1)S(1)} %get-tuple-element.92), channel_id=1, source_target_pairs={{0,2},{1,3},{2,0},{3,1},{4,6},{5,7},{6,4},{7,5},{8,10},{9,11},{10,... | collective-permute-start | bytes 786440 | tf_op jit(solution)/shard_map/ppermute | solution.py:172
  437.9 23.5 %collective-permute-start.70 = (bf16[128,1024]{1,0:T(8,128)(2,1)S(1)}, bf16[128,1024]{1,0:T(8,128)(2,1)S(1)}, u32[]{:S(2)}, u32[]{:S(2)}) collective-permute-start(bf16[128,1024]{1,0:T(8,128)(2,1)S(1)} %get-tuple-element.91), channel_id=1, source_target_pairs={{0,3},{1,0},{2,1},{3,2},{4,7},{5,4},{6,5},{7,6},{8,11},{9,8},{10,9... | collective-permute-start | bytes 786440 | tf_op jit(solution)/shard_map/ppermute | solution.py:172
  461.4 24.3 %collective-permute-start.71 = (bf16[4,128,1024]{2,1,0:T(8,128)(2,1)S(1)}, bf16[4,128,1024]{2,1,0:T(8,128)(2,1)S(1)}, u32[]{:S(2)}, u32[]{:S(2)}) collective-permute-start(bf16[4,128,1024]{2,1,0:T(8,128)(2,1)S(1)} %bitcast_dynamic-update-slice_fusion.12.refs_0_), channel_id=1, source_target_pairs={{0,8},{4,12},{8,0},{12,4},{16,24},{20,28},{24,16},{28,20},{1,9},{5... | collective-permute-start | bytes 3145736 | tf_op jit(solution)/shard_map/ppermute | solution.py:247
  463.2 57.5 %collective-permute-start.72 = (bf16[4,128,1024]{2,1,0:T(8,128)(2,1)S(1)}, bf16[4,128,1024]{2,1,0:T(8,128)(2,1)}, u32[]{:S(2)}, u32[]{:S(2)}) collective-permute-start(bf16[4,128,1024]{2,1,0:T(8,128)(2,1)S(1)} %bitcast_dynamic-update-slice_fusion.12.refs_0_), channel_id=1, source_target_pairs={{0,16},{4,20},{8,24},{12,28},{16,0},{20,4},{24,8},{28,12},{1,17},{... | collective-permute-start | bytes 3145736 | tf_op jit(solution)/shard_map/ppermute | solution.py:247
  463.4 58.9 %collective-permute-start.73 = (bf16[4,128,1024]{2,1,0:T(8,128)(2,1)S(1)}, bf16[4,128,1024]{2,1,0:T(8,128)(2,1)}, u32[]{:S(2)}, u32[]{:S(2)}) collective-permute-start(bf16[4,128,1024]{2,1,0:T(8,128)(2,1)S(1)} %bitcast_dynamic-update-slice_fusion.12.refs_0_), channel_id=1, source_target_pairs={{0,24},{4,28},{8,16},{12,20},{16,8},{20,12},{24,0},{28,4},{1,25},{... | collective-permute-start | bytes 3145736 | tf_op jit(solution)/shard_map/ppermute | solution.py:247
  465.6 58.0 %collective-permute-start.74 = (bf16[4,128,1024]{2,1,0:T(8,128)(2,1)S(1)}, bf16[4,128,1024]{2,1,0:T(8,128)(2,1)S(1)}, u32[]{:S(2)}, u32[]{:S(2)}) collective-permute-start(bf16[4,128,1024]{2,1,0:T(8,128)(2,1)S(1)} %bitcast_dynamic-update-slice_fusion.12.refs_0_), channel_id=1, source_target_pairs={{0,4},{4,0},{8,12},{12,8},{16,20},{20,16},{24,28},{28,24},{1,5},{5... | collective-permute-start | bytes 3145736 | tf_op jit(solution)/shard_map/ppermute | solution.py:247
  485.7 53.3 %collective-permute-start.75 = (bf16[4,128,1024]{2,1,0:T(8,128)(2,1)S(1)}, bf16[4,128,1024]{2,1,0:T(8,128)(2,1)}, u32[]{:S(2)}, u32[]{:S(2)}) collective-permute-start(bf16[4,128,1024]{2,1,0:T(8,128)(2,1)S(1)} %collective-permute-done.71.refs_1_), channel_id=1, source_target_pairs={{0,4},{4,0},{8,12},{12,8},{16,20},{20,16},{24,28},{28,24},{1,5},{5... | collective-permute-start | bytes 3145736 | tf_op jit(solution)/shard_map/ppermute | solution.py:247
  488.2 38.3 %collective-permute-start.55 = (bf16[64,512]{1,0:T(8,128)(2,1)S(1)}, bf16[64,512]{1,0:T(8,128)(2,1)S(1)}, u32[]{:S(2)}, u32[]{:S(2)}) collective-permute-start(bf16[64,512]{1,0:T(8,128)(2,1)S(1)} %get-tuple-element.108), channel_id=1, source_target_pairs={{0,1},{1,2},{2,3},{3,0},{4,5},{5,6},{6,7},{7,4},{8,9},{9,10},{10,1... | collective-permute-start | bytes 196616 | tf_op jit(solution)/shard_map/ppermute | solution.py:172
  526.5 23.8 %collective-permute-start.28 = (bf16[128,2048]{1,0:T(8,128)(2,1)}, bf16[128,2048]{1,0:T(8,128)(2,1)}, u32[]{:S(2)}, u32[]{:S(2)}) collective-permute-start(bf16[128,2048]{1,0:T(8,128)(2,1)} %get-tuple-element.76), channel_id=1, source_target_pairs={{0,3},{1,0},{2,1},{3,2},{4,7},{5,4},{6,5},{7,6},{8,11},{9,8},{10,9... | collective-permute-start | bytes 1572872 | tf_op jit(solution)/shard_map/ppermute | solution.py:172
  527.2 27.4 %collective-permute-start.76 = (bf16[4,128,1024]{2,1,0:T(8,128)(2,1)}, bf16[4,128,1024]{2,1,0:T(8,128)(2,1)}, u32[]{:S(2)}, u32[]{:S(2)}) collective-permute-start(bf16[4,128,1024]{2,1,0:T(8,128)(2,1)} %collective-permute-done.72.refs_2_), channel_id=1, source_target_pairs={{0,4},{4,0},{8,12},{12,8},{16,20},{20,16},{24,28},{28,24},{1,5},{5... | collective-permute-start | bytes 3145736 | tf_op jit(solution)/shard_map/ppermute | solution.py:247
  528.3 29.2 %collective-permute-start.77 = (bf16[4,128,1024]{2,1,0:T(8,128)(2,1)}, bf16[4,128,1024]{2,1,0:T(8,128)(2,1)}, u32[]{:S(2)}, u32[]{:S(2)}) collective-permute-start(bf16[4,128,1024]{2,1,0:T(8,128)(2,1)} %collective-permute-done.73.refs_3_), channel_id=1, source_target_pairs={{0,4},{4,0},{8,12},{12,8},{16,20},{20,16},{24,28},{28,24},{1,5},{5... | collective-permute-start | bytes 3145736 | tf_op jit(solution)/shard_map/ppermute | solution.py:247
  539.0 32.7 %collective-permute-start.58 = (bf16[4,128,1024]{2,1,0:T(8,128)(2,1)S(1)}, bf16[4,128,1024]{2,1,0:T(8,128)(2,1)S(1)}, u32[]{:S(2)}, u32[]{:S(2)}) collective-permute-start(bf16[4,128,1024]{2,1,0:T(8,128)(2,1)S(1)} %fusion.38.refs_0_), channel_id=1, source_target_pairs={{0,8},{4,12},{8,0},{12,4},{16,24},{20,28},{24,16},{28,20},{1,9},{5... | collective-permute-start | bytes 3145736 | tf_op jit(solution)/shard_map/ppermute | solution.py:247
  539.5 32.5 %collective-permute-start.59 = (bf16[4,128,1024]{2,1,0:T(8,128)(2,1)S(1)}, bf16[4,128,1024]{2,1,0:T(8,128)(2,1)S(1)}, u32[]{:S(2)}, u32[]{:S(2)}) collective-permute-start(bf16[4,128,1024]{2,1,0:T(8,128)(2,1)S(1)} %fusion.38.refs_0_), channel_id=1, source_target_pairs={{0,16},{4,20},{8,24},{12,28},{16,0},{20,4},{24,8},{28,12},{1,17},{... | collective-permute-start | bytes 3145736 | tf_op jit(solution)/shard_map/ppermute | solution.py:247
  550.3 44.4 %collective-permute-start.60 = (bf16[4,128,1024]{2,1,0:T(8,128)(2,1)S(1)}, bf16[4,128,1024]{2,1,0:T(8,128)(2,1)S(1)}, u32[]{:S(2)}, u32[]{:S(2)}) collective-permute-start(bf16[4,128,1024]{2,1,0:T(8,128)(2,1)S(1)} %fusion.38.refs_0_), channel_id=1, source_target_pairs={{0,24},{4,28},{8,16},{12,20},{16,8},{20,12},{24,0},{28,4},{1,25},{... | collective-permute-start | bytes 3145736 | tf_op jit(solution)/shard_map/ppermute | solution.py:247
  557.5 58.3 %collective-permute-start.38 = (bf16[3,128,1024]{2,1,0:T(8,128)(2,1)S(1)}, bf16[3,128,1024]{2,1,0:T(8,128)(2,1)S(1)}, u32[]{:S(2)}, u32[]{:S(2)}) collective-permute-start(bf16[3,128,1024]{2,1,0:T(8,128)(2,1)S(1)} %get-tuple-element.85), channel_id=1, source_target_pairs={{0,24},{4,28},{8,16},{12,20},{16,8},{20,12},{24,0},{28,4},{1,25},{... | collective-permute-start | bytes 2359304 | tf_op jit(solution)/shard_map/ppermute | solution.py:247
  559.7 77.3 %collective-permute-start.29 = (bf16[256,2048]{1,0:T(8,128)(2,1)}, bf16[256,2048]{1,0:T(8,128)(2,1)}, u32[]{:S(2)}, u32[]{:S(2)}) collective-permute-start(bf16[256,2048]{1,0:T(8,128)(2,1)} %pad_maximum_fusion.2), channel_id=1, source_target_pairs={{0,3},{1,0},{2,1},{3,2},{4,7},{5,4},{6,5},{7,6},{8,11},{9,8},{10,9... | collective-permute-start | bytes 3145736 | tf_op jit(solution)/shard_map/ppermute | solution.py:172
  571.7 40.2 %collective-permute-start.50 = (f32[4096]{0:T(1024)S(1)}, f32[4096]{0:T(1024)S(1)}, u32[]{:S(2)}, u32[]{:S(2)}) collective-permute-start(f32[4096]{0:T(1024)S(1)} %fusion.99), channel_id=1, source_target_pairs={{0,8},{4,12},{8,0},{12,4},{16,24},{20,28},{24,16},{28,20},{1,9},{5... | collective-permute-start | bytes 49160 | tf_op jit(solution)/shard_map/ppermute | solution.py:247
  572.0 53.4 %collective-permute-start.37 = (bf16[3,128,1024]{2,1,0:T(8,128)(2,1)S(1)}, bf16[3,128,1024]{2,1,0:T(8,128)(2,1)S(1)}, u32[]{:S(2)}, u32[]{:S(2)}) collective-permute-start(bf16[3,128,1024]{2,1,0:T(8,128)(2,1)S(1)} %get-tuple-element.86), channel_id=1, source_target_pairs={{0,16},{4,20},{8,24},{12,28},{16,0},{20,4},{24,8},{28,12},{1,17},{... | collective-permute-start | bytes 2359304 | tf_op jit(solution)/shard_map/ppermute | solution.py:247
  595.7 34.0 %collective-permute-start.36 = (bf16[3,128,1024]{2,1,0:T(8,128)(2,1)S(1)}, bf16[3,128,1024]{2,1,0:T(8,128)(2,1)S(1)}, u32[]{:S(2)}, u32[]{:S(2)}) collective-permute-start(bf16[3,128,1024]{2,1,0:T(8,128)(2,1)S(1)} %get-tuple-element.84), channel_id=1, source_target_pairs={{0,8},{4,12},{8,0},{12,4},{16,24},{20,28},{24,16},{28,20},{1,9},{5... | collective-permute-start | bytes 2359304 | tf_op jit(solution)/shard_map/ppermute | solution.py:247
  611.9 31.6 %collective-permute-start.27 = (bf16[256,2048]{1,0:T(8,128)(2,1)}, bf16[256,2048]{1,0:T(8,128)(2,1)}, u32[]{:S(2)}, u32[]{:S(2)}) collective-permute-start(bf16[256,2048]{1,0:T(8,128)(2,1)} %pad_maximum_fusion.1), channel_id=1, source_target_pairs={{0,1},{1,2},{2,3},{3,0},{4,5},{5,6},{6,7},{7,4},{8,9},{9,10},{10,1... | collective-permute-start | bytes 3145736 | tf_op jit(solution)/shard_map/ppermute | solution.py:172
  615.8 52.3 %collective-permute-start.21 = (bf16[256,2048]{1,0:T(8,128)(2,1)}, bf16[256,2048]{1,0:T(8,128)(2,1)}, u32[]{:S(2)}, u32[]{:S(2)}) collective-permute-start(bf16[256,2048]{1,0:T(8,128)(2,1)} %get-tuple-element.82), channel_id=1, source_target_pairs={{0,3},{1,0},{2,1},{3,2},{4,7},{5,4},{6,5},{7,6},{8,11},{9,8},{10,9... | collective-permute-start | bytes 3145736 | tf_op jit(solution)/shard_map/ppermute | solution.py:172
  625.5 43.2 %collective-permute-start.61 = (bf16[4,128,1024]{2,1,0:T(8,128)(2,1)S(1)}, bf16[4,128,1024]{2,1,0:T(8,128)(2,1)}, u32[]{:S(2)}, u32[]{:S(2)}) collective-permute-start(bf16[4,128,1024]{2,1,0:T(8,128)(2,1)S(1)} %fusion.38.refs_0_), channel_id=1, source_target_pairs={{0,4},{4,0},{8,12},{12,8},{16,20},{20,16},{24,28},{28,24},{1,5},{5... | collective-permute-start | bytes 3145736 | tf_op jit(solution)/shard_map/ppermute | solution.py:247
  629.7 39.1 %collective-permute-start.62 = (bf16[4,128,1024]{2,1,0:T(8,128)(2,1)S(1)}, bf16[4,128,1024]{2,1,0:T(8,128)(2,1)}, u32[]{:S(2)}, u32[]{:S(2)}) collective-permute-start(bf16[4,128,1024]{2,1,0:T(8,128)(2,1)S(1)} %collective-permute-done.58.refs_1_), channel_id=1, source_target_pairs={{0,4},{4,0},{8,12},{12,8},{16,20},{20,16},{24,28},{28,24},{1,5},{5... | collective-permute-start | bytes 3145736 | tf_op jit(solution)/shard_map/ppermute | solution.py:247
  636.9 43.5 %collective-permute-start.63 = (bf16[4,128,1024]{2,1,0:T(8,128)(2,1)}, bf16[4,128,1024]{2,1,0:T(8,128)(2,1)}, u32[]{:S(2)}, u32[]{:S(2)}) collective-permute-start(bf16[4,128,1024]{2,1,0:T(8,128)(2,1)} %copy-done.8), channel_id=1, source_target_pairs={{0,4},{4,0},{8,12},{12,8},{16,20},{20,16},{24,28},{28,24},{1,5},{5... | collective-permute-start | bytes 3145736 | tf_op jit(solution)/shard_map/ppermute | solution.py:247
  643.6 38.6 %collective-permute-start.64 = (bf16[4,128,1024]{2,1,0:T(8,128)(2,1)}, bf16[4,128,1024]{2,1,0:T(8,128)(2,1)}, u32[]{:S(2)}, u32[]{:S(2)}) collective-permute-start(bf16[4,128,1024]{2,1,0:T(8,128)(2,1)} %copy-done.10), channel_id=1, source_target_pairs={{0,4},{4,0},{8,12},{12,8},{16,20},{20,16},{24,28},{28,24},{1,5},{5... | collective-permute-start | bytes 3145736 | tf_op jit(solution)/shard_map/ppermute | solution.py:247
  673.3 17.7 %collective-permute-start.41 = (bf16[128,1024]{1,0:T(8,128)(2,1)S(1)}, bf16[128,1024]{1,0:T(8,128)(2,1)S(1)}, u32[]{:S(2)}, u32[]{:S(2)}) collective-permute-start(bf16[128,1024]{1,0:T(8,128)(2,1)S(1)} %get-tuple-element.98), channel_id=1, source_target_pairs={{2,0},{1,1},{0,2},{3,3},{6,4},{5,5},{4,6},{7,7},{10,8},{9,9},{8,10... | collective-permute-start | bytes 786440 | tf_op jit(solution)/shard_map/ppermute | solution.py:472
  674.0 17.1 %collective-permute-start.40 = (bf16[128,1024]{1,0:T(8,128)(2,1)S(1)}, bf16[128,1024]{1,0:T(8,128)(2,1)S(1)}, u32[]{:S(2)}, u32[]{:S(2)}) collective-permute-start(bf16[128,1024]{1,0:T(8,128)(2,1)S(1)} %get-tuple-element.99), channel_id=1, source_target_pairs={{1,0},{0,1},{3,2},{2,3},{5,4},{4,5},{7,6},{6,7},{9,8},{8,9},{11,10... | collective-permute-start | bytes 786440 | tf_op jit(solution)/shard_map/ppermute | solution.py:472
  682.9 106.0 %collective-permute-start.20 = (bf16[256,2048]{1,0:T(8,128)(2,1)}, bf16[256,2048]{1,0:T(8,128)(2,1)}, u32[]{:S(2)}, u32[]{:S(2)}) collective-permute-start(bf16[256,2048]{1,0:T(8,128)(2,1)} %get-tuple-element.83), channel_id=1, source_target_pairs={{0,2},{1,3},{2,0},{3,1},{4,6},{5,7},{6,4},{7,5},{8,10},{9,11},{10,... | collective-permute-start | bytes 3145736 | tf_op jit(solution)/shard_map/ppermute | solution.py:172
  685.6 105.7 %collective-permute-start.19 = (bf16[256,2048]{1,0:T(8,128)(2,1)}, bf16[256,2048]{1,0:T(8,128)(2,1)}, u32[]{:S(2)}, u32[]{:S(2)}) collective-permute-start(bf16[256,2048]{1,0:T(8,128)(2,1)} %get-tuple-element.81), channel_id=1, source_target_pairs={{0,1},{1,2},{2,3},{3,0},{4,5},{5,6},{6,7},{7,4},{8,9},{9,10},{10,1... | collective-permute-start | bytes 3145736 | tf_op jit(solution)/shard_map/ppermute | solution.py:172
  691.0 42.0 %collective-permute-start.53 = (f32[512]{0:T(512)S(1)}, f32[512]{0:T(512)S(1)}, u32[]{:S(2)}, u32[]{:S(2)}) collective-permute-start(f32[512]{0:T(512)S(1)} %bitcast.299), channel_id=1, source_target_pairs={{1,0},{0,1},{3,2},{2,3},{5,4},{4,5},{7,6},{6,7},{9,8},{8,9},{11,10... | collective-permute-start | bytes 6152 | tf_op jit(solution)/shard_map/ppermute | solution.py:493
  691.1 65.5 %collective-permute-start.52 = (f32[512]{0:T(512)S(1)}, f32[512]{0:T(512)S(1)}, u32[]{:S(2)}, u32[]{:S(2)}) collective-permute-start(f32[512]{0:T(512)S(1)} %bitcast.298), channel_id=1, source_target_pairs={{0,0},{3,1},{2,2},{1,3},{4,4},{7,5},{6,6},{5,7},{8,8},{11,9},{10,1... | collective-permute-start | bytes 6152 | tf_op jit(solution)/shard_map/ppermute | solution.py:493
  693.3 64.2 %collective-permute-start.34 = (f32[2,512]{1,0:T(2,128)S(1)}, f32[2,512]{1,0:T(2,128)S(1)}, u32[]{:S(2)}, u32[]{:S(2)}) collective-permute-start(f32[2,512]{1,0:T(2,128)S(1)} %add.454), channel_id=1, source_target_pairs={{0,8},{4,12},{8,0},{12,4},{16,24},{20,28},{24,16},{28,20},{1,9},{5... | collective-permute-start | bytes 12296 | tf_op jit(solution)/shard_map/ppermute | solution.py:247
  733.1 59.2 %collective-permute-start.42 = (bf16[3,128,1024]{2,1,0:T(8,128)(2,1)S(1)}, bf16[3,128,1024]{2,1,0:T(8,128)(2,1)}, u32[]{:S(2)}, u32[]{:S(2)}) collective-permute-start(bf16[3,128,1024]{2,1,0:T(8,128)(2,1)S(1)} %pad_maximum_fusion.5.refs_0_), channel_id=1, source_target_pairs={{0,8},{4,12},{8,0},{12,4},{16,24},{20,28},{24,16},{28,20},{1,9},{5... | collective-permute-start | bytes 2359304 | tf_op jit(solution)/shard_map/ppermute | solution.py:247
  756.6 36.0 %collective-permute-start.43 = (bf16[3,128,1024]{2,1,0:T(8,128)(2,1)S(1)}, bf16[3,128,1024]{2,1,0:T(8,128)(2,1)}, u32[]{:S(2)}, u32[]{:S(2)}) collective-permute-start(bf16[3,128,1024]{2,1,0:T(8,128)(2,1)S(1)} %pad_maximum_fusion.5.refs_0_), channel_id=1, source_target_pairs={{0,16},{4,20},{8,24},{12,28},{16,0},{20,4},{24,8},{28,12},{1,17},{... | collective-permute-start | bytes 2359304 | tf_op jit(solution)/shard_map/ppermute | solution.py:247
  757.6 36.0 %collective-permute-start.44 = (bf16[3,128,1024]{2,1,0:T(8,128)(2,1)S(1)}, bf16[3,128,1024]{2,1,0:T(8,128)(2,1)}, u32[]{:S(2)}, u32[]{:S(2)}) collective-permute-start(bf16[3,128,1024]{2,1,0:T(8,128)(2,1)S(1)} %pad_maximum_fusion.5.refs_0_), channel_id=1, source_target_pairs={{0,24},{4,28},{8,16},{12,20},{16,8},{20,12},{24,0},{28,4},{1,25},{... | collective-permute-start | bytes 2359304 | tf_op jit(solution)/shard_map/ppermute | solution.py:247
  (81 other events, 1602.6 us)
Sparse Core Ops, SparseCore 0:
  50.6 65.3 all-gather.3
  226.3 46.2 all-gather.5
  329.8 60.3 reduce-scatter.1
  539.1 35.3 all-gather.7

commit v2 on v1

--- a/solution.py
+++ b/solution.py
@@ -309,6 +309,29 @@
     return out.reshape(groups * chips * rows, width)
 
 
+def lay_out(x, wide):
+    reps, lead, rows, cols = x.shape
+    tile = max(8, rows // 2)
+    groups, width = (1, 2 * cols * lead) if wide else (lead, 2 * cols)
+
+    def kernel(x_ref, out):
+        for side in range(2):
+            for l in range(lead):
+                at = side * cols + (l * 2 * cols if wide else 0)
+                out[0 if wide else l, 0, :, at : at + cols] = x_ref[side, l].astype(F32)
+
+    out = pl.pallas_call(
+        kernel,
+        grid=(reps // 2, rows // tile),
+        in_specs=[pl.BlockSpec((2, lead, tile, cols), lambda p, t: (p, 0, t, 0))],
+        out_specs=pl.BlockSpec((groups, 1, tile, width), lambda p, t: (0, p, t, 0)),
+        out_shape=jax.ShapeDtypeStruct((groups, reps // 2, rows, width), F32),
+        compiler_params=pltpu.CompilerParams(vmem_limit_bytes=48 << 20),
+        name="place",
+    )(x)
+    return out.reshape(groups * (reps // 2) * rows, width)
+
+
 def hold(*xs):
     return lax.optimization_barrier(xs)
 
@@ -348,15 +371,6 @@
             kind_of[(3 * s + j) % count, j] = (3 * s + j) // count
     round_of = np.argsort(kind_of, 1).astype(np.int32)
 
-    down = jnp.concatenate(
-        [
-            lax.dynamic_slice_in_dim(shrink_weight, rep * sub, sub, 0).reshape(sub, count, inner),
-            lax.dynamic_slice_in_dim(outproj_weight, rep * sub, sub, 0).reshape(sub, count, part),
-        ],
-        2,
-    )
-    down = swap_blocks(jnp.transpose(down, (1, 0, 2)), 0, count, me)
-
     packed = jnp.concatenate([norm_gain, norm_shift, outproj_bias, shrink_bias, inproj_bias])
     packed = gather_small(packed, count, me)
     gain, shift_all, outbias, shrbias = (
@@ -364,6 +378,12 @@
     )
     inbias = packed[:, 4 * part :].reshape(3, count, part)
     inbias = pick(inbias, me, 1).reshape(3 * part).astype(F32)
+
+    slices = lax.dynamic_slice_in_dim(inproj_weight.reshape(3, part, width), rep * sub, sub, 1)
+    arrived = jnp.stack([lax.ppermute(slices[j], "shard", forward[j]) for j in range(3)])
+    my_rounds = pick(jnp.asarray(round_of), me)
+    arrived = jnp.stack([pick(arrived, my_rounds[k]) for k in range(3)])
+    in_w = lax.all_gather(arrived, "rep", axis=1, tiled=True).reshape(3 * part, width)
 
     grad_own = out_grad.reshape(span, width)
     grads = gather_row(grad_own, count, me)
@@ -376,9 +396,6 @@
     xhat = centered * inv_std
     normed_own = (xhat * gain + shift_all).astype(BF16)
     normed = gather_row(normed_own, count, me)
-
-    down = lax.all_gather(down, "rep", axis=1, tiled=True).reshape(width, inner + part)
-    shrink_w, out_w = down[:, :inner], down[:, inner:]
 
     seg = segments.reshape(length)
     starts = jnp.sum((seg[None, :] < seg[:, None]).astype(jnp.int32), 1)
@@ -397,6 +414,19 @@
     blk = min(256, length)
     back = [[(b, a) for a, b in pairs] for pairs in forward]
 
+    down = jnp.concatenate(
+        [
+            lax.dynamic_slice_in_dim(shrink_weight, rep * sub, sub, 0).reshape(sub, count, inner),
+            lax.dynamic_slice_in_dim(outproj_weight, rep * sub, sub, 0).reshape(sub, count, part),
+        ],
+        2,
+    )
+    down = jnp.transpose(down, (1, 0, 2))
+    grads, down = hold(grads, down)
+    down = swap_blocks(down, 0, count, me)
+    shrink_w = lax.all_gather(down[:, :, :inner], "rep", axis=1, tiled=True).reshape(width, inner)
+    out_w = lax.all_gather(down[:, :, inner:], "rep", axis=1, tiled=True).reshape(width, part)
+
     def col_half(x, which):
         wide = x.shape[1] // 2
         return lax.dynamic_slice_in_dim(x, which * wide, wide, 1)
@@ -408,69 +438,69 @@
     normed_mine, normed_other = col_half(normed, core), col_half(normed, 1 - core)
     expanded = nt(normed, expand_weight) + expand_bias.astype(F32)
     hidden, slope = gelu_parts(expanded)
-    hidden = hidden.astype(BF16)
+    hidden, slope = hidden.astype(BF16), slope.astype(BF16)
     hidden_mine, hidden_other = col_half(hidden, core), col_half(hidden, 1 - core)
-
-    slices = lax.dynamic_slice_in_dim(inproj_weight.reshape(3, part, width), rep * sub, sub, 1)
-    grads, slices = hold(grads, slices)
-    arrived = jnp.stack([lax.ppermute(slices[j], "shard", forward[j]) for j in range(3)])
-    my_rounds = pick(jnp.asarray(round_of), me)
-    arrived = jnp.stack([pick(arrived, my_rounds[k]) for k in range(3)])
-    in_w = lax.all_gather(arrived, "rep", axis=1, tiled=True).reshape(3 * part, width)
-
-    blocks = inner // part
     shr_send = low_term(grads, hidden_other)
     shr_arrived = flip(shr_send, 1, reps)
-    grads_1, shr_send = hold(grads, shr_send)
-    d_up = (nn(grads_1, shrink_w) * slope).astype(BF16)
-    grads_2, d_up = hold(grads_1, d_up)
-    shr_sum = low_term(grads_2, hidden_mine, shr_arrived)
+
+    normed_1, shr_send = hold(normed, shr_send)
+    mixed = nt(normed_1, in_w) + inbias
+    grads_1, mixed = hold(grads, mixed)
+    shr_sum = low_term(grads_1, hidden_mine, shr_arrived)
     shr_total = reduce_chips(shr_sum.reshape(count, part, inner // 2), rep, reps)
-    d_up, shr_sum = hold(d_up, shr_sum)
+    mixed, shr_sum = hold(mixed, shr_sum)
+    attended, q_low, k_low, v_low, lse = attend(mixed, tables, seg_col, seg_row, blk)
+    grads_2, attended = hold(grads_1, attended)
+    g_out = tn(grads_2, attended).astype(BF16)
+    g_out_1 = lax.psum_scatter(
+        g_out.reshape(count, part, part), "rep", scatter_dimension=1, tiled=True
+    )
+    blocks = inner // part
+    grads_3, g_out = hold(grads_2, g_out)
+    d_up = (nn(grads_3, shrink_w) * slope.astype(F32)).astype(BF16)
     exp_send = low_term(d_up, normed_other)
     exp_arrived = flip(exp_send, 1, reps)
-    grads_3, exp_send = hold(grads_2, exp_send)
-    d_att = nn(grads_3, out_w).astype(BF16)
-    d_up_1, d_att = hold(d_up, d_att)
+    hidden_1, exp_send = hold(hidden, exp_send)
+    branches = (nt(hidden_1, shrink_w) + nt(attended, out_w)).astype(BF16)
+    branches_sum = scatter_direct(branches, count, me)
+    d_up_1, branches = hold(d_up, branches)
     exp_sum = low_term(d_up_1, normed_mine, exp_arrived)
     exp_total = reduce_chips(exp_sum.reshape(blocks, part, width // 2), rep, reps)
-
-    normed_1, exp_sum = hold(normed, exp_sum)
-    mixed = nt(normed_1, in_w) + inbias
-    attended, q_low, k_low, v_low, lse = attend(mixed, tables, seg_col, seg_row, blk)
-    grads_4, attended = hold(grads_3, attended)
-    g_out = tn(grads_4, attended).astype(BF16)
-    hidden_1, g_out = hold(hidden, g_out)
-    g_out = lax.psum_scatter(
-        g_out.reshape(count, part, part), "rep", scatter_dimension=1, tiled=True
-    )
     g_shr = shr_total()
     g_shr = swap_blocks(g_shr, 0, count, me)
-    branches = (nt(hidden_1, shrink_w) + nt(attended, out_w)).astype(BF16)
-    branches_sum = scatter_direct(branches, count, me)
-    shr_pieces = spread(g_shr, reps)
+    g_shr = lax.all_gather(g_shr, "rep", axis=0)
+    grads_4, exp_sum = hold(grads_3, exp_sum)
+    d_att = nn(grads_4, out_w).astype(BF16)
+
+    d_q, d_k, d_v = attend_back(q_low, k_low, v_low, d_att, lse, tables, seg_col, seg_row, blk)
+    d_mixed = jnp.concatenate([d_q, d_k, d_v], 1)
+    in_send = low_term(d_mixed, normed_other)
+    in_arrived = flip(in_send, 1, reps)
     g_exp = exp_total()
     exp_pieces = spread(g_exp, reps)
-
-    d_att, branches, g_exp = hold(d_att, branches, g_exp)
-    d_q, d_k, d_v = attend_back(q_low, k_low, v_low, d_att, lse, tables, seg_col, seg_row, blk)
-    d_mixed = jnp.concatenate([d_q, d_k, d_v], 1)
-    g_out, d_mixed = hold(g_out, d_mixed)
-    in_send = low_term(d_mixed, normed_other)
-    in_arrived = flip(in_send, 1, reps)
-    g_out = jnp.transpose(swap_blocks(g_out, 0, count, me), (1, 0, 2)).reshape(sub, width)
-    in_sum = low_term(d_mixed, normed_mine, in_arrived)
+    d_mixed_1, in_send, g_exp = hold(d_mixed, in_send, g_exp)
+    in_sum = low_term(d_mixed_1, normed_mine, in_arrived)
     in_total = reduce_chips(in_sum.reshape(3, part, width // 2), rep, reps)
-    d_up_3, in_sum = hold(d_up_1, in_sum)
-    d_normed = (nn(d_up_3, expand_weight) + nn(d_mixed, in_w)).astype(BF16)
+    d_mixed_2, in_sum = hold(d_mixed_1, in_sum)
+    d_normed = nn(d_up_1, expand_weight) + nn(d_mixed_2, in_w)
+    both = jnp.stack([jnp.sum(d_normed * normed.astype(F32), 0), jnp.sum(d_normed, 0)])
+    d_normed = d_normed.astype(BF16)
+    g_out_1, d_normed = hold(g_out_1, d_normed)
     d_normed = scatter_row(d_normed, count, me)
-    g_out = lax.all_gather(g_out, "rep", axis=0, tiled=True).astype(F32)
-
-    g_shr = assemble(shr_pieces, rep, True)
+
+    b_out = jnp.sum(lax.dynamic_slice_in_dim(grads, me * part, part, 1), 0, dtype=F32)
+    b_exp = jnp.sum(d_up_1, 0, dtype=F32)
+    b_in = jnp.sum(d_mixed_2, 0, dtype=F32)
+    both = jnp.sum(swap_blocks(both.reshape(2, count, part), 1, count, me), 1)
+    sums = jnp.concatenate([both[0], both[1], b_out, b_exp, b_in])
+
     kinds = pick(jnp.asarray(kind_of), me)
     g_in = in_total()
     g_in = jnp.stack([lax.ppermute(pick(g_in, kinds[j]), "shard", back[j]) for j in range(3)])
     in_pieces = spread(g_in, reps)
+    g_out = jnp.transpose(swap_blocks(g_out_1, 0, count, me), (1, 0, 2)).reshape(sub, width)
+    g_out = lax.all_gather(g_out, "rep", axis=0, tiled=True).astype(F32)
+    g_shr = lay_out(g_shr, True)
     g_exp = assemble(exp_pieces, rep, False)
     g_in = assemble(in_pieces, rep, False)
     block_output = (residual + (branches_sum + (outbias + shrbias))).astype(BF16)
@@ -482,25 +512,18 @@
         - xhat * jnp.mean(d_hat * xhat, -1, keepdims=True)
     )
 
-    b_out = jnp.sum(lax.dynamic_slice_in_dim(grads, me * part, part, 1), 0, dtype=F32)
-    b_exp = jnp.sum(d_up, 0, dtype=F32)
-    b_in = jnp.sum(d_mixed, 0, dtype=F32)
-    sums = jnp.concatenate([b_out, b_exp, b_in])
     for bit in range(bits):
         sums = sums + flip(sums, 1 << bit, reps)
-    b_out, b_exp, b_in = sums[:part], sums[part : part + inner], sums[part + inner :]
-    b_in = b_in.reshape(3, part)
+    b_norm, b_shift, b_out = sums[:part], sums[part : 2 * part], sums[2 * part : 3 * part]
+    b_gain = (b_norm - norm_shift.astype(F32) * b_shift) / norm_gain.astype(F32)
+    b_exp, b_in = sums[3 * part : 3 * part + inner], sums[3 * part + inner :].reshape(3, part)
     b_in = jnp.concatenate([lax.ppermute(pick(b_in, kinds[j]), "shard", back[j]) for j in range(3)])
-    both = jnp.stack([jnp.sum(d_normed * xhat, 0), jnp.sum(d_normed, 0)])
-    both = jnp.sum(swap_blocks(both.reshape(2, count, part), 1, count, me), 1)
-    for bit in range(bits):
-        both = both + flip(both, 1 << bit, reps)
 
     return (
         block_output[None],
         token_grad[None],
-        both[0],
-        both[1],
+        b_gain,
+        b_shift,
         g_in,
         b_in,
         g_out,

time: 827 us -> 857 us (1.036)
  the two profiles are of different devices: /device:TPU:25 before, /device:TPU:0 now
where the time goes in v2:
time: 857 us; the launch traced here: 847 us
  waiting for transfers between devices  369 us (43%)
  matrix products  148 us (17%)
  starting transfers between devices  114 us (13%)
  Pallas kernels  79.1 us (9%)
  local copies, waits for them, and re-layouts  66.4 us (8%)
  other arithmetic  42.8 us (5%)
  between operations  27.3 us (3%)
    ppermute x30, waiting for transfers between devices, shift(): lax.ppermute(x, 'shard', [(i, (i + offset) % count) for i in range(count)])  151 us
    ppermute x29, waiting for transfers between devices, flip(): return lax.ppermute(x, 'rep', [(i, i ^ mask) for i in range(reps)])  128 us
    ppermute x3, waiting for transfers between devices, local(): lax.ppermute(pick(b_in, kinds[j]), 'shard', back[j])  86.1 us
    ppermute x30, starting transfers between devices, shift(): lax.ppermute(x, 'shard', [(i, (i + offset) % count) for i in range(count)])  74.9 us
    dot_general x4, matrix products, nt(): lax.dot_general(a, b, (((1,), (1,)), ((), ())), preferred_element_type=F32)  51.5 us
    dot_general x7, matrix products, tn(): lax.dot_general(a, b, (((0,), (0,)), ((), ())), preferred_element_type=F32)  49.3 us
    dot_general x4, matrix products, nn(): lax.dot_general(a, b, (((1,), (0,)), ((), ())), preferred_element_type=F32)  47.6 us
    pallas_call x1, Pallas kernels, attend_back(): pl.pallas_call(functools.partial(attend_back_kernel, blk), grid=(pairs,),...  25.6 us
  transfers between devices with their start and end apart: 74, of which 28 were waited for; matrix products, arithmetic and copies ran while one was open for 29% of the time, Pallas kernels for 9%

profile of v2, /device:TPU:0, one launch (start us, length us, event | category | flops | bytes accessed | tf_op | source)
XLA Modules:
  0.0 846.7 jit_solution(1892187855284025518)
XLA Ops:
  9.4 6.0 collective-permute-start.13
  24.5 3.1 collective-permute-done.12
  30.0 3.3 collective-permute-start.7
  37.0 2.6 reshape.242
  39.6 2.5 broadcast.84.clone
  43.8 14.8 %collective-permute-done.7 = bf16[256,2048]{1,0:T(8,128)(2,1)} collective-permute-done((bf16[256,2048]{1,0:T(8,128)(2,1)S(1)}, bf16[256,2048]{1,0:T(8,128)(2,1)}, u32[]{:S(2)}, u32[]{:S(2)}) %collective-permute-start.7) | collective-permute-done | bytes 1048608 | tf_op jit(solution)/shard_map/ppermute | solution.py:172
  60.5 20.5 %collective-permute-done.8 = bf16[256,2048]{1,0:T(8,128)(2,1)} collective-permute-done((bf16[256,2048]{1,0:T(8,128)(2,1)S(1)}, bf16[256,2048]{1,0:T(8,128)(2,1)}, u32[]{:S(2)}, u32[]{:S(2)}) %collective-permute-start.8) | collective-permute-done | bytes 1048608 | tf_op jit(solution)/shard_map/ppermute | solution.py:172
  82.1 2.8 collective-permute-start.10
  89.5 2.8 collective-permute-done.9
  93.1 8.8 %collective-permute-done.10 = bf16[128,2048]{1,0:T(8,128)(2,1)S(1)} collective-permute-done((bf16[128,2048]{1,0:T(8,128)(2,1)S(1)}, bf16[128,2048]{1,0:T(8,128)(2,1)S(1)}, u32[]{:S(2)}, u32[]{:S(2)}) %collective-permute-start.10) | collective-permute-done | bytes 524320 | tf_op jit(solution)/shard_map/ppermute | solution.py:172
  102.7 2.7 constant_dynamic-slice_fusion.8
  106.1 2.5 collective-permute-start.16
  109.8 8.2 collective-permute-done.15
  118.1 13.1 %collective-permute-done.16 = bf16[64,2560]{1,0:T(8,128)(2,1)S(1)} collective-permute-done((bf16[64,2560]{1,0:T(8,128)(2,1)S(1)}, bf16[64,2560]{1,0:T(8,128)(2,1)S(1)}, u32[]{:S(2)}, u32[]{:S(2)}) %collective-permute-start.16) | collective-permute-done | bytes 327712 | tf_op jit(solution)/shard_map/ppermute | solution.py:172
  133.4 7.0 collective-permute-start
  147.2 3.3 collective-permute-start.4
  151.6 23.2 %collective-permute-done.3 = bf16[256,2048]{1,0:T(8,128)(2,1)S(1)} collective-permute-done((bf16[256,2048]{1,0:T(8,128)(2,1)}, bf16[256,2048]{1,0:T(8,128)(2,1)S(1)}, u32[]{:S(2)}, u32[]{:S(2)}) %collective-permute-start.3) | collective-permute-done | bytes 1048608 | tf_op jit(solution)/shard_map/ppermute | solution.py:172
  174.8 17.9 %collective-permute-start.5 = (bf16[128,2048]{1,0:T(8,128)(2,1)S(1)}, bf16[128,2048]{1,0:T(8,128)(2,1)S(1)}, u32[]{:S(2)}, u32[]{:S(2)}) collective-permute-start(bf16[128,2048]{1,0:T(8,128)(2,1)S(1)} %slice.190), channel_id=1, source_target_pairs={{0,1},{1,2},{2,3},{3,0},{4,5},{5,6},{6,7},{7,4},{8,9},{9,10},{10,1... | collective-permute-start | bytes 1572872 | tf_op jit(solution)/shard_map/ppermute | solution.py:172
  195.7 3.5 collective-permute-start.6
  200.6 8.8 %collective-permute-done.5 = bf16[128,2048]{1,0:T(8,128)(2,1)S(1)} collective-permute-done((bf16[128,2048]{1,0:T(8,128)(2,1)S(1)}, bf16[128,2048]{1,0:T(8,128)(2,1)S(1)}, u32[]{:S(2)}, u32[]{:S(2)}) %collective-permute-start.5) | collective-permute-done | bytes 524320 | tf_op jit(solution)/shard_map/ppermute | solution.py:172
  209.5 7.4 collective-permute-done.6
  216.9 16.4 %multiply_convert_fusion.1 = (bf16[1024,2048]{1,0:T(8,128)(2,1)S(1)}, f32[1024,2048]{1,0:T(8,128)}) fusion(f32[2048]{0:T(1024)S(1)} %convert_element_type.258, bf16[1024,2048]{1,0:T(8,128)(2,1)S(1)} %bitcast.270, bf16[2048,2048]{1,0:T(8,128)(2,1)} %param.24), kind=kOutput, calls=%fused_computation.10 | convolution fusion | flops 8610906112 | bytes 25174016 | tf_op jit(solution)/shard_map/dot_general | solution.py:22
  233.3 9.9 %convolution_convert_fusion.2 = bf16[2048,1024]{1,0:T(8,128)(2,1)} fusion(bf16[1024,2048]{1,0:T(8,128)(2,1)} %bitcast.11, bf16[1024,2048]{1,0:T(8,128)(2,1)S(1)} %get-tuple-element.46, s32[]{:T(128)S(6)} %select_n.251), kind=kOutput, calls=%fused_computation.19 | convolution fusion | flops 4297064448 | bytes 10485764 | tf_op jit(solution)/shard_map/dot_general | solution.py:30
  243.9 3.0 multiply_sine_fusion
  246.9 2.7 concatenate.36.slo_ref
  255.3 11.9 %convolution_add_fusion.q_ref.k_ref.v_ref = f32[1024,1536]{1,0:T(8,128)} fusion(bf16[1024,2048]{1,0:T(8,128)(2,1)} %bitcast.271, bf16[1536,2048]{1,0:T(8,128)(2,1)} %bitcast.312, f32[1536]{0:T(1024)S(1)} %reshape.258), kind=kOutput, calls=%fused_computation.14 | convolution fusion | flops 6444023808 | bytes 16783360 | tf_op jit(solution)/shard_map/dot_general | solution.py:22
  267.2 7.7 add_convert_fusion.3
  274.9 24.0 %attend.1 = (bf16[1024,512]{1,0:T(8,128)(2,1)}, bf16[1024,512]{1,0:T(8,128)(2,1)}, bf16[1024,512]{1,0:T(8,128)(2,1)}, bf16[1024,512]{1,0:T(8,128)(2,1)}, f32[4,2,1024]{2,1,0:T(2,128)}) custom-call(f32[1024,1536]{1,0:T(8,128)} %convolution_add_fusion.q_ref.k_ref.v_ref, f32[1024,1536]{1,0:T(8,128)} %convolution_add_fusion.q_ref.k_ref.v_ref, ...), custom_call_target="tpu_custom_call" | custom-call | tf_op jit(solution)/shard_map/attend/pallas_call | solution.py:92
  298.9 6.2 convolution_convert_fusion.3
  306.8 2.5 collective-permute-start.64
  310.8 17.8 %multiply_convert_fusion = bf16[1024,2048]{1,0:T(8,128)(2,1)S(1)} fusion(f32[1024,2048]{1,0:T(8,128)} %get-tuple-element.129, f32[2048]{0:T(1024)S(1)} %convert_element_type.258, bf16[1024,2048]{1,0:T(8,128)(2,1)} %bitcast.11, bf16[2048,2048]{1,0:T(8,128)(2,1)} %bitcast.310), kind=kOutput, calls=%fused_computation.7 | convolution fusion | flops 8633974784 | bytes 25174016 | tf_op jit(solution)/shard_map/dot_general | solution.py:26
  328.6 6.2 convolution_convert_fusion.1
  335.9 28.5 %collective-permute-done.63 = bf16[4,128,1024]{2,1,0:T(8,128)(2,1)S(1)} collective-permute-done((bf16[4,128,1024]{2,1,0:T(8,128)(2,1)}, bf16[4,128,1024]{2,1,0:T(8,128)(2,1)S(1)}, u32[]{:S(2)}, u32[]{:S(2)}) %collective-permute-start.63) | collective-permute-done | bytes 1048608 | tf_op jit(solution)/shard_map/ppermute | solution.py:247
  371.2 7.0 collective-permute-done.65
  378.3 10.2 %collective-permute-done.66 = bf16[128,1024]{1,0:T(8,128)(2,1)S(1)} collective-permute-done((bf16[128,1024]{1,0:T(8,128)(2,1)S(1)}, bf16[128,1024]{1,0:T(8,128)(2,1)S(1)}, u32[]{:S(2)}, u32[]{:S(2)}) %collective-permute-start.66) | collective-permute-done | bytes 262176 | tf_op jit(solution)/shard_map/ppermute | solution.py:172
  389.8 14.6 %fusion.64 = f32[1024,2048]{1,0:T(8,128)} fusion(bf16[1024,2048]{1,0:T(8,128)(2,1)} %copy-done.45, bf16[2048,2048]{1,0:T(8,128)(2,1)} %bitcast.311), kind=kOutput, calls=%fused_computation.197 | convolution fusion | flops 8589934592 | bytes 20971520 | tf_op jit(solution)/shard_map/dot_general | solution.py:22
  404.5 8.6 %add_convert_fusion.1 = bf16[1024,2048]{1,0:T(8,128)(2,1)} fusion(f32[1024,2048]{1,0:T(8,128)} %fusion.64, bf16[1024,512]{1,0:T(8,128)(2,1)S(1)} %copy-done.44, bf16[2048,512]{1,0:T(8,128)(2,1)} %bitcast.316), kind=kOutput, calls=%fused_computation.6 | convolution fusion | flops 2151677952 | bytes 15728640 | tf_op jit(solution)/shard_map/dot_general | solution.py:22
  413.1 8.0 add_convert_fusion
  421.1 5.5 convolution_convert_fusion.4.g_ref
  426.6 25.6 %attend_back.1 = (bf16[1024,512]{1,0:T(8,128)(2,1)}, bf16[1024,512]{1,0:T(8,128)(2,1)}, bf16[1024,512]{1,0:T(8,128)(2,1)}) custom-call(bf16[1024,512]{1,0:T(8,128)(2,1)} %get-tuple-element.48.q_ref, bf16[1024,512]{1,0:T(8,128)(2,1)} %get-tuple-element.49.k_ref, bf16[1024,512]{1,0:T(8,128)(2,1)} %get-tuple-element.50.v_ref, ...), custom_call_target="tpu_custom_call" | custom-call | tf_op jit(solution)/shard_map/attend_back/pallas_call | solution.py:152
  455.0 4.9 convolution_convert_fusion
  467.3 13.4 %fusion.65 = f32[1024,2048]{1,0:T(8,128)} fusion(bf16[1024,2048]{1,0:T(8,128)(2,1)S(1)} %copy-done.12, bf16[2048,2048]{1,0:T(8,128)(2,1)} %param.24), kind=kOutput, calls=%fused_computation.198 | convolution fusion | flops 8589934592 | bytes 20971520 | tf_op jit(solution)/shard_map/dot_general | solution.py:26
  482.4 5.6 collective-permute-start.20
  490.7 22.0 %collective-permute-done.23 = bf16[4,128,1024]{2,1,0:T(8,128)(2,1)S(1)} collective-permute-done((bf16[4,128,1024]{2,1,0:T(8,128)(2,1)S(1)}, bf16[4,128,1024]{2,1,0:T(8,128)(2,1)S(1)}, u32[]{:S(2)}, u32[]{:S(2)}) %collective-permute-start.23) | collective-permute-done | bytes 1048608 | tf_op jit(solution)/shard_map/ppermute | solution.py:247
  516.9 6.3 add_convert_fusion.4
  523.2 10.9 %fusion.60 = (f32[2048]{0:T(1024)S(1)}, f32[2048]{0:T(1024)S(1)}, bf16[1024,2048]{1,0:T(8,128)(2,1)}) fusion(bf16[4,256,2048]{2,1,0:T(8,128)(2,1)S(1)} %copy-done.16, f32[1024,2048]{1,0:T(8,128)} %fusion.65, bf16[1024,1536]{1,0:T(8,128)(2,1)S(1)} %copy-done.6, bf16[1536,2048]{1,0:T(8,128)(2,1)S(1)} %bitcast.315), kind=kOutput, calls=%fused_computation.193 | convolution fusion | flops 6455029760 | bytes 26230784 | tf_op jit(solution)/shard_map/dot_general | solution.py:26
  534.3 5.2 collective-permute-start.30
  550.1 2.9 dynamic-slice_bitcast_fusion.16
  553.0 38.2 %collective-permute-done.56.refs_2_ = bf16[4,128,1024]{2,1,0:T(8,128)(2,1)S(1)} collective-permute-done((bf16[4,128,1024]{2,1,0:T(8,128)(2,1)S(1)}, bf16[4,128,1024]{2,1,0:T(8,128)(2,1)S(1)}, u32[]{:S(2)}, u32[]{:S(2)}) %collective-permute-start.56) | collective-permute-done | bytes 1048608 | tf_op jit(solution)/shard_map/ppermute | solution.py:247
  591.2 3.8 collective-permute-start.28
  595.1 22.7 %collective-permute-done.53 = bf16[64,512]{1,0:T(8,128)(2,1)S(1)} collective-permute-done((bf16[64,512]{1,0:T(8,128)(2,1)S(1)}, bf16[64,512]{1,0:T(8,128)(2,1)S(1)}, u32[]{:S(2)}, u32[]{:S(2)}) %collective-permute-start.53) | collective-permute-done | bytes 65568 | tf_op jit(solution)/shard_map/ppermute | solution.py:172
  637.4 24.7 %collective-permute-done.35 = f32[5120]{0:T(1024)S(1)} collective-permute-done((f32[5120]{0:T(1024)}, f32[5120]{0:T(1024)S(1)}, u32[]{:S(2)}, u32[]{:S(2)}) %collective-permute-start.35) | collective-permute-done | bytes 20512 | tf_op jit(solution)/shard_map/ppermute | solution.py:247
  665.8 2.5 collective-permute-start.29
  678.2 3.1 collective-permute-start.41
  681.4 3.6 collective-permute-start.51
  685.1 76.1 %collective-permute-done.51 = f32[512]{0:T(512)S(1)} collective-permute-done((f32[512]{0:T(512)S(1)}, f32[512]{0:T(512)S(1)}, u32[]{:S(2)}, u32[]{:S(2)}) %collective-permute-start.51) | collective-permute-done | bytes 2080 | tf_op jit(solution)/shard_map/ppermute | solution.py:520
  765.2 10.0 %collective-permute-done.50 = f32[512]{0:T(512)S(1)} collective-permute-done((f32[512]{0:T(512)S(1)}, f32[512]{0:T(512)S(1)}, u32[]{:S(2)}, u32[]{:S(2)}) %collective-permute-start.50) | collective-permute-done | bytes 2080 | tf_op jit(solution)/shard_map/ppermute | solution.py:520
  777.7 3.4 collective-permute-start.44
  781.8 10.9 %assemble.3 = f32[4,4,128,2048]{3,2,1,0:T(8,128)} custom-call(s32[2]{0:T(128)S(1)} %pad_add_fusion.place_ref, bf16[4,128,1024]{2,1,0:T(8,128)(2,1)S(1)} %fusion.29.refs_0_, bf16[4,128,1024]{2,1,0:T(8,128)(2,1)S(1)} %collective-permute-done.55.refs_1_, bf16[4,128,1024]{2,1,0:T(8,128)(2,1)S(1)} %collective-permute-done.56.refs_2_, ...), custom_call_target="tpu_custom_call" | custom-call | tf_op jit(solution)/shard_map/assemble/pallas_call | solution.py:295
  797.7 10.7 %collective-permute-done.43.refs_2_ = bf16[3,128,1024]{2,1,0:T(8,128)(2,1)S(1)} collective-permute-done((bf16[3,128,1024]{2,1,0:T(8,128)(2,1)S(1)}, bf16[3,128,1024]{2,1,0:T(8,128)(2,1)S(1)}, u32[]{:S(2)}, u32[]{:S(2)}) %collective-permute-start.43) | collective-permute-done | bytes 786464 | tf_op jit(solution)/shard_map/ppermute | solution.py:247
  808.9 6.6 fusion.15
  816.4 8.1 assemble.2
  824.5 10.5 %place.1 = f32[1,4,128,8192]{3,2,1,0:T(8,128)} custom-call(bf16[8,4,128,1024]{3,2,1,0:T(8,128)(2,1)} %all-gather.14.cloned.1.call-done.x_ref), custom_call_target="tpu_custom_call" | custom-call | tf_op jit(solution)/shard_map/place/pallas_call | solution.py:323
  835.0 4.1 convert_element_type.314
  (364 shorter events, 128.1 us)
Async XLA Ops:
  7.2 248.1 %all-gather.6.cloned.1.call-start = ((), (), s32[]{:S(2)}) async-start(), calls=%async_computation.1 | async-start | bytes 7077888 | tf_op jit(solution)/shard_map/all_gather | solution.py:386
  9.4 15.1 %collective-permute-start.13 = (bf16[64,2048]{1,0:T(8,128)(2,1)}, bf16[64,2048]{1,0:T(8,128)(2,1)}, u32[]{:S(2)}, u32[]{:S(2)}) collective-permute-start(bf16[64,2048]{1,0:T(8,128)(2,1)} %get-tuple-element.69), channel_id=1, source_target_pairs={{0,2},{1,1},{2,0},{3,3},{4,6},{5,5},{6,4},{7,7},{8,10},{9,9},{10,8... | collective-permute-start | bytes 786440 | tf_op jit(solution)/shard_map/ppermute | solution.py:383
  15.4 12.2 %collective-permute-start.12 = (bf16[64,2048]{1,0:T(8,128)(2,1)}, bf16[64,2048]{1,0:T(8,128)(2,1)}, u32[]{:S(2)}, u32[]{:S(2)}) collective-permute-start(bf16[64,2048]{1,0:T(8,128)(2,1)} %get-tuple-element.68), channel_id=1, source_target_pairs={{0,1},{1,0},{2,3},{3,2},{4,5},{5,4},{6,7},{7,6},{8,9},{9,8},{10,11... | collective-permute-start | bytes 786440 | tf_op jit(solution)/shard_map/ppermute | solution.py:383
  16.1 11.6 %collective-permute-start.11 = (bf16[64,2048]{1,0:T(8,128)(2,1)S(1)}, bf16[64,2048]{1,0:T(8,128)(2,1)}, u32[]{:S(2)}, u32[]{:S(2)}) collective-permute-start(bf16[64,2048]{1,0:T(8,128)(2,1)S(1)} %get-tuple-element.67), channel_id=1, source_target_pairs={{0,0},{1,3},{2,2},{3,1},{4,4},{5,7},{6,6},{7,5},{8,8},{9,11},{10,1... | collective-permute-start | bytes 786440 | tf_op jit(solution)/shard_map/ppermute | solution.py:383
  29.9 280.9 %all-gather.8.cloned.1.call-start = ((), (), s32[]{:S(2)}) async-start(), calls=%async_computation.2 | async-start | bytes 9437184 | tf_op jit(solution)/shard_map/all_gather | solution.py:427
  30.0 28.7 %collective-permute-start.7 = (bf16[256,2048]{1,0:T(8,128)(2,1)S(1)}, bf16[256,2048]{1,0:T(8,128)(2,1)}, u32[]{:S(2)}, u32[]{:S(2)}) collective-permute-start(bf16[256,2048]{1,0:T(8,128)(2,1)S(1)} %bitcast.266), channel_id=1, source_target_pairs={{0,1},{1,2},{2,3},{3,0},{4,5},{5,6},{6,7},{7,4},{8,9},{9,10},{10,1... | collective-permute-start | bytes 3145736 | tf_op jit(solution)/shard_map/ppermute | solution.py:172
  33.3 47.7 %collective-permute-start.8 = (bf16[256,2048]{1,0:T(8,128)(2,1)S(1)}, bf16[256,2048]{1,0:T(8,128)(2,1)}, u32[]{:S(2)}, u32[]{:S(2)}) collective-permute-start(bf16[256,2048]{1,0:T(8,128)(2,1)S(1)} %bitcast.267), channel_id=1, source_target_pairs={{0,3},{1,0},{2,1},{3,2},{4,7},{5,4},{6,5},{7,6},{8,11},{9,8},{10,9... | collective-permute-start | bytes 3145736 | tf_op jit(solution)/shard_map/ppermute | solution.py:172
  59.7 32.6 %collective-permute-start.9 = (bf16[128,2048]{1,0:T(8,128)(2,1)S(1)}, bf16[128,2048]{1,0:T(8,128)(2,1)S(1)}, u32[]{:S(2)}, u32[]{:S(2)}) collective-permute-start(bf16[128,2048]{1,0:T(8,128)(2,1)S(1)} %slice.192), channel_id=1, source_target_pairs={{0,1},{1,2},{2,3},{3,0},{4,5},{5,6},{6,7},{7,4},{8,9},{9,10},{10,1... | collective-permute-start | bytes 1572872 | tf_op jit(solution)/shard_map/ppermute | solution.py:172
  82.1 19.8 %collective-permute-start.10 = (bf16[128,2048]{1,0:T(8,128)(2,1)S(1)}, bf16[128,2048]{1,0:T(8,128)(2,1)S(1)}, u32[]{:S(2)}, u32[]{:S(2)}) collective-permute-start(bf16[128,2048]{1,0:T(8,128)(2,1)S(1)} %slice.193), channel_id=1, source_target_pairs={{0,3},{1,0},{2,1},{3,2},{4,7},{5,4},{6,5},{7,6},{8,11},{9,8},{10,9... | collective-permute-start | bytes 1572872 | tf_op jit(solution)/shard_map/ppermute | solution.py:172
  105.5 12.6 %collective-permute-start.15 = (bf16[64,2560]{1,0:T(8,128)(2,1)S(1)}, bf16[64,2560]{1,0:T(8,128)(2,1)S(1)}, u32[]{:S(2)}, u32[]{:S(2)}) collective-permute-start(bf16[64,2560]{1,0:T(8,128)(2,1)S(1)} %bitcast.287), channel_id=1, source_target_pairs={{0,1},{1,2},{2,3},{3,0},{4,5},{5,6},{6,7},{7,4},{8,9},{9,10},{10,1... | collective-permute-start | bytes 983048 | tf_op jit(solution)/shard_map/ppermute | solution.py:172
  106.1 25.0 %collective-permute-start.16 = (bf16[64,2560]{1,0:T(8,128)(2,1)S(1)}, bf16[64,2560]{1,0:T(8,128)(2,1)S(1)}, u32[]{:S(2)}, u32[]{:S(2)}) collective-permute-start(bf16[64,2560]{1,0:T(8,128)(2,1)S(1)} %bitcast.286), channel_id=1, source_target_pairs={{0,2},{1,3},{2,0},{3,1},{4,6},{5,7},{6,4},{7,5},{8,10},{9,11},{10,... | collective-permute-start | bytes 983048 | tf_op jit(solution)/shard_map/ppermute | solution.py:172
  108.8 22.4 %collective-permute-start.17 = (bf16[64,2560]{1,0:T(8,128)(2,1)S(1)}, bf16[64,2560]{1,0:T(8,128)(2,1)S(1)}, u32[]{:S(2)}, u32[]{:S(2)}) collective-permute-start(bf16[64,2560]{1,0:T(8,128)(2,1)S(1)} %bitcast.285), channel_id=1, source_target_pairs={{0,3},{1,0},{2,1},{3,2},{4,7},{5,4},{6,5},{7,6},{8,11},{9,8},{10,9... | collective-permute-start | bytes 983048 | tf_op jit(solution)/shard_map/ppermute | solution.py:172
  132.4 272.0 %all-gather.10.cloned.1.call-start = ((), (), s32[]{:S(2)}) async-start(), calls=%async_computation.3 | async-start | bytes 2359296 | tf_op jit(solution)/shard_map/all_gather | solution.py:428
  133.4 10.3 %collective-permute-start = (bf16[3584]{0:T(1024)(128)(2,1)S(1)}, bf16[3584]{0:T(1024)(128)(2,1)S(1)}, u32[]{:S(2)}, u32[]{:S(2)}) collective-permute-start(bf16[3584]{0:T(1024)(128)(2,1)S(1)} %constant_dynamic-update-slice_fusion.7), channel_id=1, source_target_pairs={{0,1},{1,2},{2,3},{3,0},{4,5},{5,6},{6,7},{7,4},{8,9},{9,10},{10,1... | collective-permute-start | bytes 21512 | tf_op jit(solution)/shard_map/ppermute | solution.py:172
  146.7 28.0 %collective-permute-start.3 = (bf16[256,2048]{1,0:T(8,128)(2,1)}, bf16[256,2048]{1,0:T(8,128)(2,1)S(1)}, u32[]{:S(2)}, u32[]{:S(2)}) collective-permute-start(bf16[256,2048]{1,0:T(8,128)(2,1)} %fusion.10), channel_id=1, source_target_pairs={{0,1},{1,2},{2,3},{3,0},{4,5},{5,6},{6,7},{7,4},{8,9},{9,10},{10,1... | collective-permute-start | bytes 3145736 | tf_op jit(solution)/shard_map/ppermute | solution.py:172
  147.2 47.4 %collective-permute-start.4 = (bf16[256,2048]{1,0:T(8,128)(2,1)}, bf16[256,2048]{1,0:T(8,128)(2,1)}, u32[]{:S(2)}, u32[]{:S(2)}) collective-permute-start(bf16[256,2048]{1,0:T(8,128)(2,1)} %fusion.10), channel_id=1, source_target_pairs={{0,3},{1,0},{2,1},{3,2},{4,7},{5,4},{6,5},{7,6},{8,11},{9,8},{10,9... | collective-permute-start | bytes 3145736 | tf_op jit(solution)/shard_map/ppermute | solution.py:172
  174.8 34.6 %collective-permute-start.5 = (bf16[128,2048]{1,0:T(8,128)(2,1)S(1)}, bf16[128,2048]{1,0:T(8,128)(2,1)S(1)}, u32[]{:S(2)}, u32[]{:S(2)}) collective-permute-start(bf16[128,2048]{1,0:T(8,128)(2,1)S(1)} %slice.190), channel_id=1, source_target_pairs={{0,1},{1,2},{2,3},{3,0},{4,5},{5,6},{6,7},{7,4},{8,9},{9,10},{10,1... | collective-permute-start | bytes 1572872 | tf_op jit(solution)/shard_map/ppermute | solution.py:172
  195.7 21.2 %collective-permute-start.6 = (bf16[128,2048]{1,0:T(8,128)(2,1)S(1)}, bf16[128,2048]{1,0:T(8,128)(2,1)S(1)}, u32[]{:S(2)}, u32[]{:S(2)}) collective-permute-start(bf16[128,2048]{1,0:T(8,128)(2,1)S(1)} %slice.191), channel_id=1, source_target_pairs={{0,3},{1,0},{2,1},{3,2},{4,7},{5,4},{6,5},{7,6},{8,11},{9,8},{10,9... | collective-permute-start | bytes 1572872 | tf_op jit(solution)/shard_map/ppermute | solution.py:172
  243.3 23.9 %collective-permute-start.14 = (bf16[2048,1024]{1,0:T(8,128)(2,1)}, bf16[2048,1024]{1,0:T(8,128)(2,1)}, u32[]{:S(2)}, u32[]{:S(2)}) collective-permute-start(bf16[2048,1024]{1,0:T(8,128)(2,1)} %convolution_convert_fusion.2), channel_id=1, source_target_pairs={{0,4},{4,0},{8,12},{12,8},{16,20},{20,16},{24,28},{28,24},{1,5},{5... | collective-permute-start | bytes 12582920 | tf_op jit(solution)/shard_map/ppermute | solution.py:247
  255.0 289.3 %reduce-scatter.2.cloned.1.call-start = ((), (), s32[]{:S(2)}) async-start(), calls=%async_computation.4 | async-start | bytes 2359296 | tf_op jit(solution)/shard_map/reduce_scatter | solution.py:455
  306.8 29.1 %collective-permute-start.64 = (bf16[4,128,1024]{2,1,0:T(8,128)(2,1)}, bf16[4,128,1024]{2,1,0:T(8,128)(2,1)S(1)}, u32[]{:S(2)}, u32[]{:S(2)}) collective-permute-start(bf16[4,128,1024]{2,1,0:T(8,128)(2,1)} %get-tuple-element.71), channel_id=1, source_target_pairs={{0,24},{4,28},{8,16},{12,20},{16,8},{20,12},{24,0},{28,4},{1,25},{... | collective-permute-start | bytes 3145736 | tf_op jit(solution)/shard_map/ppermute | solution.py:247
  309.3 55.1 %collective-permute-start.63 = (bf16[4,128,1024]{2,1,0:T(8,128)(2,1)}, bf16[4,128,1024]{2,1,0:T(8,128)(2,1)S(1)}, u32[]{:S(2)}, u32[]{:S(2)}) collective-permute-start(bf16[4,128,1024]{2,1,0:T(8,128)(2,1)} %get-tuple-element.72), channel_id=1, source_target_pairs={{0,16},{4,20},{8,24},{12,28},{16,0},{20,4},{24,8},{28,12},{1,17},{... | collective-permute-start | bytes 3145736 | tf_op jit(solution)/shard_map/ppermute | solution.py:247
  309.8 54.8 %collective-permute-start.62 = (bf16[4,128,1024]{2,1,0:T(8,128)(2,1)S(1)}, bf16[4,128,1024]{2,1,0:T(8,128)(2,1)}, u32[]{:S(2)}, u32[]{:S(2)}) collective-permute-start(bf16[4,128,1024]{2,1,0:T(8,128)(2,1)S(1)} %get-tuple-element.70), channel_id=1, source_target_pairs={{0,8},{4,12},{8,0},{12,4},{16,24},{20,28},{24,16},{28,20},{1,9},{5... | collective-permute-start | bytes 3145736 | tf_op jit(solution)/shard_map/ppermute | solution.py:247
  310.3 514.2 %all-gather.14.cloned.1.call-start = ((), (), s32[]{:S(2)}) async-start(), calls=%async_computation.6 | async-start | bytes 9437184 | tf_op jit(solution)/shard_map/all_gather | solution.py:471
  334.8 78.3 %collective-permute-start.21 = (bf16[2048,1024]{1,0:T(8,128)(2,1)}, bf16[2048,1024]{1,0:T(8,128)(2,1)}, u32[]{:S(2)}, u32[]{:S(2)}) collective-permute-start(bf16[2048,1024]{1,0:T(8,128)(2,1)} %convolution_convert_fusion.1), channel_id=1, source_target_pairs={{0,4},{4,0},{8,12},{12,8},{16,20},{20,16},{24,28},{28,24},{1,5},{5... | collective-permute-start | bytes 12582920 | tf_op jit(solution)/shard_map/ppermute | solution.py:247
  367.1 11.1 %collective-permute-start.65 = (bf16[128,1024]{1,0:T(8,128)(2,1)S(1)}, bf16[128,1024]{1,0:T(8,128)(2,1)S(1)}, u32[]{:S(2)}, u32[]{:S(2)}) collective-permute-start(bf16[128,1024]{1,0:T(8,128)(2,1)S(1)} %get-tuple-element.94), channel_id=1, source_target_pairs={{0,1},{1,2},{2,3},{3,0},{4,5},{5,6},{6,7},{7,4},{8,9},{9,10},{10,1... | collective-permute-start | bytes 786440 | tf_op jit(solution)/shard_map/ppermute | solution.py:172
  367.7 20.8 %collective-permute-start.66 = (bf16[128,1024]{1,0:T(8,128)(2,1)S(1)}, bf16[128,1024]{1,0:T(8,128)(2,1)S(1)}, u32[]{:S(2)}, u32[]{:S(2)}) collective-permute-start(bf16[128,1024]{1,0:T(8,128)(2,1)S(1)} %get-tuple-element.93), channel_id=1, source_target_pairs={{0,2},{1,3},{2,0},{3,1},{4,6},{5,7},{6,4},{7,5},{8,10},{9,11},{10,... | collective-permute-start | bytes 786440 | tf_op jit(solution)/shard_map/ppermute | solution.py:172
  369.2 19.3 %collective-permute-start.67 = (bf16[128,1024]{1,0:T(8,128)(2,1)S(1)}, bf16[128,1024]{1,0:T(8,128)(2,1)S(1)}, u32[]{:S(2)}, u32[]{:S(2)}) collective-permute-start(bf16[128,1024]{1,0:T(8,128)(2,1)S(1)} %get-tuple-element.92), channel_id=1, source_target_pairs={{0,3},{1,0},{2,1},{3,2},{4,7},{5,4},{6,5},{7,6},{8,11},{9,8},{10,9... | collective-permute-start | bytes 786440 | tf_op jit(solution)/shard_map/ppermute | solution.py:172
  389.6 445.4 %all-gather.12.cloned.1.call-start = ((), (), s32[]{:S(2)}) async-start(), calls=%async_computation.5 | async-start | bytes 2359296 | tf_op jit(solution)/shard_map/all_gather | solution.py:502
  459.9 57.0 %collective-permute-start.25 = (bf16[1536,1024]{1,0:T(8,128)(2,1)}, bf16[1536,1024]{1,0:T(8,128)(2,1)}, u32[]{:S(2)}, u32[]{:S(2)}) collective-permute-start(bf16[1536,1024]{1,0:T(8,128)(2,1)} %convolution_convert_fusion), channel_id=1, source_target_pairs={{0,4},{4,0},{8,12},{12,8},{16,20},{20,16},{24,28},{28,24},{1,5},{5... | collective-permute-start | bytes 9437192 | tf_op jit(solution)/shard_map/ppermute | solution.py:247
  463.7 27.0 %collective-permute-start.24 = (bf16[4,128,1024]{2,1,0:T(8,128)(2,1)S(1)}, bf16[4,128,1024]{2,1,0:T(8,128)(2,1)S(1)}, u32[]{:S(2)}, u32[]{:S(2)}) collective-permute-start(bf16[4,128,1024]{2,1,0:T(8,128)(2,1)S(1)} %get-tuple-element.80), channel_id=1, source_target_pairs={{0,24},{4,28},{8,16},{12,20},{16,8},{20,12},{24,0},{28,4},{1,25},{... | collective-permute-start | bytes 3145736 | tf_op jit(solution)/shard_map/ppermute | solution.py:247
  465.8 46.9 %collective-permute-start.23 = (bf16[4,128,1024]{2,1,0:T(8,128)(2,1)S(1)}, bf16[4,128,1024]{2,1,0:T(8,128)(2,1)S(1)}, u32[]{:S(2)}, u32[]{:S(2)}) collective-permute-start(bf16[4,128,1024]{2,1,0:T(8,128)(2,1)S(1)} %get-tuple-element.81), channel_id=1, source_target_pairs={{0,16},{4,20},{8,24},{12,28},{16,0},{20,4},{24,8},{28,12},{1,17},{... | collective-permute-start | bytes 3145736 | tf_op jit(solution)/shard_map/ppermute | solution.py:247
  467.1 45.9 %collective-permute-start.22 = (bf16[4,128,1024]{2,1,0:T(8,128)(2,1)S(1)}, bf16[4,128,1024]{2,1,0:T(8,128)(2,1)S(1)}, u32[]{:S(2)}, u32[]{:S(2)}) collective-permute-start(bf16[4,128,1024]{2,1,0:T(8,128)(2,1)S(1)} %get-tuple-element.79), channel_id=1, source_target_pairs={{0,8},{4,12},{8,0},{12,4},{16,24},{20,28},{24,16},{28,20},{1,9},{5... | collective-permute-start | bytes 3145736 | tf_op jit(solution)/shard_map/ppermute | solution.py:247
  482.4 66.4 %collective-permute-start.20 = (bf16[256,2048]{1,0:T(8,128)(2,1)}, bf16[256,2048]{1,0:T(8,128)(2,1)}, u32[]{:S(2)}, u32[]{:S(2)}) collective-permute-start(bf16[256,2048]{1,0:T(8,128)(2,1)} %get-tuple-element.83), channel_id=1, source_target_pairs={{0,3},{1,0},{2,1},{3,2},{4,7},{5,4},{6,5},{7,6},{8,11},{9,8},{10,9... | collective-permute-start | bytes 3145736 | tf_op jit(solution)/shard_map/ppermute | solution.py:172
  515.3 33.6 %collective-permute-start.55 = (bf16[4,128,1024]{2,1,0:T(8,128)(2,1)S(1)}, bf16[4,128,1024]{2,1,0:T(8,128)(2,1)S(1)}, u32[]{:S(2)}, u32[]{:S(2)}) collective-permute-start(bf16[4,128,1024]{2,1,0:T(8,128)(2,1)S(1)} %fusion.29.refs_0_), channel_id=1, source_target_pairs={{0,8},{4,12},{8,0},{12,4},{16,24},{20,28},{24,16},{28,20},{1,9},{5... | collective-permute-start | bytes 3145736 | tf_op jit(solution)/shard_map/ppermute | solution.py:247
  544.4 46.8 %collective-permute-start.56 = (bf16[4,128,1024]{2,1,0:T(8,128)(2,1)S(1)}, bf16[4,128,1024]{2,1,0:T(8,128)(2,1)S(1)}, u32[]{:S(2)}, u32[]{:S(2)}) collective-permute-start(bf16[4,128,1024]{2,1,0:T(8,128)(2,1)S(1)} %fusion.29.refs_0_), channel_id=1, source_target_pairs={{0,16},{4,20},{8,24},{12,28},{16,0},{20,4},{24,8},{28,12},{1,17},{... | collective-permute-start | bytes 3145736 | tf_op jit(solution)/shard_map/ppermute | solution.py:247
  545.5 87.3 %collective-permute-start.57 = (bf16[4,128,1024]{2,1,0:T(8,128)(2,1)S(1)}, bf16[4,128,1024]{2,1,0:T(8,128)(2,1)}, u32[]{:S(2)}, u32[]{:S(2)}) collective-permute-start(bf16[4,128,1024]{2,1,0:T(8,128)(2,1)S(1)} %fusion.29.refs_0_), channel_id=1, source_target_pairs={{0,24},{4,28},{8,16},{12,20},{16,8},{20,12},{24,0},{28,4},{1,25},{... | collective-permute-start | bytes 3145736 | tf_op jit(solution)/shard_map/ppermute | solution.py:247
  548.4 88.9 %collective-permute-start.58 = (bf16[4,128,1024]{2,1,0:T(8,128)(2,1)S(1)}, bf16[4,128,1024]{2,1,0:T(8,128)(2,1)}, u32[]{:S(2)}, u32[]{:S(2)}) collective-permute-start(bf16[4,128,1024]{2,1,0:T(8,128)(2,1)S(1)} %fusion.29.refs_0_), channel_id=1, source_target_pairs={{0,4},{4,0},{8,12},{12,8},{16,20},{20,16},{24,28},{28,24},{1,5},{5... | collective-permute-start | bytes 3145736 | tf_op jit(solution)/shard_map/ppermute | solution.py:247
  548.8 46.3 %collective-permute-start.52 = (bf16[64,512]{1,0:T(8,128)(2,1)S(1)}, bf16[64,512]{1,0:T(8,128)(2,1)S(1)}, u32[]{:S(2)}, u32[]{:S(2)}) collective-permute-start(bf16[64,512]{1,0:T(8,128)(2,1)S(1)} %get-tuple-element.105), channel_id=1, source_target_pairs={{0,1},{1,2},{2,3},{3,0},{4,5},{5,6},{6,7},{7,4},{8,9},{9,10},{10,1... | collective-permute-start | bytes 196616 | tf_op jit(solution)/shard_map/ppermute | solution.py:172
  548.8 42.4 %collective-permute-start.34 = (f32[5120]{0:T(1024)S(1)}, f32[5120]{0:T(1024)S(1)}, u32[]{:S(2)}, u32[]{:S(2)}) collective-permute-start(f32[5120]{0:T(1024)S(1)} %add.446), channel_id=1, source_target_pairs={{0,8},{4,12},{8,0},{12,4},{16,24},{20,28},{24,16},{28,20},{1,9},{5... | collective-permute-start | bytes 61448 | tf_op jit(solution)/shard_map/ppermute | solution.py:247
  591.2 42.3 %collective-permute-start.26 = (bf16[128,2048]{1,0:T(8,128)(2,1)}, bf16[128,2048]{1,0:T(8,128)(2,1)}, u32[]{:S(2)}, u32[]{:S(2)}) collective-permute-start(bf16[128,2048]{1,0:T(8,128)(2,1)} %get-tuple-element.75), channel_id=1, source_target_pairs={{0,1},{1,2},{2,3},{3,0},{4,5},{5,6},{6,7},{7,4},{8,9},{9,10},{10,1... | collective-permute-start | bytes 1572872 | tf_op jit(solution)/shard_map/ppermute | solution.py:172
  591.2 44.1 %collective-permute-start.28 = (bf16[128,2048]{1,0:T(8,128)(2,1)}, bf16[128,2048]{1,0:T(8,128)(2,1)}, u32[]{:S(2)}, u32[]{:S(2)}) collective-permute-start(bf16[128,2048]{1,0:T(8,128)(2,1)} %get-tuple-element.77), channel_id=1, source_target_pairs={{0,3},{1,0},{2,1},{3,2},{4,7},{5,4},{6,5},{7,6},{8,11},{9,8},{10,9... | collective-permute-start | bytes 1572872 | tf_op jit(solution)/shard_map/ppermute | solution.py:172
  595.0 22.7 %collective-permute-start.53 = (bf16[64,512]{1,0:T(8,128)(2,1)S(1)}, bf16[64,512]{1,0:T(8,128)(2,1)S(1)}, u32[]{:S(2)}, u32[]{:S(2)}) collective-permute-start(bf16[64,512]{1,0:T(8,128)(2,1)S(1)} %get-tuple-element.104), channel_id=1, source_target_pairs={{0,2},{1,3},{2,0},{3,1},{4,6},{5,7},{6,4},{7,5},{8,10},{9,11},{10,... | collective-permute-start | bytes 196616 | tf_op jit(solution)/shard_map/ppermute | solution.py:172
  622.0 40.1 %collective-permute-start.38 = (bf16[3,128,1024]{2,1,0:T(8,128)(2,1)}, bf16[3,128,1024]{2,1,0:T(8,128)(2,1)}, u32[]{:S(2)}, u32[]{:S(2)}) collective-permute-start(bf16[3,128,1024]{2,1,0:T(8,128)(2,1)} %get-tuple-element.86), channel_id=1, source_target_pairs={{0,24},{4,28},{8,16},{12,20},{16,8},{20,12},{24,0},{28,4},{1,25},{... | collective-permute-start | bytes 2359304 | tf_op jit(solution)/shard_map/ppermute | solution.py:247
  632.8 33.0 %collective-permute-start.37 = (bf16[3,128,1024]{2,1,0:T(8,128)(2,1)}, bf16[3,128,1024]{2,1,0:T(8,128)(2,1)}, u32[]{:S(2)}, u32[]{:S(2)}) collective-permute-start(bf16[3,128,1024]{2,1,0:T(8,128)(2,1)} %get-tuple-element.87), channel_id=1, source_target_pairs={{0,16},{4,20},{8,24},{12,28},{16,0},{20,4},{24,8},{28,12},{1,17},{... | collective-permute-start | bytes 2359304 | tf_op jit(solution)/shard_map/ppermute | solution.py:247
  633.5 34.9 %collective-permute-start.36 = (bf16[3,128,1024]{2,1,0:T(8,128)(2,1)}, bf16[3,128,1024]{2,1,0:T(8,128)(2,1)}, u32[]{:S(2)}, u32[]{:S(2)}) collective-permute-start(bf16[3,128,1024]{2,1,0:T(8,128)(2,1)} %get-tuple-element.85), channel_id=1, source_target_pairs={{0,8},{4,12},{8,0},{12,4},{16,24},{20,28},{24,16},{28,20},{1,9},{5... | collective-permute-start | bytes 2359304 | tf_op jit(solution)/shard_map/ppermute | solution.py:247
  635.3 26.8 %collective-permute-start.35 = (f32[5120]{0:T(1024)}, f32[5120]{0:T(1024)S(1)}, u32[]{:S(2)}, u32[]{:S(2)}) collective-permute-start(f32[5120]{0:T(1024)} %add.447), channel_id=1, source_target_pairs={{0,16},{4,20},{8,24},{12,28},{16,0},{20,4},{24,8},{28,12},{1,17},{... | collective-permute-start | bytes 61448 | tf_op jit(solution)/shard_map/ppermute | solution.py:247
  637.3 40.9 %collective-permute-start.59 = (bf16[4,128,1024]{2,1,0:T(8,128)(2,1)S(1)}, bf16[4,128,1024]{2,1,0:T(8,128)(2,1)}, u32[]{:S(2)}, u32[]{:S(2)}) collective-permute-start(bf16[4,128,1024]{2,1,0:T(8,128)(2,1)S(1)} %collective-permute-done.55.refs_1_), channel_id=1, source_target_pairs={{0,4},{4,0},{8,12},{12,8},{16,20},{20,16},{24,28},{28,24},{1,5},{5... | collective-permute-start | bytes 3145736 | tf_op jit(solution)/shard_map/ppermute | solution.py:247
  662.1 19.3 %collective-permute-start.60 = (bf16[4,128,1024]{2,1,0:T(8,128)(2,1)S(1)}, bf16[4,128,1024]{2,1,0:T(8,128)(2,1)}, u32[]{:S(2)}, u32[]{:S(2)}) collective-permute-start(bf16[4,128,1024]{2,1,0:T(8,128)(2,1)S(1)} %collective-permute-done.56.refs_2_), channel_id=1, source_target_pairs={{0,4},{4,0},{8,12},{12,8},{16,20},{20,16},{24,28},{28,24},{1,5},{5... | collective-permute-start | bytes 3145736 | tf_op jit(solution)/shard_map/ppermute | solution.py:247
  662.1 22.9 %collective-permute-start.61 = (bf16[4,128,1024]{2,1,0:T(8,128)(2,1)}, bf16[4,128,1024]{2,1,0:T(8,128)(2,1)}, u32[]{:S(2)}, u32[]{:S(2)}) collective-permute-start(bf16[4,128,1024]{2,1,0:T(8,128)(2,1)} %collective-permute-done.57.refs_3_), channel_id=1, source_target_pairs={{0,4},{4,0},{8,12},{12,8},{16,20},{20,16},{24,28},{28,24},{1,5},{5... | collective-permute-start | bytes 3145736 | tf_op jit(solution)/shard_map/ppermute | solution.py:247
  665.8 111.8 %collective-permute-start.29 = (bf16[256,2048]{1,0:T(8,128)(2,1)}, bf16[256,2048]{1,0:T(8,128)(2,1)}, u32[]{:S(2)}, u32[]{:S(2)}) collective-permute-start(bf16[256,2048]{1,0:T(8,128)(2,1)} %pad_maximum_fusion.1), channel_id=1, source_target_pairs={{0,3},{1,0},{2,1},{3,2},{4,7},{5,4},{6,5},{7,6},{8,11},{9,8},{10,9... | collective-permute-start | bytes 3145736 | tf_op jit(solution)/shard_map/ppermute | solution.py:172
  668.4 109.3 %collective-permute-start.27 = (bf16[256,2048]{1,0:T(8,128)(2,1)}, bf16[256,2048]{1,0:T(8,128)(2,1)}, u32[]{:S(2)}, u32[]{:S(2)}) collective-permute-start(bf16[256,2048]{1,0:T(8,128)(2,1)} %pad_maximum_fusion), channel_id=1, source_target_pairs={{0,1},{1,2},{2,3},{3,0},{4,5},{5,6},{6,7},{7,4},{8,9},{9,10},{10,1... | collective-permute-start | bytes 3145736 | tf_op jit(solution)/shard_map/ppermute | solution.py:172
  678.2 84.3 %collective-permute-start.41 = (bf16[128,1024]{1,0:T(8,128)(2,1)S(1)}, bf16[128,1024]{1,0:T(8,128)(2,1)S(1)}, u32[]{:S(2)}, u32[]{:S(2)}) collective-permute-start(bf16[128,1024]{1,0:T(8,128)(2,1)S(1)} %get-tuple-element.98), channel_id=1, source_target_pairs={{2,0},{1,1},{0,2},{3,3},{6,4},{5,5},{4,6},{7,7},{10,8},{9,9},{8,10... | collective-permute-start | bytes 786440 | tf_op jit(solution)/shard_map/ppermute | solution.py:499
  681.4 79.8 %collective-permute-start.51 = (f32[512]{0:T(512)S(1)}, f32[512]{0:T(512)S(1)}, u32[]{:S(2)}, u32[]{:S(2)}) collective-permute-start(f32[512]{0:T(512)S(1)} %bitcast.309), channel_id=1, source_target_pairs={{2,0},{1,1},{0,2},{3,3},{6,4},{5,5},{4,6},{7,7},{10,8},{9,9},{8,10... | collective-permute-start | bytes 6152 | tf_op jit(solution)/shard_map/ppermute | solution.py:520
  685.0 78.3 %collective-permute-start.40 = (bf16[128,1024]{1,0:T(8,128)(2,1)}, bf16[128,1024]{1,0:T(8,128)(2,1)}, u32[]{:S(2)}, u32[]{:S(2)}) collective-permute-start(bf16[128,1024]{1,0:T(8,128)(2,1)} %get-tuple-element.99), channel_id=1, source_target_pairs={{1,0},{0,1},{3,2},{2,3},{5,4},{4,5},{7,6},{6,7},{9,8},{8,9},{11,10... | collective-permute-start | bytes 786440 | tf_op jit(solution)/shard_map/ppermute | solution.py:499
  762.5 34.6 %collective-permute-start.19 = (bf16[256,2048]{1,0:T(8,128)(2,1)}, bf16[256,2048]{1,0:T(8,128)(2,1)}, u32[]{:S(2)}, u32[]{:S(2)}) collective-permute-start(bf16[256,2048]{1,0:T(8,128)(2,1)} %get-tuple-element.84), channel_id=1, source_target_pairs={{0,2},{1,3},{2,0},{3,1},{4,6},{5,7},{6,4},{7,5},{8,10},{9,11},{10,... | collective-permute-start | bytes 3145736 | tf_op jit(solution)/shard_map/ppermute | solution.py:172
  763.3 11.9 %collective-permute-start.50 = (f32[512]{0:T(512)S(1)}, f32[512]{0:T(512)S(1)}, u32[]{:S(2)}, u32[]{:S(2)}) collective-permute-start(f32[512]{0:T(512)S(1)} %bitcast.308), channel_id=1, source_target_pairs={{1,0},{0,1},{3,2},{2,3},{5,4},{4,5},{7,6},{6,7},{9,8},{8,9},{11,10... | collective-permute-start | bytes 6152 | tf_op jit(solution)/shard_map/ppermute | solution.py:520
  763.3 14.3 %collective-permute-start.49 = (f32[512]{0:T(512)S(1)}, f32[512]{0:T(512)S(1)}, u32[]{:S(2)}, u32[]{:S(2)}) collective-permute-start(f32[512]{0:T(512)S(1)} %bitcast.307), channel_id=1, source_target_pairs={{0,0},{3,1},{2,2},{1,3},{4,4},{7,5},{6,6},{5,7},{8,8},{11,9},{10,1... | collective-permute-start | bytes 6152 | tf_op jit(solution)/shard_map/ppermute | solution.py:520
  775.2 33.7 %collective-permute-start.18 = (bf16[256,2048]{1,0:T(8,128)(2,1)}, bf16[256,2048]{1,0:T(8,128)(2,1)S(1)}, u32[]{:S(2)}, u32[]{:S(2)}) collective-permute-start(bf16[256,2048]{1,0:T(8,128)(2,1)} %get-tuple-element.82), channel_id=1, source_target_pairs={{0,1},{1,2},{2,3},{3,0},{4,5},{5,6},{6,7},{7,4},{8,9},{9,10},{10,1... | collective-permute-start | bytes 3145736 | tf_op jit(solution)/shard_map/ppermute | solution.py:172
  777.6 20.1 %collective-permute-start.42 = (bf16[3,128,1024]{2,1,0:T(8,128)(2,1)S(1)}, bf16[3,128,1024]{2,1,0:T(8,128)(2,1)S(1)}, u32[]{:S(2)}, u32[]{:S(2)}) collective-permute-start(bf16[3,128,1024]{2,1,0:T(8,128)(2,1)S(1)} %pad_maximum_fusion.4.refs_0_), channel_id=1, source_target_pairs={{0,8},{4,12},{8,0},{12,4},{16,24},{20,28},{24,16},{28,20},{1,9},{5... | collective-permute-start | bytes 2359304 | tf_op jit(solution)/shard_map/ppermute | solution.py:247
  777.6 30.7 %collective-permute-start.43 = (bf16[3,128,1024]{2,1,0:T(8,128)(2,1)S(1)}, bf16[3,128,1024]{2,1,0:T(8,128)(2,1)S(1)}, u32[]{:S(2)}, u32[]{:S(2)}) collective-permute-start(bf16[3,128,1024]{2,1,0:T(8,128)(2,1)S(1)} %pad_maximum_fusion.4.refs_0_), channel_id=1, source_target_pairs={{0,16},{4,20},{8,24},{12,28},{16,0},{20,4},{24,8},{28,12},{1,17},{... | collective-permute-start | bytes 2359304 | tf_op jit(solution)/shard_map/ppermute | solution.py:247
  777.7 30.7 %collective-permute-start.44 = (bf16[3,128,1024]{2,1,0:T(8,128)(2,1)S(1)}, bf16[3,128,1024]{2,1,0:T(8,128)(2,1)S(1)}, u32[]{:S(2)}, u32[]{:S(2)}) collective-permute-start(bf16[3,128,1024]{2,1,0:T(8,128)(2,1)S(1)} %pad_maximum_fusion.4.refs_0_), channel_id=1, source_target_pairs={{0,24},{4,28},{8,16},{12,20},{16,8},{20,12},{24,0},{28,4},{1,25},{... | collective-permute-start | bytes 2359304 | tf_op jit(solution)/shard_map/ppermute | solution.py:247
  797.1 18.4 %collective-permute-start.45 = (bf16[3,128,1024]{2,1,0:T(8,128)(2,1)S(1)}, bf16[3,128,1024]{2,1,0:T(8,128)(2,1)S(1)}, u32[]{:S(2)}, u32[]{:S(2)}) collective-permute-start(bf16[3,128,1024]{2,1,0:T(8,128)(2,1)S(1)} %pad_maximum_fusion.4.refs_0_), channel_id=1, source_target_pairs={{0,4},{4,0},{8,12},{12,8},{16,20},{20,16},{24,28},{28,24},{1,5},{5... | collective-permute-start | bytes 2359304 | tf_op jit(solution)/shard_map/ppermute | solution.py:247
  797.7 17.8 %collective-permute-start.46 = (bf16[3,128,1024]{2,1,0:T(8,128)(2,1)S(1)}, bf16[3,128,1024]{2,1,0:T(8,128)(2,1)S(1)}, u32[]{:S(2)}, u32[]{:S(2)}) collective-permute-start(bf16[3,128,1024]{2,1,0:T(8,128)(2,1)S(1)} %collective-permute-done.42.refs_1_), channel_id=1, source_target_pairs={{0,4},{4,0},{8,12},{12,8},{16,20},{20,16},{24,28},{28,24},{1,5},{5... | collective-permute-start | bytes 2359304 | tf_op jit(solution)/shard_map/ppermute | solution.py:247
  (59 other events, 989.2 us)
Sparse Core Ops, SparseCore 0:
  30.0 47.4 all-gather.5
  132.5 58.8 all-gather.7
  255.2 26.9 all-gather.9
  310.4 48.9 reduce-scatter.1
  389.7 56.3 all-gather.13
  632.9 33.4 all-gather.11

commit v3 on v2

--- a/solution.py
+++ b/solution.py
@@ -384,9 +384,16 @@
     my_rounds = pick(jnp.asarray(round_of), me)
     arrived = jnp.stack([pick(arrived, my_rounds[k]) for k in range(3)])
     in_w = lax.all_gather(arrived, "rep", axis=1, tiled=True).reshape(3 * part, width)
-
-    grad_own = out_grad.reshape(span, width)
-    grads = gather_row(grad_own, count, me)
+    down = jnp.concatenate(
+        [
+            lax.dynamic_slice_in_dim(shrink_weight, rep * sub, sub, 0).reshape(sub, count, inner),
+            lax.dynamic_slice_in_dim(outproj_weight, rep * sub, sub, 0).reshape(sub, count, part),
+        ],
+        2,
+    )
+    down = swap_blocks(jnp.transpose(down, (1, 0, 2)), 0, count, me)
+    shrink_w = lax.all_gather(down[:, :, :inner], "rep", axis=1, tiled=True).reshape(width, inner)
+    out_w = lax.all_gather(down[:, :, inner:], "rep", axis=1, tiled=True).reshape(width, part)
 
     residual = tokens.reshape(span, width).astype(F32)
     row_mean = jnp.mean(residual, -1, keepdims=True)
@@ -397,35 +404,24 @@
     normed_own = (xhat * gain + shift_all).astype(BF16)
     normed = gather_row(normed_own, count, me)
 
+    grad_own = out_grad.reshape(span, width)
+    grads = gather_row(grad_own, count, me)
+
     seg = segments.reshape(length)
     starts = jnp.sum((seg[None, :] < seg[:, None]).astype(jnp.int32), 1)
     place = (jnp.arange(length, dtype=jnp.int32) - starts).astype(F32)
-    inverse_freq = 10000.0 ** (-jnp.arange(ROT // 2).astype(F32) * 2.0 / ROT)
+    lane = jnp.arange(PAIR) % HEAD_DIM
+    inverse_freq = 10000.0 ** (-(lane % (ROT // 2)).astype(F32) * 2.0 / ROT)
     angle = place[:, None] * inverse_freq[None, :]
-    cosine, sine = jnp.cos(angle), jnp.sin(angle)
-    quiet = jnp.zeros_like(sine)
-    rest = jnp.zeros((length, HEAD_DIM - ROT), F32)
+    sine = jnp.sin(angle)
     tables = (
-        jnp.concatenate([cosine, cosine, rest + 1.0] * 2, 1),
-        jnp.concatenate([-sine, quiet, rest] * 2, 1),
-        jnp.concatenate([quiet, sine, rest] * 2, 1),
+        jnp.where(lane < ROT, jnp.cos(angle), 1.0),
+        jnp.where(lane < ROT // 2, -sine, 0.0),
+        jnp.where((lane >= ROT // 2) & (lane < ROT), sine, 0.0),
     )
     seg_col, seg_row = seg[:, None], seg[None, :]
     blk = min(256, length)
     back = [[(b, a) for a, b in pairs] for pairs in forward]
-
-    down = jnp.concatenate(
-        [
-            lax.dynamic_slice_in_dim(shrink_weight, rep * sub, sub, 0).reshape(sub, count, inner),
-            lax.dynamic_slice_in_dim(outproj_weight, rep * sub, sub, 0).reshape(sub, count, part),
-        ],
-        2,
-    )
-    down = jnp.transpose(down, (1, 0, 2))
-    grads, down = hold(grads, down)
-    down = swap_blocks(down, 0, count, me)
-    shrink_w = lax.all_gather(down[:, :, :inner], "rep", axis=1, tiled=True).reshape(width, inner)
-    out_w = lax.all_gather(down[:, :, inner:], "rep", axis=1, tiled=True).reshape(width, part)
 
     def col_half(x, which):
         wide = x.shape[1] // 2
@@ -440,65 +436,68 @@
     hidden, slope = gelu_parts(expanded)
     hidden, slope = hidden.astype(BF16), slope.astype(BF16)
     hidden_mine, hidden_other = col_half(hidden, core), col_half(hidden, 1 - core)
+    normed_1, hidden = hold(normed, hidden)
+    mixed = nt(normed_1, in_w) + inbias
+    attended, q_low, k_low, v_low, lse = attend(mixed, tables, seg_col, seg_row, blk)
+    hidden_1, attended = hold(hidden, attended)
+    branches = (nt(hidden_1, shrink_w) + nt(attended, out_w)).astype(BF16)
+    branches_sum = scatter_direct(branches, count, me)
+
+    grads, branches = hold(grads, branches)
+    blocks = inner // part
     shr_send = low_term(grads, hidden_other)
     shr_arrived = flip(shr_send, 1, reps)
-
-    normed_1, shr_send = hold(normed, shr_send)
-    mixed = nt(normed_1, in_w) + inbias
-    grads_1, mixed = hold(grads, mixed)
-    shr_sum = low_term(grads_1, hidden_mine, shr_arrived)
+    grads_1, shr_send = hold(grads, shr_send)
+    d_up = (nn(grads_1, shrink_w) * slope.astype(F32)).astype(BF16)
+    grads_2, d_up = hold(grads_1, d_up)
+    shr_sum = low_term(grads_2, hidden_mine, shr_arrived)
     shr_total = reduce_chips(shr_sum.reshape(count, part, inner // 2), rep, reps)
-    mixed, shr_sum = hold(mixed, shr_sum)
-    attended, q_low, k_low, v_low, lse = attend(mixed, tables, seg_col, seg_row, blk)
-    grads_2, attended = hold(grads_1, attended)
-    g_out = tn(grads_2, attended).astype(BF16)
-    g_out_1 = lax.psum_scatter(
-        g_out.reshape(count, part, part), "rep", scatter_dimension=1, tiled=True
-    )
-    blocks = inner // part
-    grads_3, g_out = hold(grads_2, g_out)
-    d_up = (nn(grads_3, shrink_w) * slope.astype(F32)).astype(BF16)
+    d_up, shr_sum = hold(d_up, shr_sum)
     exp_send = low_term(d_up, normed_other)
     exp_arrived = flip(exp_send, 1, reps)
-    hidden_1, exp_send = hold(hidden, exp_send)
-    branches = (nt(hidden_1, shrink_w) + nt(attended, out_w)).astype(BF16)
-    branches_sum = scatter_direct(branches, count, me)
-    d_up_1, branches = hold(d_up, branches)
+    grads_3, exp_send = hold(grads_2, exp_send)
+    d_att = nn(grads_3, out_w).astype(BF16)
+    d_up_1, d_att = hold(d_up, d_att)
     exp_sum = low_term(d_up_1, normed_mine, exp_arrived)
     exp_total = reduce_chips(exp_sum.reshape(blocks, part, width // 2), rep, reps)
-    g_shr = shr_total()
-    g_shr = swap_blocks(g_shr, 0, count, me)
-    g_shr = lax.all_gather(g_shr, "rep", axis=0)
+
     grads_4, exp_sum = hold(grads_3, exp_sum)
-    d_att = nn(grads_4, out_w).astype(BF16)
-
+    g_out_1 = tn(grads_4, attended).astype(BF16)
+    g_out = lax.psum_scatter(
+        g_out_1.reshape(count, part, part), "rep", scatter_dimension=1, tiled=True
+    )
+    d_att, g_out_1 = hold(d_att, g_out_1)
     d_q, d_k, d_v = attend_back(q_low, k_low, v_low, d_att, lse, tables, seg_col, seg_row, blk)
     d_mixed = jnp.concatenate([d_q, d_k, d_v], 1)
     in_send = low_term(d_mixed, normed_other)
     in_arrived = flip(in_send, 1, reps)
+    g_shr = shr_total()
+    d_mixed_1, in_send, g_shr = hold(d_mixed, in_send, g_shr)
+    g_shr = swap_blocks(g_shr, 0, count, me)
+    g_shr = lax.all_gather(g_shr, "rep", axis=0)
+    g_out = jnp.transpose(swap_blocks(g_out, 0, count, me), (1, 0, 2)).reshape(sub, width)
+    in_sum = low_term(d_mixed_1, normed_mine, in_arrived)
+    in_total = reduce_chips(in_sum.reshape(3, part, width // 2), rep, reps)
+    d_mixed_2, d_up_2, in_sum = hold(d_mixed_1, d_up_1, in_sum)
+    b_out = jnp.sum(lax.dynamic_slice_in_dim(grads_4, me * part, part, 1), 0, dtype=F32)
+    b_exp = jnp.sum(d_up_2, 0, dtype=F32)
+    b_in = jnp.sum(d_mixed_2, 0, dtype=F32)
     g_exp = exp_total()
     exp_pieces = spread(g_exp, reps)
-    d_mixed_1, in_send, g_exp = hold(d_mixed, in_send, g_exp)
-    in_sum = low_term(d_mixed_1, normed_mine, in_arrived)
-    in_total = reduce_chips(in_sum.reshape(3, part, width // 2), rep, reps)
-    d_mixed_2, in_sum = hold(d_mixed_1, in_sum)
-    d_normed = nn(d_up_1, expand_weight) + nn(d_mixed_2, in_w)
+    d_mixed_2, b_in, g_exp = hold(d_mixed_2, b_in, g_exp)
+    d_normed = nn(d_up_2, expand_weight) + nn(d_mixed_2, in_w)
     both = jnp.stack([jnp.sum(d_normed * normed.astype(F32), 0), jnp.sum(d_normed, 0)])
     d_normed = d_normed.astype(BF16)
-    g_out_1, d_normed = hold(g_out_1, d_normed)
     d_normed = scatter_row(d_normed, count, me)
-
-    b_out = jnp.sum(lax.dynamic_slice_in_dim(grads, me * part, part, 1), 0, dtype=F32)
-    b_exp = jnp.sum(d_up_1, 0, dtype=F32)
-    b_in = jnp.sum(d_mixed_2, 0, dtype=F32)
+    kinds = pick(jnp.asarray(kind_of), me)
+    g_in = in_total()
+    both, g_in = hold(both, g_in)
+    g_in = jnp.stack([lax.ppermute(pick(g_in, kinds[j]), "shard", back[j]) for j in range(3)])
+    in_pieces = spread(g_in, reps)
+
     both = jnp.sum(swap_blocks(both.reshape(2, count, part), 1, count, me), 1)
     sums = jnp.concatenate([both[0], both[1], b_out, b_exp, b_in])
 
-    kinds = pick(jnp.asarray(kind_of), me)
-    g_in = in_total()
-    g_in = jnp.stack([lax.ppermute(pick(g_in, kinds[j]), "shard", back[j]) for j in range(3)])
-    in_pieces = spread(g_in, reps)
-    g_out = jnp.transpose(swap_blocks(g_out_1, 0, count, me), (1, 0, 2)).reshape(sub, width)
     g_out = lax.all_gather(g_out, "rep", axis=0, tiled=True).astype(F32)
     g_shr = lay_out(g_shr, True)
     g_exp = assemble(exp_pieces, rep, False)

time: 857 us -> 916 us (1.069)
  the two profiles are of different devices: /device:TPU:0 before, /device:TPU:25 now
where the time goes in v3:
time: 916 us; the launch traced here: 906 us
  waiting for transfers between devices  425 us (46%)
  matrix products  147 us (16%)
  starting transfers between devices  118 us (13%)
  Pallas kernels  77.4 us (8%)
  local copies, waits for them, and re-layouts  73 us (8%)
  other arithmetic  38.4 us (4%)
  between operations  27.4 us (3%)
    ppermute x30, waiting for transfers between devices, shift(): lax.ppermute(x, 'shard', [(i, (i + offset) % count) for i in range(count)])  170 us
    ppermute x29, waiting for transfers between devices, flip(): return lax.ppermute(x, 'rep', [(i, i ^ mask) for i in range(reps)])  156 us
    ppermute x29, starting transfers between devices, flip(): return lax.ppermute(x, 'rep', [(i, i ^ mask) for i in range(reps)])  52.3 us
    dot_general x4, matrix products, nt(): lax.dot_general(a, b, (((1,), (1,)), ((), ())), preferred_element_type=F32)  52.2 us
    dot_general x4, matrix products, nn(): lax.dot_general(a, b, (((1,), (0,)), ((), ())), preferred_element_type=F32)  47.9 us
    dot_general x7, matrix products, tn(): lax.dot_general(a, b, (((0,), (0,)), ((), ())), preferred_element_type=F32)  46.5 us
    reduce_scatter x1, waiting for transfers between devices, local(): lax.psum_scatter(g_out_1.reshape(count, part, part), 'rep', scatter_dimen...  41.7 us
    ppermute x30, starting transfers between devices, shift(): lax.ppermute(x, 'shard', [(i, (i + offset) % count) for i in range(count)])  37.8 us
  transfers between devices with their start and end apart: 74, of which 32 were waited for; matrix products, arithmetic and copies ran while one was open for 22% of the time, Pallas kernels for 7%

profile of v3, /device:TPU:25, one launch (start us, length us, event | category | flops | bytes accessed | tf_op | source)
XLA Modules:
  0.0 905.9 jit_solution(6318733773149839784)
XLA Ops:
  10.7 4.2 collective-permute-start.7
  39.0 7.1 collective-permute-done.10
  47.1 15.9 %collective-permute-done.11 = bf16[64,2560]{1,0:T(8,128)(2,1)} collective-permute-done((bf16[64,2560]{1,0:T(8,128)(2,1)}, bf16[64,2560]{1,0:T(8,128)(2,1)}, u32[]{:S(2)}, u32[]{:S(2)}) %collective-permute-start.11) | collective-permute-done | bytes 327712 | tf_op jit(solution)/shard_map/ppermute | solution.py:172
  67.2 3.7 collective-permute-start.1
  79.1 3.2 fusion.49
  85.6 3.2 collective-permute-start.3
  92.7 3.4 collective-permute-done.16
  97.3 3.8 collective-permute-start.18
  101.0 18.5 %collective-permute-done.17 = bf16[256,2048]{1,0:T(8,128)(2,1)} collective-permute-done((bf16[256,2048]{1,0:T(8,128)(2,1)S(1)}, bf16[256,2048]{1,0:T(8,128)(2,1)}, u32[]{:S(2)}, u32[]{:S(2)}) %collective-permute-start.17) | collective-permute-done | bytes 1048608 | tf_op jit(solution)/shard_map/ppermute | solution.py:172
  126.5 14.6 %collective-permute-done.3 = bf16[256,2048]{1,0:T(8,128)(2,1)} collective-permute-done((bf16[256,2048]{1,0:T(8,128)(2,1)}, bf16[256,2048]{1,0:T(8,128)(2,1)}, u32[]{:S(2)}, u32[]{:S(2)}) %collective-permute-start.3) | collective-permute-done | bytes 1048608 | tf_op jit(solution)/shard_map/ppermute | solution.py:172
  142.2 3.8 collective-permute-start.5
  146.0 18.5 %collective-permute-done.4 = bf16[256,2048]{1,0:T(8,128)(2,1)} collective-permute-done((bf16[256,2048]{1,0:T(8,128)(2,1)}, bf16[256,2048]{1,0:T(8,128)(2,1)}, u32[]{:S(2)}, u32[]{:S(2)}) %collective-permute-start.4) | collective-permute-done | bytes 1048608 | tf_op jit(solution)/shard_map/ppermute | solution.py:172
  169.3 5.4 collective-permute-done.18
  175.6 11.3 %collective-permute-done.19 = bf16[128,2048]{1,0:T(8,128)(2,1)S(1)} collective-permute-done((bf16[128,2048]{1,0:T(8,128)(2,1)S(1)}, bf16[128,2048]{1,0:T(8,128)(2,1)S(1)}, u32[]{:S(2)}, u32[]{:S(2)}) %collective-permute-start.19) | collective-permute-done | bytes 524320 | tf_op jit(solution)/shard_map/ppermute | solution.py:172
  187.7 9.5 %collective-permute-done.5 = bf16[128,2048]{1,0:T(8,128)(2,1)S(1)} collective-permute-done((bf16[128,2048]{1,0:T(8,128)(2,1)S(1)}, bf16[128,2048]{1,0:T(8,128)(2,1)S(1)}, u32[]{:S(2)}, u32[]{:S(2)}) %collective-permute-start.5) | collective-permute-done | bytes 524320 | tf_op jit(solution)/shard_map/ppermute | solution.py:172
  197.2 12.1 %collective-permute-done.6 = bf16[128,2048]{1,0:T(8,128)(2,1)S(1)} collective-permute-done((bf16[128,2048]{1,0:T(8,128)(2,1)S(1)}, bf16[128,2048]{1,0:T(8,128)(2,1)S(1)}, u32[]{:S(2)}, u32[]{:S(2)}) %collective-permute-start.6) | collective-permute-done | bytes 524320 | tf_op jit(solution)/shard_map/ppermute | solution.py:172
  209.4 17.1 %multiply_convert_fusion.1 = (bf16[1024,2048]{1,0:T(8,128)(2,1)}, f32[1024,2048]{1,0:T(8,128)}) fusion(f32[2048]{0:T(1024)S(1)} %convert_element_type.258, bf16[1024,2048]{1,0:T(8,128)(2,1)S(1)} %bitcast.272, bf16[2048,2048]{1,0:T(8,128)(2,1)} %param.24), kind=kOutput, calls=%fused_computation.10 | convolution fusion | flops 8610906112 | bytes 25174016 | tf_op jit(solution)/shard_map/dot_general | solution.py:22
  226.5 11.7 %convolution_add_fusion.q_ref.k_ref.v_ref = f32[1024,1536]{1,0:T(8,128)} fusion(bf16[1024,2048]{1,0:T(8,128)(2,1)} %bitcast.273, bf16[1536,2048]{1,0:T(8,128)(2,1)} %bitcast.316, f32[1536]{0:T(1024)S(1)} %reshape.281), kind=kOutput, calls=%fused_computation.14 | convolution fusion | flops 6444023808 | bytes 16783360 | tf_op jit(solution)/shard_map/dot_general | solution.py:22
  238.2 22.5 %attend.1 = (bf16[1024,512]{1,0:T(8,128)(2,1)}, bf16[1024,512]{1,0:T(8,128)(2,1)}, bf16[1024,512]{1,0:T(8,128)(2,1)}, bf16[1024,512]{1,0:T(8,128)(2,1)}, f32[4,2,1024]{2,1,0:T(2,128)}) custom-call(f32[1024,1536]{1,0:T(8,128)} %convolution_add_fusion.q_ref.k_ref.v_ref, f32[1024,1536]{1,0:T(8,128)} %convolution_add_fusion.q_ref.k_ref.v_ref, ...), custom_call_target="tpu_custom_call" | custom-call | tf_op jit(solution)/shard_map/attend/pallas_call | solution.py:92
  260.7 14.8 %fusion.71 = f32[1024,2048]{1,0:T(8,128)} fusion(bf16[1024,2048]{1,0:T(8,128)(2,1)} %get-tuple-element.45, bf16[2048,2048]{1,0:T(8,128)(2,1)} %bitcast.314), kind=kOutput, calls=%fused_computation.210 | convolution fusion | flops 8589934592 | bytes 20971520 | tf_op jit(solution)/shard_map/dot_general | solution.py:22
  275.6 8.5 add_convert_fusion.3
  284.1 8.3 convolution_convert_fusion.2
  294.1 18.0 %multiply_convert_fusion = bf16[1024,2048]{1,0:T(8,128)(2,1)S(1)} fusion(f32[1024,2048]{1,0:T(8,128)} %get-tuple-element.141, f32[2048]{0:T(1024)S(1)} %convert_element_type.258, bf16[1024,2048]{1,0:T(8,128)(2,1)} %bitcast.35, bf16[2048,2048]{1,0:T(8,128)(2,1)} %bitcast.315), kind=kOutput, calls=%fused_computation.7 | convolution fusion | flops 8633974784 | bytes 25174016 | tf_op jit(solution)/shard_map/dot_general | solution.py:26
  312.1 10.5 %add_convert_fusion.1 = bf16[2048,1024]{1,0:T(8,128)(2,1)} fusion(bf16[2048,1024]{1,0:T(8,128)(2,1)} %collective-permute-done.20, bf16[1024,2048]{1,0:T(8,128)(2,1)} %bitcast.35, bf16[1024,2048]{1,0:T(8,128)(2,1)S(1)} %copy-done.44, s32[]{:T(128)S(6)} %select_n.296), kind=kOutput, calls=%fused_computation.6 | convolution fusion | flops 4301258752 | bytes 14680068 | tf_op jit(solution)/shard_map/dot_general | solution.py:30
  322.6 4.8 convolution_convert_fusion.1
  327.6 5.5 convolution_convert_fusion.4.g_ref
  334.7 6.4 add_convert_fusion
  341.1 5.9 convolution_convert_fusion.3
  347.1 41.7 %reduce-scatter.2.cloned.1.call-done = bf16[4,64,512]{2,1,0:T(8,128)(2,1)} async-done(((bf16[4,512,512]{2,1,0:T(8,128)(2,1)}), bf16[4,64,512]{2,1,0:T(8,128)(2,1)}) %reduce-scatter.2.cloned.1.call-update) | async-done | bytes 262160 | tf_op jit(solution)/shard_map/reduce_scatter | solution.py:466
  400.8 3.5 dynamic-slice_bitcast_fusion.5
  406.9 23.4 %collective-permute-done.24 = bf16[4,128,1024]{2,1,0:T(8,128)(2,1)S(1)} collective-permute-done((bf16[4,128,1024]{2,1,0:T(8,128)(2,1)}, bf16[4,128,1024]{2,1,0:T(8,128)(2,1)S(1)}, u32[]{:S(2)}, u32[]{:S(2)}) %collective-permute-start.24) | collective-permute-done | bytes 1048608 | tf_op jit(solution)/shard_map/ppermute | solution.py:247
  430.4 31.1 %collective-permute-done.23 = bf16[4,128,1024]{2,1,0:T(8,128)(2,1)S(1)} collective-permute-done((bf16[4,128,1024]{2,1,0:T(8,128)(2,1)}, bf16[4,128,1024]{2,1,0:T(8,128)(2,1)S(1)}, u32[]{:S(2)}, u32[]{:S(2)}) %collective-permute-start.23) | collective-permute-done | bytes 1048608 | tf_op jit(solution)/shard_map/ppermute | solution.py:247
  463.9 25.6 %attend_back.1 = (bf16[1024,512]{1,0:T(8,128)(2,1)}, bf16[1024,512]{1,0:T(8,128)(2,1)}, bf16[1024,512]{1,0:T(8,128)(2,1)}) custom-call(bf16[1024,512]{1,0:T(8,128)(2,1)} %get-tuple-element.47.q_ref, bf16[1024,512]{1,0:T(8,128)(2,1)} %get-tuple-element.48.k_ref, bf16[1024,512]{1,0:T(8,128)(2,1)} %get-tuple-element.49.v_ref, ...), custom_call_target="tpu_custom_call" | custom-call | tf_op jit(solution)/shard_map/attend_back/pallas_call | solution.py:152
  493.7 5.0 convolution_convert_fusion
  502.7 3.4 collective-permute-done.65
  506.1 17.8 %collective-permute-done.66 = bf16[128,1024]{1,0:T(8,128)(2,1)S(1)} collective-permute-done((bf16[128,1024]{1,0:T(8,128)(2,1)S(1)}, bf16[128,1024]{1,0:T(8,128)(2,1)S(1)}, u32[]{:S(2)}, u32[]{:S(2)}) %collective-permute-start.66) | collective-permute-done | bytes 262176 | tf_op jit(solution)/shard_map/ppermute | solution.py:172
  526.3 3.5 dynamic-slice_bitcast_fusion.2
  532.5 4.3 dynamic-slice_bitcast_fusion.8
  538.3 28.6 %collective-permute-done.28 = bf16[4,128,1024]{2,1,0:T(8,128)(2,1)S(1)} collective-permute-done((bf16[4,128,1024]{2,1,0:T(8,128)(2,1)}, bf16[4,128,1024]{2,1,0:T(8,128)(2,1)S(1)}, u32[]{:S(2)}, u32[]{:S(2)}) %collective-permute-start.28) | collective-permute-done | bytes 1048608 | tf_op jit(solution)/shard_map/ppermute | solution.py:247
  566.9 26.1 %collective-permute-done.27 = bf16[4,128,1024]{2,1,0:T(8,128)(2,1)S(1)} collective-permute-done((bf16[4,128,1024]{2,1,0:T(8,128)(2,1)}, bf16[4,128,1024]{2,1,0:T(8,128)(2,1)S(1)}, u32[]{:S(2)}, u32[]{:S(2)}) %collective-permute-start.27) | collective-permute-done | bytes 1048608 | tf_op jit(solution)/shard_map/ppermute | solution.py:247
  597.5 5.6 add_convert_fusion.4
  606.6 11.1 %fusion.72 = f32[1024,2048]{1,0:T(8,128)} fusion(bf16[1024,2048]{1,0:T(8,128)(2,1)S(1)} %copy-done.12, bf16[2048,2048]{1,0:T(8,128)(2,1)S(1)} %bitcast.313), kind=kOutput, calls=%fused_computation.211 | convolution fusion | flops 8589934592 | bytes 20971520 | tf_op jit(solution)/shard_map/dot_general | solution.py:26
  617.7 13.3 %multiply_reduce_fusion = (f32[2048]{0:T(1024)S(1)}, f32[2048]{0:T(1024)S(1)}, bf16[1024,2048]{1,0:T(8,128)(2,1)}) fusion(bf16[4,256,2048]{2,1,0:T(8,128)(2,1)S(1)} %copy-done.18, f32[1024,2048]{1,0:T(8,128)} %fusion.72, bf16[1024,1536]{1,0:T(8,128)(2,1)S(1)} %copy-done.8, bf16[1536,2048]{1,0:T(8,128)(2,1)} %bitcast.317), kind=kOutput, calls=%fused_computation.4 | convolution fusion | flops 6455029760 | bytes 26230784 | tf_op jit(solution)/shard_map/dot_general | solution.py:26
  631.7 19.7 %collective-permute-done.35 = bf16[3,128,1024]{2,1,0:T(8,128)(2,1)S(1)} collective-permute-done((bf16[3,128,1024]{2,1,0:T(8,128)(2,1)S(1)}, bf16[3,128,1024]{2,1,0:T(8,128)(2,1)S(1)}, u32[]{:S(2)}, u32[]{:S(2)}) %collective-permute-start.35) | collective-permute-done | bytes 786464 | tf_op jit(solution)/shard_map/ppermute | solution.py:247
  651.4 16.7 %collective-permute-done.34 = bf16[3,128,1024]{2,1,0:T(8,128)(2,1)S(1)} collective-permute-done((bf16[3,128,1024]{2,1,0:T(8,128)(2,1)S(1)}, bf16[3,128,1024]{2,1,0:T(8,128)(2,1)S(1)}, u32[]{:S(2)}, u32[]{:S(2)}) %collective-permute-start.34) | collective-permute-done | bytes 786464 | tf_op jit(solution)/shard_map/ppermute | solution.py:247
  681.2 7.7 collective-permute-done.29
  688.9 4.3 collective-permute-start.62
  693.3 7.6 collective-permute-done.31
  700.8 5.0 collective-permute-start.39
  710.5 12.7 %collective-permute-done.15 = bf16[256,2048]{1,0:T(8,128)(2,1)S(1)} collective-permute-done((bf16[256,2048]{1,0:T(8,128)(2,1)}, bf16[256,2048]{1,0:T(8,128)(2,1)S(1)}, u32[]{:S(2)}, u32[]{:S(2)}) %collective-permute-start.15) | collective-permute-done | bytes 1048608 | tf_op jit(solution)/shard_map/ppermute | solution.py:172
  740.0 3.6 collective-permute-start.44
  752.4 10.8 %assemble.3 = f32[4,4,128,2048]{3,2,1,0:T(8,128)} custom-call(s32[2]{0:T(128)S(1)} %pad_add_fusion.place_ref, bf16[4,128,1024]{2,1,0:T(8,128)(2,1)S(1)} %fusion.26.refs_0_, bf16[4,128,1024]{2,1,0:T(8,128)(2,1)S(1)} %collective-permute-done.58.refs_1_, bf16[4,128,1024]{2,1,0:T(8,128)(2,1)S(1)} %collective-permute-done.59.refs_2_, ...), custom_call_target="tpu_custom_call" | custom-call | tf_op jit(solution)/shard_map/assemble/pallas_call | solution.py:295
  763.2 21.5 %collective-permute-done.43 = bf16[128,1024]{1,0:T(8,128)(2,1)} collective-permute-done((bf16[128,1024]{1,0:T(8,128)(2,1)}, bf16[128,1024]{1,0:T(8,128)(2,1)}, u32[]{:S(2)}, u32[]{:S(2)}) %collective-permute-start.43) | collective-permute-done | bytes 262176 | tf_op jit(solution)/shard_map/ppermute | solution.py:495
  784.7 8.1 collective-permute-start.53
  792.8 4.2 collective-permute-start.52
  798.2 6.2 collective-permute-done.53
  805.3 26.1 %collective-permute-done.52 = f32[512]{0:T(512)S(1)} collective-permute-done((f32[512]{0:T(512)S(1)}, f32[512]{0:T(512)S(1)}, u32[]{:S(2)}, u32[]{:S(2)}) %collective-permute-start.52) | collective-permute-done | bytes 2080 | tf_op jit(solution)/shard_map/ppermute | solution.py:519
  840.8 8.2 collective-permute-done.45.refs_1_
  849.0 4.3 collective-permute-start.49
  853.3 15.3 %collective-permute-start.50 = (bf16[3,128,1024]{2,1,0:T(8,128)(2,1)S(1)}, bf16[3,128,1024]{2,1,0:T(8,128)(2,1)S(1)}, u32[]{:S(2)}, u32[]{:S(2)}) collective-permute-start(bf16[3,128,1024]{2,1,0:T(8,128)(2,1)S(1)} %collective-permute-done.46.refs_2_), channel_id=1, source_target_pairs={{0,4},{4,0},{8,12},{12,8},{16,20},{20,16},{24,28},{28,24},{1,5},{5... | collective-permute-start | bytes 2359304 | tf_op jit(solution)/shard_map/ppermute | solution.py:247
  868.7 6.0 fusion.15
  875.6 8.1 assemble.2
  883.7 4.1 convert_element_type.320
  887.8 10.5 %place.1 = f32[1,4,128,8192]{3,2,1,0:T(8,128)} custom-call(bf16[8,4,128,1024]{3,2,1,0:T(8,128)(2,1)} %all-gather.14.cloned.1.call-done.x_ref), custom_call_target="tpu_custom_call" | custom-call | tf_op jit(solution)/shard_map/place/pallas_call | solution.py:323
  (356 shorter events, 151.5 us)
Async XLA Ops:
  7.2 219.3 %all-gather.6.cloned.1.call-start = ((), (), s32[]{:S(2)}) async-start(), calls=%async_computation.1 | async-start | bytes 7077888 | tf_op jit(solution)/shard_map/all_gather | solution.py:386
  8.6 13.5 %collective-permute-start.9 = (bf16[64,2048]{1,0:T(8,128)(2,1)S(1)}, bf16[64,2048]{1,0:T(8,128)(2,1)S(1)}, u32[]{:S(2)}, u32[]{:S(2)}) collective-permute-start(bf16[64,2048]{1,0:T(8,128)(2,1)S(1)} %get-tuple-element.81), channel_id=1, source_target_pairs={{0,2},{1,1},{2,0},{3,3},{4,6},{5,5},{6,4},{7,7},{8,10},{9,9},{10,8... | collective-permute-start | bytes 786440 | tf_op jit(solution)/shard_map/ppermute | solution.py:383
  9.2 12.9 %collective-permute-start.8 = (bf16[64,2048]{1,0:T(8,128)(2,1)S(1)}, bf16[64,2048]{1,0:T(8,128)(2,1)S(1)}, u32[]{:S(2)}, u32[]{:S(2)}) collective-permute-start(bf16[64,2048]{1,0:T(8,128)(2,1)S(1)} %get-tuple-element.80), channel_id=1, source_target_pairs={{0,1},{1,0},{2,3},{3,2},{4,5},{5,4},{6,7},{7,6},{8,9},{9,8},{10,11... | collective-permute-start | bytes 786440 | tf_op jit(solution)/shard_map/ppermute | solution.py:383
  10.7 14.5 %collective-permute-start.7 = (bf16[64,2048]{1,0:T(8,128)(2,1)S(1)}, bf16[64,2048]{1,0:T(8,128)(2,1)}, u32[]{:S(2)}, u32[]{:S(2)}) collective-permute-start(bf16[64,2048]{1,0:T(8,128)(2,1)S(1)} %get-tuple-element.79), channel_id=1, source_target_pairs={{0,0},{1,3},{2,2},{3,1},{4,4},{5,7},{6,6},{7,5},{8,8},{9,11},{10,1... | collective-permute-start | bytes 786440 | tf_op jit(solution)/shard_map/ppermute | solution.py:383
  27.3 233.4 %all-gather.8.cloned.1.call-start = ((), (), s32[]{:S(2)}) async-start(), calls=%async_computation.2 | async-start | bytes 9437184 | tf_op jit(solution)/shard_map/all_gather | solution.py:395
  35.7 10.3 %collective-permute-start.10 = (bf16[64,2560]{1,0:T(8,128)(2,1)}, bf16[64,2560]{1,0:T(8,128)(2,1)}, u32[]{:S(2)}, u32[]{:S(2)}) collective-permute-start(bf16[64,2560]{1,0:T(8,128)(2,1)} %bitcast.257), channel_id=1, source_target_pairs={{0,1},{1,2},{2,3},{3,0},{4,5},{5,6},{6,7},{7,4},{8,9},{9,10},{10,1... | collective-permute-start | bytes 983048 | tf_op jit(solution)/shard_map/ppermute | solution.py:172
  36.5 26.5 %collective-permute-start.11 = (bf16[64,2560]{1,0:T(8,128)(2,1)}, bf16[64,2560]{1,0:T(8,128)(2,1)}, u32[]{:S(2)}, u32[]{:S(2)}) collective-permute-start(bf16[64,2560]{1,0:T(8,128)(2,1)} %bitcast.256), channel_id=1, source_target_pairs={{0,2},{1,3},{2,0},{3,1},{4,6},{5,7},{6,4},{7,5},{8,10},{9,11},{10,... | collective-permute-start | bytes 983048 | tf_op jit(solution)/shard_map/ppermute | solution.py:172
  37.3 26.7 %collective-permute-start.12 = (bf16[64,2560]{1,0:T(8,128)(2,1)}, bf16[64,2560]{1,0:T(8,128)(2,1)}, u32[]{:S(2)}, u32[]{:S(2)}) collective-permute-start(bf16[64,2560]{1,0:T(8,128)(2,1)} %bitcast.255), channel_id=1, source_target_pairs={{0,3},{1,0},{2,1},{3,2},{4,7},{5,4},{6,5},{7,6},{8,11},{9,8},{10,9... | collective-permute-start | bytes 983048 | tf_op jit(solution)/shard_map/ppermute | solution.py:172
  66.2 209.4 %all-gather.10.cloned.1.call-start = ((), (), s32[]{:S(2)}) async-start(), calls=%async_computation.3 | async-start | bytes 2359296 | tf_op jit(solution)/shard_map/all_gather | solution.py:396
  67.2 16.4 %collective-permute-start = (bf16[3584]{0:T(1024)(128)(2,1)S(1)}, bf16[3584]{0:T(1024)(128)(2,1)S(1)}, u32[]{:S(2)}, u32[]{:S(2)}) collective-permute-start(bf16[3584]{0:T(1024)(128)(2,1)S(1)} %constant_dynamic-update-slice_fusion.7), channel_id=1, source_target_pairs={{0,1},{1,2},{2,3},{3,0},{4,5},{5,6},{6,7},{7,4},{8,9},{9,10},{10,1... | collective-permute-start | bytes 21512 | tf_op jit(solution)/shard_map/ppermute | solution.py:172
  67.2 16.5 %collective-permute-start.1 = (bf16[3584]{0:T(1024)(128)(2,1)S(1)}, bf16[3584]{0:T(1024)(128)(2,1)S(1)}, u32[]{:S(2)}, u32[]{:S(2)}) collective-permute-start(bf16[3584]{0:T(1024)(128)(2,1)S(1)} %constant_dynamic-update-slice_fusion.7), channel_id=1, source_target_pairs={{0,2},{1,3},{2,0},{3,1},{4,6},{5,7},{6,4},{7,5},{8,10},{9,11},{10,... | collective-permute-start | bytes 21512 | tf_op jit(solution)/shard_map/ppermute | solution.py:172
  70.9 13.0 %collective-permute-start.2 = (bf16[3584]{0:T(1024)(128)(2,1)S(1)}, bf16[3584]{0:T(1024)(128)(2,1)S(1)}, u32[]{:S(2)}, u32[]{:S(2)}) collective-permute-start(bf16[3584]{0:T(1024)(128)(2,1)S(1)} %constant_dynamic-update-slice_fusion.7), channel_id=1, source_target_pairs={{0,3},{1,0},{2,1},{3,2},{4,7},{5,4},{6,5},{7,6},{8,11},{9,8},{10,9... | collective-permute-start | bytes 21512 | tf_op jit(solution)/shard_map/ppermute | solution.py:172
  72.3 23.8 %collective-permute-start.16 = (bf16[256,2048]{1,0:T(8,128)(2,1)S(1)}, bf16[256,2048]{1,0:T(8,128)(2,1)}, u32[]{:S(2)}, u32[]{:S(2)}) collective-permute-start(bf16[256,2048]{1,0:T(8,128)(2,1)S(1)} %bitcast.268), channel_id=1, source_target_pairs={{0,1},{1,2},{2,3},{3,0},{4,5},{5,6},{6,7},{7,4},{8,9},{9,10},{10,1... | collective-permute-start | bytes 3145736 | tf_op jit(solution)/shard_map/ppermute | solution.py:172
  74.2 45.3 %collective-permute-start.17 = (bf16[256,2048]{1,0:T(8,128)(2,1)S(1)}, bf16[256,2048]{1,0:T(8,128)(2,1)}, u32[]{:S(2)}, u32[]{:S(2)}) collective-permute-start(bf16[256,2048]{1,0:T(8,128)(2,1)S(1)} %bitcast.269), channel_id=1, source_target_pairs={{0,3},{1,0},{2,1},{3,2},{4,7},{5,4},{6,5},{7,6},{8,11},{9,8},{10,9... | collective-permute-start | bytes 3145736 | tf_op jit(solution)/shard_map/ppermute | solution.py:172
  85.6 55.6 %collective-permute-start.3 = (bf16[256,2048]{1,0:T(8,128)(2,1)}, bf16[256,2048]{1,0:T(8,128)(2,1)}, u32[]{:S(2)}, u32[]{:S(2)}) collective-permute-start(bf16[256,2048]{1,0:T(8,128)(2,1)} %fusion.10), channel_id=1, source_target_pairs={{0,1},{1,2},{2,3},{3,0},{4,5},{5,6},{6,7},{7,4},{8,9},{9,10},{10,1... | collective-permute-start | bytes 3145736 | tf_op jit(solution)/shard_map/ppermute | solution.py:172
  88.8 75.7 %collective-permute-start.4 = (bf16[256,2048]{1,0:T(8,128)(2,1)}, bf16[256,2048]{1,0:T(8,128)(2,1)}, u32[]{:S(2)}, u32[]{:S(2)}) collective-permute-start(bf16[256,2048]{1,0:T(8,128)(2,1)} %fusion.10), channel_id=1, source_target_pairs={{0,3},{1,0},{2,1},{3,2},{4,7},{5,4},{6,5},{7,6},{8,11},{9,8},{10,9... | collective-permute-start | bytes 3145736 | tf_op jit(solution)/shard_map/ppermute | solution.py:172
  92.7 296.1 %reduce-scatter.2.cloned.1.call-start = ((), (), s32[]{:S(2)}) async-start(), calls=%async_computation.4 | async-start | bytes 2359296 | tf_op jit(solution)/shard_map/reduce_scatter | solution.py:466
  97.3 77.5 %collective-permute-start.18 = (bf16[128,2048]{1,0:T(8,128)(2,1)S(1)}, bf16[128,2048]{1,0:T(8,128)(2,1)S(1)}, u32[]{:S(2)}, u32[]{:S(2)}) collective-permute-start(bf16[128,2048]{1,0:T(8,128)(2,1)S(1)} %slice.197), channel_id=1, source_target_pairs={{0,1},{1,2},{2,3},{3,0},{4,5},{5,6},{6,7},{7,4},{8,9},{9,10},{10,1... | collective-permute-start | bytes 1572872 | tf_op jit(solution)/shard_map/ppermute | solution.py:172
  120.6 66.3 %collective-permute-start.19 = (bf16[128,2048]{1,0:T(8,128)(2,1)S(1)}, bf16[128,2048]{1,0:T(8,128)(2,1)S(1)}, u32[]{:S(2)}, u32[]{:S(2)}) collective-permute-start(bf16[128,2048]{1,0:T(8,128)(2,1)S(1)} %slice.198), channel_id=1, source_target_pairs={{0,3},{1,0},{2,1},{3,2},{4,7},{5,4},{6,5},{7,6},{8,11},{9,8},{10,9... | collective-permute-start | bytes 1572872 | tf_op jit(solution)/shard_map/ppermute | solution.py:172
  142.2 55.0 %collective-permute-start.5 = (bf16[128,2048]{1,0:T(8,128)(2,1)S(1)}, bf16[128,2048]{1,0:T(8,128)(2,1)S(1)}, u32[]{:S(2)}, u32[]{:S(2)}) collective-permute-start(bf16[128,2048]{1,0:T(8,128)(2,1)S(1)} %slice.190), channel_id=1, source_target_pairs={{0,1},{1,2},{2,3},{3,0},{4,5},{5,6},{6,7},{7,4},{8,9},{9,10},{10,1... | collective-permute-start | bytes 1572872 | tf_op jit(solution)/shard_map/ppermute | solution.py:172
  165.5 43.8 %collective-permute-start.6 = (bf16[128,2048]{1,0:T(8,128)(2,1)S(1)}, bf16[128,2048]{1,0:T(8,128)(2,1)S(1)}, u32[]{:S(2)}, u32[]{:S(2)}) collective-permute-start(bf16[128,2048]{1,0:T(8,128)(2,1)S(1)} %slice.191), channel_id=1, source_target_pairs={{0,3},{1,0},{2,1},{3,2},{4,7},{5,4},{6,5},{7,6},{8,11},{9,8},{10,9... | collective-permute-start | bytes 1572872 | tf_op jit(solution)/shard_map/ppermute | solution.py:172
  292.4 19.7 %collective-permute-start.20 = (bf16[2048,1024]{1,0:T(8,128)(2,1)}, bf16[2048,1024]{1,0:T(8,128)(2,1)}, u32[]{:S(2)}, u32[]{:S(2)}) collective-permute-start(bf16[2048,1024]{1,0:T(8,128)(2,1)} %convolution_convert_fusion.2), channel_id=1, source_target_pairs={{0,4},{4,0},{8,12},{12,8},{16,20},{20,16},{24,28},{28,24},{1,5},{5... | collective-permute-start | bytes 12582920 | tf_op jit(solution)/shard_map/ppermute | solution.py:247
  327.5 7.2 collective-permute-start.21
  347.0 536.7 %all-gather.12.cloned.1.call-start = ((), (), s32[]{:S(2)}) async-start(), calls=%async_computation.5 | async-start | bytes 2359296 | tf_op jit(solution)/shard_map/all_gather | solution.py:501
  400.7 487.1 %all-gather.14.cloned.1.call-start = ((), (), s32[]{:S(2)}) async-start(), calls=%async_computation.6 | async-start | bytes 9437184 | tf_op jit(solution)/shard_map/all_gather | solution.py:477
  404.3 26.1 %collective-permute-start.24 = (bf16[4,128,1024]{2,1,0:T(8,128)(2,1)}, bf16[4,128,1024]{2,1,0:T(8,128)(2,1)S(1)}, u32[]{:S(2)}, u32[]{:S(2)}) collective-permute-start(bf16[4,128,1024]{2,1,0:T(8,128)(2,1)} %get-tuple-element.92), channel_id=1, source_target_pairs={{0,24},{4,28},{8,16},{12,20},{16,8},{20,12},{24,0},{28,4},{1,25},{... | collective-permute-start | bytes 3145736 | tf_op jit(solution)/shard_map/ppermute | solution.py:247
  405.5 56.0 %collective-permute-start.23 = (bf16[4,128,1024]{2,1,0:T(8,128)(2,1)}, bf16[4,128,1024]{2,1,0:T(8,128)(2,1)S(1)}, u32[]{:S(2)}, u32[]{:S(2)}) collective-permute-start(bf16[4,128,1024]{2,1,0:T(8,128)(2,1)} %get-tuple-element.93), channel_id=1, source_target_pairs={{0,16},{4,20},{8,24},{12,28},{16,0},{20,4},{24,8},{28,12},{1,17},{... | collective-permute-start | bytes 3145736 | tf_op jit(solution)/shard_map/ppermute | solution.py:247
  406.7 54.8 %collective-permute-start.22 = (bf16[4,128,1024]{2,1,0:T(8,128)(2,1)S(1)}, bf16[4,128,1024]{2,1,0:T(8,128)(2,1)}, u32[]{:S(2)}, u32[]{:S(2)}) collective-permute-start(bf16[4,128,1024]{2,1,0:T(8,128)(2,1)S(1)} %get-tuple-element.91), channel_id=1, source_target_pairs={{0,8},{4,12},{8,0},{12,4},{16,24},{20,28},{24,16},{28,20},{1,9},{5... | collective-permute-start | bytes 3145736 | tf_op jit(solution)/shard_map/ppermute | solution.py:247
  498.8 7.3 collective-permute-start.65
  500.0 23.9 %collective-permute-start.66 = (bf16[128,1024]{1,0:T(8,128)(2,1)S(1)}, bf16[128,1024]{1,0:T(8,128)(2,1)S(1)}, u32[]{:S(2)}, u32[]{:S(2)}) collective-permute-start(bf16[128,1024]{1,0:T(8,128)(2,1)S(1)} %get-tuple-element.105), channel_id=1, source_target_pairs={{0,2},{1,3},{2,0},{3,1},{4,6},{5,7},{6,4},{7,5},{8,10},{9,11},{10,... | collective-permute-start | bytes 786440 | tf_op jit(solution)/shard_map/ppermute | solution.py:172
  501.3 22.7 %collective-permute-start.67 = (bf16[128,1024]{1,0:T(8,128)(2,1)S(1)}, bf16[128,1024]{1,0:T(8,128)(2,1)S(1)}, u32[]{:S(2)}, u32[]{:S(2)}) collective-permute-start(bf16[128,1024]{1,0:T(8,128)(2,1)S(1)} %get-tuple-element.104), channel_id=1, source_target_pairs={{0,3},{1,0},{2,1},{3,2},{4,7},{5,4},{6,5},{7,6},{8,11},{9,8},{10,9... | collective-permute-start | bytes 786440 | tf_op jit(solution)/shard_map/ppermute | solution.py:172
  525.0 72.5 %collective-permute-start.25 = (bf16[1536,1024]{1,0:T(8,128)(2,1)}, bf16[1536,1024]{1,0:T(8,128)(2,1)}, u32[]{:S(2)}, u32[]{:S(2)}) collective-permute-start(bf16[1536,1024]{1,0:T(8,128)(2,1)} %convolution_convert_fusion), channel_id=1, source_target_pairs={{0,4},{4,0},{8,12},{12,8},{16,20},{20,16},{24,28},{28,24},{1,5},{5... | collective-permute-start | bytes 9437192 | tf_op jit(solution)/shard_map/ppermute | solution.py:247
  529.8 37.1 %collective-permute-start.28 = (bf16[4,128,1024]{2,1,0:T(8,128)(2,1)}, bf16[4,128,1024]{2,1,0:T(8,128)(2,1)S(1)}, u32[]{:S(2)}, u32[]{:S(2)}) collective-permute-start(bf16[4,128,1024]{2,1,0:T(8,128)(2,1)} %get-tuple-element.89), channel_id=1, source_target_pairs={{0,24},{4,28},{8,16},{12,20},{16,8},{20,12},{24,0},{28,4},{1,25},{... | collective-permute-start | bytes 3145736 | tf_op jit(solution)/shard_map/ppermute | solution.py:247
  531.0 62.0 %collective-permute-start.27 = (bf16[4,128,1024]{2,1,0:T(8,128)(2,1)}, bf16[4,128,1024]{2,1,0:T(8,128)(2,1)S(1)}, u32[]{:S(2)}, u32[]{:S(2)}) collective-permute-start(bf16[4,128,1024]{2,1,0:T(8,128)(2,1)} %get-tuple-element.90), channel_id=1, source_target_pairs={{0,16},{4,20},{8,24},{12,28},{16,0},{20,4},{24,8},{28,12},{1,17},{... | collective-permute-start | bytes 3145736 | tf_op jit(solution)/shard_map/ppermute | solution.py:247
  532.1 61.0 %collective-permute-start.26 = (bf16[4,128,1024]{2,1,0:T(8,128)(2,1)S(1)}, bf16[4,128,1024]{2,1,0:T(8,128)(2,1)}, u32[]{:S(2)}, u32[]{:S(2)}) collective-permute-start(bf16[4,128,1024]{2,1,0:T(8,128)(2,1)S(1)} %get-tuple-element.88), channel_id=1, source_target_pairs={{0,8},{4,12},{8,0},{12,4},{16,24},{20,28},{24,16},{28,20},{1,9},{5... | collective-permute-start | bytes 3145736 | tf_op jit(solution)/shard_map/ppermute | solution.py:247
  595.5 83.6 %collective-permute-start.58 = (bf16[4,128,1024]{2,1,0:T(8,128)(2,1)S(1)}, bf16[4,128,1024]{2,1,0:T(8,128)(2,1)S(1)}, u32[]{:S(2)}, u32[]{:S(2)}) collective-permute-start(bf16[4,128,1024]{2,1,0:T(8,128)(2,1)S(1)} %fusion.26.refs_0_), channel_id=1, source_target_pairs={{0,8},{4,12},{8,0},{12,4},{16,24},{20,28},{24,16},{28,20},{1,9},{5... | collective-permute-start | bytes 3145736 | tf_op jit(solution)/shard_map/ppermute | solution.py:247
  596.5 82.7 %collective-permute-start.59 = (bf16[4,128,1024]{2,1,0:T(8,128)(2,1)S(1)}, bf16[4,128,1024]{2,1,0:T(8,128)(2,1)S(1)}, u32[]{:S(2)}, u32[]{:S(2)}) collective-permute-start(bf16[4,128,1024]{2,1,0:T(8,128)(2,1)S(1)} %fusion.26.refs_0_), channel_id=1, source_target_pairs={{0,16},{4,20},{8,24},{12,28},{16,0},{20,4},{24,8},{28,12},{1,17},{... | collective-permute-start | bytes 3145736 | tf_op jit(solution)/shard_map/ppermute | solution.py:247
  603.9 47.5 %collective-permute-start.35 = (bf16[3,128,1024]{2,1,0:T(8,128)(2,1)S(1)}, bf16[3,128,1024]{2,1,0:T(8,128)(2,1)S(1)}, u32[]{:S(2)}, u32[]{:S(2)}) collective-permute-start(bf16[3,128,1024]{2,1,0:T(8,128)(2,1)S(1)} %get-tuple-element.98), channel_id=1, source_target_pairs={{0,24},{4,28},{8,16},{12,20},{16,8},{20,12},{24,0},{28,4},{1,25},{... | collective-permute-start | bytes 2359304 | tf_op jit(solution)/shard_map/ppermute | solution.py:247
  605.1 63.0 %collective-permute-start.34 = (bf16[3,128,1024]{2,1,0:T(8,128)(2,1)S(1)}, bf16[3,128,1024]{2,1,0:T(8,128)(2,1)S(1)}, u32[]{:S(2)}, u32[]{:S(2)}) collective-permute-start(bf16[3,128,1024]{2,1,0:T(8,128)(2,1)S(1)} %get-tuple-element.99), channel_id=1, source_target_pairs={{0,16},{4,20},{8,24},{12,28},{16,0},{20,4},{24,8},{28,12},{1,17},{... | collective-permute-start | bytes 2359304 | tf_op jit(solution)/shard_map/ppermute | solution.py:247
  606.6 61.5 %collective-permute-start.33 = (bf16[3,128,1024]{2,1,0:T(8,128)(2,1)S(1)}, bf16[3,128,1024]{2,1,0:T(8,128)(2,1)S(1)}, u32[]{:S(2)}, u32[]{:S(2)}) collective-permute-start(bf16[3,128,1024]{2,1,0:T(8,128)(2,1)S(1)} %get-tuple-element.97), channel_id=1, source_target_pairs={{0,8},{4,12},{8,0},{12,4},{16,24},{20,28},{24,16},{28,20},{1,9},{5... | collective-permute-start | bytes 2359304 | tf_op jit(solution)/shard_map/ppermute | solution.py:247
  671.2 7.7 collective-permute-start.38
  675.5 32.3 %collective-permute-start.60 = (bf16[4,128,1024]{2,1,0:T(8,128)(2,1)S(1)}, bf16[4,128,1024]{2,1,0:T(8,128)(2,1)}, u32[]{:S(2)}, u32[]{:S(2)}) collective-permute-start(bf16[4,128,1024]{2,1,0:T(8,128)(2,1)S(1)} %fusion.26.refs_0_), channel_id=1, source_target_pairs={{0,24},{4,28},{8,16},{12,20},{16,8},{20,12},{24,0},{28,4},{1,25},{... | collective-permute-start | bytes 3145736 | tf_op jit(solution)/shard_map/ppermute | solution.py:247
  676.9 12.1 %collective-permute-start.29 = (bf16[128,2048]{1,0:T(8,128)(2,1)}, bf16[128,2048]{1,0:T(8,128)(2,1)}, u32[]{:S(2)}, u32[]{:S(2)}) collective-permute-start(bf16[128,2048]{1,0:T(8,128)(2,1)} %get-tuple-element.84), channel_id=1, source_target_pairs={{0,1},{1,2},{2,3},{3,0},{4,5},{5,6},{6,7},{7,4},{8,9},{9,10},{10,1... | collective-permute-start | bytes 1572872 | tf_op jit(solution)/shard_map/ppermute | solution.py:172
  678.8 22.0 %collective-permute-start.31 = (bf16[128,2048]{1,0:T(8,128)(2,1)}, bf16[128,2048]{1,0:T(8,128)(2,1)}, u32[]{:S(2)}, u32[]{:S(2)}) collective-permute-start(bf16[128,2048]{1,0:T(8,128)(2,1)} %get-tuple-element.86), channel_id=1, source_target_pairs={{0,3},{1,0},{2,1},{3,2},{4,7},{5,4},{6,5},{7,6},{8,11},{9,8},{10,9... | collective-permute-start | bytes 1572872 | tf_op jit(solution)/shard_map/ppermute | solution.py:172
  679.1 44.1 %collective-permute-start.15 = (bf16[256,2048]{1,0:T(8,128)(2,1)}, bf16[256,2048]{1,0:T(8,128)(2,1)S(1)}, u32[]{:S(2)}, u32[]{:S(2)}) collective-permute-start(bf16[256,2048]{1,0:T(8,128)(2,1)} %get-tuple-element.95), channel_id=1, source_target_pairs={{0,3},{1,0},{2,1},{3,2},{4,7},{5,4},{6,5},{7,6},{8,11},{9,8},{10,9... | collective-permute-start | bytes 3145736 | tf_op jit(solution)/shard_map/ppermute | solution.py:172
  679.2 46.2 %collective-permute-start.61 = (bf16[4,128,1024]{2,1,0:T(8,128)(2,1)S(1)}, bf16[4,128,1024]{2,1,0:T(8,128)(2,1)S(1)}, u32[]{:S(2)}, u32[]{:S(2)}) collective-permute-start(bf16[4,128,1024]{2,1,0:T(8,128)(2,1)S(1)} %fusion.26.refs_0_), channel_id=1, source_target_pairs={{0,4},{4,0},{8,12},{12,8},{16,20},{20,16},{24,28},{28,24},{1,5},{5... | collective-permute-start | bytes 3145736 | tf_op jit(solution)/shard_map/ppermute | solution.py:247
  688.9 47.9 %collective-permute-start.62 = (bf16[4,128,1024]{2,1,0:T(8,128)(2,1)S(1)}, bf16[4,128,1024]{2,1,0:T(8,128)(2,1)}, u32[]{:S(2)}, u32[]{:S(2)}) collective-permute-start(bf16[4,128,1024]{2,1,0:T(8,128)(2,1)S(1)} %collective-permute-done.58.refs_1_), channel_id=1, source_target_pairs={{0,4},{4,0},{8,12},{12,8},{16,20},{20,16},{24,28},{28,24},{1,5},{5... | collective-permute-start | bytes 3145736 | tf_op jit(solution)/shard_map/ppermute | solution.py:247
  707.8 35.8 %collective-permute-start.63 = (bf16[4,128,1024]{2,1,0:T(8,128)(2,1)S(1)}, bf16[4,128,1024]{2,1,0:T(8,128)(2,1)}, u32[]{:S(2)}, u32[]{:S(2)}) collective-permute-start(bf16[4,128,1024]{2,1,0:T(8,128)(2,1)S(1)} %collective-permute-done.59.refs_2_), channel_id=1, source_target_pairs={{0,4},{4,0},{8,12},{12,8},{16,20},{20,16},{24,28},{28,24},{1,5},{5... | collective-permute-start | bytes 3145736 | tf_op jit(solution)/shard_map/ppermute | solution.py:247
  707.9 36.4 %collective-permute-start.64 = (bf16[4,128,1024]{2,1,0:T(8,128)(2,1)}, bf16[4,128,1024]{2,1,0:T(8,128)(2,1)}, u32[]{:S(2)}, u32[]{:S(2)}) collective-permute-start(bf16[4,128,1024]{2,1,0:T(8,128)(2,1)} %collective-permute-done.60.refs_3_), channel_id=1, source_target_pairs={{0,4},{4,0},{8,12},{12,8},{16,20},{20,16},{24,28},{28,24},{1,5},{5... | collective-permute-start | bytes 3145736 | tf_op jit(solution)/shard_map/ppermute | solution.py:247
  726.3 105.5 %collective-permute-start.32 = (bf16[256,2048]{1,0:T(8,128)(2,1)}, bf16[256,2048]{1,0:T(8,128)(2,1)}, u32[]{:S(2)}, u32[]{:S(2)}) collective-permute-start(bf16[256,2048]{1,0:T(8,128)(2,1)} %pad_maximum_fusion.1), channel_id=1, source_target_pairs={{0,3},{1,0},{2,1},{3,2},{4,7},{5,4},{6,5},{7,6},{8,11},{9,8},{10,9... | collective-permute-start | bytes 3145736 | tf_op jit(solution)/shard_map/ppermute | solution.py:172
  728.0 104.9 %collective-permute-start.30 = (bf16[256,2048]{1,0:T(8,128)(2,1)}, bf16[256,2048]{1,0:T(8,128)(2,1)}, u32[]{:S(2)}, u32[]{:S(2)}) collective-permute-start(bf16[256,2048]{1,0:T(8,128)(2,1)} %pad_maximum_fusion), channel_id=1, source_target_pairs={{0,1},{1,2},{2,3},{3,0},{4,5},{5,6},{6,7},{7,4},{8,9},{9,10},{10,1... | collective-permute-start | bytes 3145736 | tf_op jit(solution)/shard_map/ppermute | solution.py:172
  740.0 9.2 %collective-permute-start.44 = (bf16[128,1024]{1,0:T(8,128)(2,1)}, bf16[128,1024]{1,0:T(8,128)(2,1)}, u32[]{:S(2)}, u32[]{:S(2)}) collective-permute-start(bf16[128,1024]{1,0:T(8,128)(2,1)} %get-tuple-element.110), channel_id=1, source_target_pairs={{2,0},{1,1},{0,2},{3,3},{6,4},{5,5},{4,6},{7,7},{10,8},{9,9},{8,10... | collective-permute-start | bytes 786440 | tf_op jit(solution)/shard_map/ppermute | solution.py:495
  744.3 40.4 %collective-permute-start.43 = (bf16[128,1024]{1,0:T(8,128)(2,1)}, bf16[128,1024]{1,0:T(8,128)(2,1)}, u32[]{:S(2)}, u32[]{:S(2)}) collective-permute-start(bf16[128,1024]{1,0:T(8,128)(2,1)} %get-tuple-element.111), channel_id=1, source_target_pairs={{1,0},{0,1},{3,2},{2,3},{5,4},{4,5},{7,6},{6,7},{9,8},{8,9},{11,10... | collective-permute-start | bytes 786440 | tf_op jit(solution)/shard_map/ppermute | solution.py:495
  746.0 46.7 %collective-permute-start.42 = (bf16[128,1024]{1,0:T(8,128)(2,1)S(1)}, bf16[128,1024]{1,0:T(8,128)(2,1)}, u32[]{:S(2)}, u32[]{:S(2)}) collective-permute-start(bf16[128,1024]{1,0:T(8,128)(2,1)S(1)} %get-tuple-element.109), channel_id=1, source_target_pairs={{0,0},{3,1},{2,2},{1,3},{4,4},{7,5},{6,6},{5,7},{8,8},{11,9},{10,1... | collective-permute-start | bytes 786440 | tf_op jit(solution)/shard_map/ppermute | solution.py:495
  749.2 89.2 %collective-permute-start.14 = (bf16[256,2048]{1,0:T(8,128)(2,1)}, bf16[256,2048]{1,0:T(8,128)(2,1)S(1)}, u32[]{:S(2)}, u32[]{:S(2)}) collective-permute-start(bf16[256,2048]{1,0:T(8,128)(2,1)} %get-tuple-element.96), channel_id=1, source_target_pairs={{0,2},{1,3},{2,0},{3,1},{4,6},{5,7},{6,4},{7,5},{8,10},{9,11},{10,... | collective-permute-start | bytes 3145736 | tf_op jit(solution)/shard_map/ppermute | solution.py:172
  784.7 19.8 %collective-permute-start.53 = (f32[512]{0:T(512)S(1)}, f32[512]{0:T(512)S(1)}, u32[]{:S(2)}, u32[]{:S(2)}) collective-permute-start(f32[512]{0:T(512)S(1)} %bitcast.310), channel_id=1, source_target_pairs={{1,0},{0,1},{3,2},{2,3},{5,4},{4,5},{7,6},{6,7},{9,8},{8,9},{11,10... | collective-permute-start | bytes 6152 | tf_op jit(solution)/shard_map/ppermute | solution.py:519
  792.8 38.7 %collective-permute-start.52 = (f32[512]{0:T(512)S(1)}, f32[512]{0:T(512)S(1)}, u32[]{:S(2)}, u32[]{:S(2)}) collective-permute-start(f32[512]{0:T(512)S(1)} %bitcast.309), channel_id=1, source_target_pairs={{0,0},{3,1},{2,2},{1,3},{4,4},{7,5},{6,6},{5,7},{8,8},{11,9},{10,1... | collective-permute-start | bytes 6152 | tf_op jit(solution)/shard_map/ppermute | solution.py:519
  804.4 64.2 %collective-permute-start.13 = (bf16[256,2048]{1,0:T(8,128)(2,1)}, bf16[256,2048]{1,0:T(8,128)(2,1)S(1)}, u32[]{:S(2)}, u32[]{:S(2)}) collective-permute-start(bf16[256,2048]{1,0:T(8,128)(2,1)} %get-tuple-element.94), channel_id=1, source_target_pairs={{0,1},{1,2},{2,3},{3,0},{4,5},{5,6},{6,7},{7,4},{8,9},{9,10},{10,1... | collective-permute-start | bytes 3145736 | tf_op jit(solution)/shard_map/ppermute | solution.py:172
  831.4 17.6 %collective-permute-start.45 = (bf16[3,128,1024]{2,1,0:T(8,128)(2,1)S(1)}, bf16[3,128,1024]{2,1,0:T(8,128)(2,1)S(1)}, u32[]{:S(2)}, u32[]{:S(2)}) collective-permute-start(bf16[3,128,1024]{2,1,0:T(8,128)(2,1)S(1)} %pad_maximum_fusion.4.refs_0_), channel_id=1, source_target_pairs={{0,8},{4,12},{8,0},{12,4},{16,24},{20,28},{24,16},{28,20},{1,9},{5... | collective-permute-start | bytes 2359304 | tf_op jit(solution)/shard_map/ppermute | solution.py:247
  831.8 21.5 %collective-permute-start.46 = (bf16[3,128,1024]{2,1,0:T(8,128)(2,1)S(1)}, bf16[3,128,1024]{2,1,0:T(8,128)(2,1)S(1)}, u32[]{:S(2)}, u32[]{:S(2)}) collective-permute-start(bf16[3,128,1024]{2,1,0:T(8,128)(2,1)S(1)} %pad_maximum_fusion.4.refs_0_), channel_id=1, source_target_pairs={{0,16},{4,20},{8,24},{12,28},{16,0},{20,4},{24,8},{28,12},{1,17},{... | collective-permute-start | bytes 2359304 | tf_op jit(solution)/shard_map/ppermute | solution.py:247
  832.9 35.7 %collective-permute-start.47 = (bf16[3,128,1024]{2,1,0:T(8,128)(2,1)S(1)}, bf16[3,128,1024]{2,1,0:T(8,128)(2,1)S(1)}, u32[]{:S(2)}, u32[]{:S(2)}) collective-permute-start(bf16[3,128,1024]{2,1,0:T(8,128)(2,1)S(1)} %pad_maximum_fusion.4.refs_0_), channel_id=1, source_target_pairs={{0,24},{4,28},{8,16},{12,20},{16,8},{20,12},{24,0},{28,4},{1,25},{... | collective-permute-start | bytes 2359304 | tf_op jit(solution)/shard_map/ppermute | solution.py:247
  838.4 36.3 %collective-permute-start.48 = (bf16[3,128,1024]{2,1,0:T(8,128)(2,1)S(1)}, bf16[3,128,1024]{2,1,0:T(8,128)(2,1)S(1)}, u32[]{:S(2)}, u32[]{:S(2)}) collective-permute-start(bf16[3,128,1024]{2,1,0:T(8,128)(2,1)S(1)} %pad_maximum_fusion.4.refs_0_), channel_id=1, source_target_pairs={{0,4},{4,0},{8,12},{12,8},{16,20},{20,16},{24,28},{28,24},{1,5},{5... | collective-permute-start | bytes 2359304 | tf_op jit(solution)/shard_map/ppermute | solution.py:247
  849.0 25.6 %collective-permute-start.49 = (bf16[3,128,1024]{2,1,0:T(8,128)(2,1)S(1)}, bf16[3,128,1024]{2,1,0:T(8,128)(2,1)S(1)}, u32[]{:S(2)}, u32[]{:S(2)}) collective-permute-start(bf16[3,128,1024]{2,1,0:T(8,128)(2,1)S(1)} %collective-permute-done.45.refs_1_), channel_id=1, source_target_pairs={{0,4},{4,0},{8,12},{12,8},{16,20},{20,16},{24,28},{28,24},{1,5},{5... | collective-permute-start | bytes 2359304 | tf_op jit(solution)/shard_map/ppermute | solution.py:247
  853.3 21.3 %collective-permute-start.50 = (bf16[3,128,1024]{2,1,0:T(8,128)(2,1)S(1)}, bf16[3,128,1024]{2,1,0:T(8,128)(2,1)S(1)}, u32[]{:S(2)}, u32[]{:S(2)}) collective-permute-start(bf16[3,128,1024]{2,1,0:T(8,128)(2,1)S(1)} %collective-permute-done.46.refs_2_), channel_id=1, source_target_pairs={{0,4},{4,0},{8,12},{12,8},{16,20},{20,16},{24,28},{28,24},{1,5},{5... | collective-permute-start | bytes 2359304 | tf_op jit(solution)/shard_map/ppermute | solution.py:247
  (57 other events, 1686.3 us)
Sparse Core Ops, SparseCore 0:
  27.4 46.5 all-gather.5
  76.5 54.2 all-gather.7
  132.7 27.7 all-gather.9
  347.1 41.5 reduce-scatter.1
  400.8 56.1 all-gather.11
  525.2 102.2 all-gather.13

commit v4 on v3

--- a/solution.py
+++ b/solution.py
@@ -462,42 +462,44 @@
     exp_total = reduce_chips(exp_sum.reshape(blocks, part, width // 2), rep, reps)
 
     grads_4, exp_sum = hold(grads_3, exp_sum)
-    g_out_1 = tn(grads_4, attended).astype(BF16)
-    g_out = lax.psum_scatter(
-        g_out_1.reshape(count, part, part), "rep", scatter_dimension=1, tiled=True
-    )
-    d_att, g_out_1 = hold(d_att, g_out_1)
+    g_out = tn(grads_4, attended).astype(BF16)
+    g_out_1 = lax.psum_scatter(
+        g_out.reshape(count, part, part), "rep", scatter_dimension=1, tiled=True
+    )
+    d_up_2, g_out = hold(d_up_1, g_out)
+    d_normed = nn(d_up_2, expand_weight)
+    g_shr = shr_total()
+    d_att, d_normed, g_shr = hold(d_att, d_normed, g_shr)
+    g_shr = swap_blocks(g_shr, 0, count, me)
+    g_shr = lax.all_gather(g_shr, "rep", axis=0)
     d_q, d_k, d_v = attend_back(q_low, k_low, v_low, d_att, lse, tables, seg_col, seg_row, blk)
     d_mixed = jnp.concatenate([d_q, d_k, d_v], 1)
     in_send = low_term(d_mixed, normed_other)
     in_arrived = flip(in_send, 1, reps)
-    g_shr = shr_total()
-    d_mixed_1, in_send, g_shr = hold(d_mixed, in_send, g_shr)
-    g_shr = swap_blocks(g_shr, 0, count, me)
-    g_shr = lax.all_gather(g_shr, "rep", axis=0)
-    g_out = jnp.transpose(swap_blocks(g_out, 0, count, me), (1, 0, 2)).reshape(sub, width)
+    d_mixed_1, in_send = hold(d_mixed, in_send)
+    b_out = jnp.sum(lax.dynamic_slice_in_dim(grads_3, me * part, part, 1), 0, dtype=F32)
+    b_exp = jnp.sum(d_up_2, 0, dtype=F32)
+    b_in = jnp.sum(d_mixed_1, 0, dtype=F32)
+    d_mixed_1, b_in = hold(d_mixed_1, b_in)
     in_sum = low_term(d_mixed_1, normed_mine, in_arrived)
     in_total = reduce_chips(in_sum.reshape(3, part, width // 2), rep, reps)
-    d_mixed_2, d_up_2, in_sum = hold(d_mixed_1, d_up_1, in_sum)
-    b_out = jnp.sum(lax.dynamic_slice_in_dim(grads_4, me * part, part, 1), 0, dtype=F32)
-    b_exp = jnp.sum(d_up_2, 0, dtype=F32)
-    b_in = jnp.sum(d_mixed_2, 0, dtype=F32)
+    d_mixed_2, in_sum = hold(d_mixed_1, in_sum)
     g_exp = exp_total()
     exp_pieces = spread(g_exp, reps)
-    d_mixed_2, b_in, g_exp = hold(d_mixed_2, b_in, g_exp)
-    d_normed = nn(d_up_2, expand_weight) + nn(d_mixed_2, in_w)
+    d_mixed_2, g_exp, g_out_1 = hold(d_mixed_2, g_exp, g_out_1)
+    d_normed = d_normed + nn(d_mixed_2, in_w)
     both = jnp.stack([jnp.sum(d_normed * normed.astype(F32), 0), jnp.sum(d_normed, 0)])
     d_normed = d_normed.astype(BF16)
     d_normed = scatter_row(d_normed, count, me)
     kinds = pick(jnp.asarray(kind_of), me)
     g_in = in_total()
-    both, g_in = hold(both, g_in)
     g_in = jnp.stack([lax.ppermute(pick(g_in, kinds[j]), "shard", back[j]) for j in range(3)])
     in_pieces = spread(g_in, reps)
 
     both = jnp.sum(swap_blocks(both.reshape(2, count, part), 1, count, me), 1)
     sums = jnp.concatenate([both[0], both[1], b_out, b_exp, b_in])
 
+    g_out = jnp.transpose(swap_blocks(g_out_1, 0, count, me), (1, 0, 2)).reshape(sub, width)
     g_out = lax.all_gather(g_out, "rep", axis=0, tiled=True).astype(F32)
     g_shr = lay_out(g_shr, True)
     g_exp = assemble(exp_pieces, rep, False)

time: 916 us -> 885 us (0.966)
  the two profiles are of different devices: /device:TPU:25 before, /device:TPU:0 now
where the time goes in v4:
time: 885 us; the launch traced here: 875 us
  waiting for transfers between devices  371 us (42%)
  matrix products  152 us (17%)
  starting transfers between devices  134 us (15%)
  Pallas kernels  77.6 us (9%)
  local copies, waits for them, and re-layouts  69.5 us (8%)
  other arithmetic  43.7 us (5%)
  between operations  27.5 us (3%)
    ppermute x29, waiting for transfers between devices, flip(): return lax.ppermute(x, 'rep', [(i, i ^ mask) for i in range(reps)])  193 us
    ppermute x30, waiting for transfers between devices, shift(): lax.ppermute(x, 'shard', [(i, (i + offset) % count) for i in range(count)])  98.5 us
    ppermute x30, starting transfers between devices, shift(): lax.ppermute(x, 'shard', [(i, (i + offset) % count) for i in range(count)])  94.4 us
    ppermute x3, waiting for transfers between devices, local(): lax.ppermute(pick(b_in, kinds[j]), 'shard', back[j])  76 us
    dot_general x4, matrix products, nt(): lax.dot_general(a, b, (((1,), (1,)), ((), ())), preferred_element_type=F32)  52.1 us
    dot_general x7, matrix products, tn(): lax.dot_general(a, b, (((0,), (0,)), ((), ())), preferred_element_type=F32)  50.5 us
    dot_general x4, matrix products, nn(): lax.dot_general(a, b, (((1,), (0,)), ((), ())), preferred_element_type=F32)  49.1 us
    pallas_call x1, Pallas kernels, attend_back(): pl.pallas_call(functools.partial(attend_back_kernel, blk), grid=(pairs,),...  25.6 us
  transfers between devices with their start and end apart: 74, of which 31 were waited for; matrix products, arithmetic and copies ran while one was open for 21% of the time, Pallas kernels for 5%

profile of v4, /device:TPU:0, one launch (start us, length us, event | category | flops | bytes accessed | tf_op | source)
XLA Modules:
  0.0 874.8 jit_solution(1198077607692699548)
XLA Ops:
  8.6 6.0 collective-permute-start.9
  23.1 3.3 collective-permute-done.8
  43.1 6.7 collective-permute-done.10
  50.8 12.2 %collective-permute-done.11 = bf16[64,2560]{1,0:T(8,128)(2,1)} collective-permute-done((bf16[64,2560]{1,0:T(8,128)(2,1)}, bf16[64,2560]{1,0:T(8,128)(2,1)}, u32[]{:S(2)}, u32[]{:S(2)}) %collective-permute-start.11) | collective-permute-done | bytes 327712 | tf_op jit(solution)/shard_map/ppermute | solution.py:172
  67.2 6.5 collective-permute-start
  76.3 3.6 collective-permute-start.17
  84.9 3.2 fusion.49
  91.4 3.8 collective-permute-start.4
  99.1 5.0 collective-permute-done.16
  105.2 18.2 %collective-permute-start.18 = (bf16[128,2048]{1,0:T(8,128)(2,1)S(1)}, bf16[128,2048]{1,0:T(8,128)(2,1)S(1)}, u32[]{:S(2)}, u32[]{:S(2)}) collective-permute-start(bf16[128,2048]{1,0:T(8,128)(2,1)S(1)} %slice.197), channel_id=1, source_target_pairs={{0,1},{1,2},{2,3},{3,0},{4,5},{5,6},{6,7},{7,4},{8,9},{9,10},{10,1... | collective-permute-start | bytes 1572872 | tf_op jit(solution)/shard_map/ppermute | solution.py:172
  123.4 2.9 collective-permute-done.17
  133.7 15.3 %collective-permute-done.3 = bf16[256,2048]{1,0:T(8,128)(2,1)} collective-permute-done((bf16[256,2048]{1,0:T(8,128)(2,1)}, bf16[256,2048]{1,0:T(8,128)(2,1)}, u32[]{:S(2)}, u32[]{:S(2)}) %collective-permute-start.3) | collective-permute-done | bytes 1048608 | tf_op jit(solution)/shard_map/ppermute | solution.py:172
  150.1 18.2 %collective-permute-start.5 = (bf16[128,2048]{1,0:T(8,128)(2,1)S(1)}, bf16[128,2048]{1,0:T(8,128)(2,1)S(1)}, u32[]{:S(2)}, u32[]{:S(2)}) collective-permute-start(bf16[128,2048]{1,0:T(8,128)(2,1)S(1)} %slice.190), channel_id=1, source_target_pairs={{0,1},{1,2},{2,3},{3,0},{4,5},{5,6},{6,7},{7,4},{8,9},{9,10},{10,1... | collective-permute-start | bytes 1572872 | tf_op jit(solution)/shard_map/ppermute | solution.py:172
  176.5 6.2 collective-permute-done.18
  183.5 9.9 %collective-permute-done.19 = bf16[128,2048]{1,0:T(8,128)(2,1)S(1)} collective-permute-done((bf16[128,2048]{1,0:T(8,128)(2,1)S(1)}, bf16[128,2048]{1,0:T(8,128)(2,1)S(1)}, u32[]{:S(2)}, u32[]{:S(2)}) %collective-permute-start.19) | collective-permute-done | bytes 524320 | tf_op jit(solution)/shard_map/ppermute | solution.py:172
  194.3 10.9 %collective-permute-done.5 = bf16[128,2048]{1,0:T(8,128)(2,1)S(1)} collective-permute-done((bf16[128,2048]{1,0:T(8,128)(2,1)S(1)}, bf16[128,2048]{1,0:T(8,128)(2,1)S(1)}, u32[]{:S(2)}, u32[]{:S(2)}) %collective-permute-start.5) | collective-permute-done | bytes 524320 | tf_op jit(solution)/shard_map/ppermute | solution.py:172
  205.3 7.8 collective-permute-done.6
  213.1 17.1 %multiply_convert_fusion.1 = (bf16[1024,2048]{1,0:T(8,128)(2,1)}, f32[1024,2048]{1,0:T(8,128)}) fusion(f32[2048]{0:T(1024)S(1)} %convert_element_type.258, bf16[1024,2048]{1,0:T(8,128)(2,1)S(1)} %bitcast.270, bf16[2048,2048]{1,0:T(8,128)(2,1)} %param.24), kind=kOutput, calls=%fused_computation.10 | convolution fusion | flops 8610906112 | bytes 25174016 | tf_op jit(solution)/shard_map/dot_general | solution.py:22
  230.2 11.7 %convolution_add_fusion.q_ref.k_ref.v_ref = f32[1024,1536]{1,0:T(8,128)} fusion(bf16[1024,2048]{1,0:T(8,128)(2,1)} %bitcast.271, bf16[1536,2048]{1,0:T(8,128)(2,1)} %bitcast.312, f32[1536]{0:T(1024)S(1)} %reshape.282), kind=kOutput, calls=%fused_computation.14 | convolution fusion | flops 6444023808 | bytes 16783360 | tf_op jit(solution)/shard_map/dot_general | solution.py:22
  241.9 22.5 %attend.1 = (bf16[1024,512]{1,0:T(8,128)(2,1)}, bf16[1024,512]{1,0:T(8,128)(2,1)}, bf16[1024,512]{1,0:T(8,128)(2,1)}, bf16[1024,512]{1,0:T(8,128)(2,1)}, f32[4,2,1024]{2,1,0:T(2,128)}) custom-call(f32[1024,1536]{1,0:T(8,128)} %convolution_add_fusion.q_ref.k_ref.v_ref, f32[1024,1536]{1,0:T(8,128)} %convolution_add_fusion.q_ref.k_ref.v_ref, ...), custom_call_target="tpu_custom_call" | custom-call | tf_op jit(solution)/shard_map/attend/pallas_call | solution.py:92
  264.5 14.8 %fusion.72 = f32[1024,2048]{1,0:T(8,128)} fusion(bf16[1024,2048]{1,0:T(8,128)(2,1)} %get-tuple-element.46, bf16[2048,2048]{1,0:T(8,128)(2,1)} %bitcast.310), kind=kOutput, calls=%fused_computation.212 | convolution fusion | flops 8589934592 | bytes 20971520 | tf_op jit(solution)/shard_map/dot_general | solution.py:22
  279.3 8.5 add_convert_fusion.3
  287.8 8.4 convolution_convert_fusion.2
  296.2 18.1 %multiply_convert_fusion = bf16[1024,2048]{1,0:T(8,128)(2,1)S(1)} fusion(f32[1024,2048]{1,0:T(8,128)} %get-tuple-element.143, f32[2048]{0:T(1024)S(1)} %convert_element_type.258, bf16[1024,2048]{1,0:T(8,128)(2,1)} %bitcast.35, bf16[2048,2048]{1,0:T(8,128)(2,1)} %bitcast.311), kind=kOutput, calls=%fused_computation.7 | convolution fusion | flops 8633974784 | bytes 25174016 | tf_op jit(solution)/shard_map/dot_general | solution.py:26
  314.3 10.5 %add_convert_fusion.1 = bf16[2048,1024]{1,0:T(8,128)(2,1)} fusion(bf16[2048,1024]{1,0:T(8,128)(2,1)} %collective-permute-done.20, bf16[1024,2048]{1,0:T(8,128)(2,1)} %bitcast.35, bf16[1024,2048]{1,0:T(8,128)(2,1)S(1)} %copy-done.47, s32[]{:T(128)S(6)} %select_n.296), kind=kOutput, calls=%fused_computation.6 | convolution fusion | flops 4301258752 | bytes 14680068 | tf_op jit(solution)/shard_map/dot_general | solution.py:30
  324.8 6.3 convolution_convert_fusion.1
  331.6 3.5 dynamic-slice_bitcast_fusion.5
  338.6 6.3 convolution_convert_fusion.4.g_ref
  344.9 17.4 %collective-permute-done.24 = bf16[4,128,1024]{2,1,0:T(8,128)(2,1)S(1)} collective-permute-done((bf16[4,128,1024]{2,1,0:T(8,128)(2,1)}, bf16[4,128,1024]{2,1,0:T(8,128)(2,1)S(1)}, u32[]{:S(2)}, u32[]{:S(2)}) %collective-permute-start.24) | collective-permute-done | bytes 1048608 | tf_op jit(solution)/shard_map/ppermute | solution.py:247
  362.3 21.5 %collective-permute-done.23 = bf16[4,128,1024]{2,1,0:T(8,128)(2,1)S(1)} collective-permute-done((bf16[4,128,1024]{2,1,0:T(8,128)(2,1)}, bf16[4,128,1024]{2,1,0:T(8,128)(2,1)S(1)}, u32[]{:S(2)}, u32[]{:S(2)}) %collective-permute-start.23) | collective-permute-done | bytes 1048608 | tf_op jit(solution)/shard_map/ppermute | solution.py:247
  384.8 2.8 fusion.29
  387.6 8.1 add_convert_fusion
  395.7 5.9 convolution_convert_fusion.3
  401.6 11.1 %fusion.73 = f32[1024,2048]{1,0:T(8,128)} fusion(bf16[1024,2048]{1,0:T(8,128)(2,1)S(1)} %copy-done.11, bf16[2048,2048]{1,0:T(8,128)(2,1)S(1)} %bitcast.309), kind=kOutput, calls=%fused_computation.213 | convolution fusion | flops 8589934592 | bytes 20971520 | tf_op jit(solution)/shard_map/dot_general | solution.py:26
  412.7 25.6 %attend_back.1 = (bf16[1024,512]{1,0:T(8,128)(2,1)}, bf16[1024,512]{1,0:T(8,128)(2,1)}, bf16[1024,512]{1,0:T(8,128)(2,1)}) custom-call(bf16[1024,512]{1,0:T(8,128)(2,1)} %get-tuple-element.59.q_ref, bf16[1024,512]{1,0:T(8,128)(2,1)} %get-tuple-element.60.k_ref, bf16[1024,512]{1,0:T(8,128)(2,1)} %get-tuple-element.61.v_ref, ...), custom_call_target="tpu_custom_call" | custom-call | tf_op jit(solution)/shard_map/attend_back/pallas_call | solution.py:152
  441.1 5.0 convolution_convert_fusion
  452.0 2.9 convert_reduce_fusion.1
  455.0 26.2 %collective-permute-done.28 = bf16[4,128,1024]{2,1,0:T(8,128)(2,1)S(1)} collective-permute-done((bf16[4,128,1024]{2,1,0:T(8,128)(2,1)S(1)}, bf16[4,128,1024]{2,1,0:T(8,128)(2,1)S(1)}, u32[]{:S(2)}, u32[]{:S(2)}) %collective-permute-start.28) | collective-permute-done | bytes 1048608 | tf_op jit(solution)/shard_map/ppermute | solution.py:247
  481.1 24.7 %collective-permute-done.27 = bf16[4,128,1024]{2,1,0:T(8,128)(2,1)S(1)} collective-permute-done((bf16[4,128,1024]{2,1,0:T(8,128)(2,1)S(1)}, bf16[4,128,1024]{2,1,0:T(8,128)(2,1)S(1)}, u32[]{:S(2)}, u32[]{:S(2)}) %collective-permute-start.27) | collective-permute-done | bytes 1048608 | tf_op jit(solution)/shard_map/ppermute | solution.py:247
  508.1 6.3 add_convert_fusion.4
  533.2 7.0 collective-permute-done.65
  540.2 8.8 %collective-permute-done.66 = bf16[128,1024]{1,0:T(8,128)(2,1)S(1)} collective-permute-done((bf16[128,1024]{1,0:T(8,128)(2,1)S(1)}, bf16[128,1024]{1,0:T(8,128)(2,1)S(1)}, u32[]{:S(2)}, u32[]{:S(2)}) %collective-permute-start.66) | collective-permute-done | bytes 262176 | tf_op jit(solution)/shard_map/ppermute | solution.py:172
  550.1 3.8 dynamic-slice_bitcast_fusion.8
  553.9 6.6 collective-permute-start.15
  561.9 13.6 %fusion.68 = (f32[2048]{0:T(1024)S(1)}, f32[2048]{0:T(1024)S(1)}, bf16[1024,2048]{1,0:T(8,128)(2,1)}) fusion(bf16[4,256,2048]{2,1,0:T(8,128)(2,1)S(1)} %copy-done.18, f32[1024,2048]{1,0:T(8,128)} %fusion.73, bf16[1024,1536]{1,0:T(8,128)(2,1)S(1)} %copy-done.7, bf16[1536,2048]{1,0:T(8,128)(2,1)} %bitcast.313), kind=kOutput, calls=%fused_computation.208 | convolution fusion | flops 6455029760 | bytes 26230784 | tf_op jit(solution)/shard_map/dot_general | solution.py:26
  576.4 3.2 collective-permute-start.35
  579.6 2.8 convert_reduce_fusion
  587.9 3.2 dynamic-slice_bitcast_fusion.16
  591.1 37.3 %collective-permute-done.58.refs_1_ = bf16[4,128,1024]{2,1,0:T(8,128)(2,1)S(1)} collective-permute-done((bf16[4,128,1024]{2,1,0:T(8,128)(2,1)S(1)}, bf16[4,128,1024]{2,1,0:T(8,128)(2,1)S(1)}, u32[]{:S(2)}, u32[]{:S(2)}) %collective-permute-start.58) | collective-permute-done | bytes 1048608 | tf_op jit(solution)/shard_map/ppermute | solution.py:247
  628.5 3.8 collective-permute-start.31
  632.3 19.4 %collective-permute-done.59.refs_2_ = bf16[4,128,1024]{2,1,0:T(8,128)(2,1)S(1)} collective-permute-done((bf16[4,128,1024]{2,1,0:T(8,128)(2,1)S(1)}, bf16[4,128,1024]{2,1,0:T(8,128)(2,1)S(1)}, u32[]{:S(2)}, u32[]{:S(2)}) %collective-permute-start.59) | collective-permute-done | bytes 1048608 | tf_op jit(solution)/shard_map/ppermute | solution.py:247
  674.1 12.9 %collective-permute-done.40 = bf16[3,128,1024]{2,1,0:T(8,128)(2,1)S(1)} collective-permute-done((bf16[3,128,1024]{2,1,0:T(8,128)(2,1)}, bf16[3,128,1024]{2,1,0:T(8,128)(2,1)S(1)}, u32[]{:S(2)}, u32[]{:S(2)}) %collective-permute-start.40) | collective-permute-done | bytes 786464 | tf_op jit(solution)/shard_map/ppermute | solution.py:247
  687.6 6.9 collective-permute-start.30
  700.3 2.8 collective-permute-start.44
  703.2 3.9 collective-permute-start.54
  707.2 67.4 %collective-permute-done.54 = f32[512]{0:T(512)S(1)} collective-permute-done((f32[512]{0:T(512)S(1)}, f32[512]{0:T(512)S(1)}, u32[]{:S(2)}, u32[]{:S(2)}) %collective-permute-start.54) | collective-permute-done | bytes 2080 | tf_op jit(solution)/shard_map/ppermute | solution.py:521
  776.9 10.9 %assemble.3 = f32[4,4,128,2048]{3,2,1,0:T(8,128)} custom-call(s32[2]{0:T(128)S(1)} %pad_add_fusion.place_ref, bf16[4,128,1024]{2,1,0:T(8,128)(2,1)S(1)} %fusion.26.refs_0_, bf16[4,128,1024]{2,1,0:T(8,128)(2,1)S(1)} %collective-permute-done.58.refs_1_, bf16[4,128,1024]{2,1,0:T(8,128)(2,1)S(1)} %collective-permute-done.59.refs_2_, ...), custom_call_target="tpu_custom_call" | custom-call | tf_op jit(solution)/shard_map/assemble/pallas_call | solution.py:295
  789.9 8.6 collective-permute-done.53
  809.4 12.1 %collective-permute-done.45.refs_1_ = bf16[3,128,1024]{2,1,0:T(8,128)(2,1)S(1)} collective-permute-done((bf16[3,128,1024]{2,1,0:T(8,128)(2,1)S(1)}, bf16[3,128,1024]{2,1,0:T(8,128)(2,1)S(1)}, u32[]{:S(2)}, u32[]{:S(2)}) %collective-permute-start.45) | collective-permute-done | bytes 786464 | tf_op jit(solution)/shard_map/ppermute | solution.py:247
  821.5 13.9 %collective-permute-done.46.refs_2_ = bf16[3,128,1024]{2,1,0:T(8,128)(2,1)S(1)} collective-permute-done((bf16[3,128,1024]{2,1,0:T(8,128)(2,1)S(1)}, bf16[3,128,1024]{2,1,0:T(8,128)(2,1)S(1)}, u32[]{:S(2)}, u32[]{:S(2)}) %collective-permute-start.46) | collective-permute-done | bytes 786464 | tf_op jit(solution)/shard_map/ppermute | solution.py:247
  837.3 6.3 fusion.15
  844.5 8.1 assemble.2
  852.6 4.1 convert_element_type.320
  856.7 10.5 %place.1 = f32[1,4,128,8192]{3,2,1,0:T(8,128)} custom-call(bf16[8,4,128,1024]{3,2,1,0:T(8,128)(2,1)} %all-gather.14.cloned.1.call-done.x_ref), custom_call_target="tpu_custom_call" | custom-call | tf_op jit(solution)/shard_map/place/pallas_call | solution.py:323
  (364 shorter events, 144.5 us)
Async XLA Ops:
  7.2 223.0 %all-gather.6.cloned.1.call-start = ((), (), s32[]{:S(2)}) async-start(), calls=%async_computation.1 | async-start | bytes 7077888 | tf_op jit(solution)/shard_map/all_gather | solution.py:386
  8.6 14.5 %collective-permute-start.9 = (bf16[64,2048]{1,0:T(8,128)(2,1)S(1)}, bf16[64,2048]{1,0:T(8,128)(2,1)S(1)}, u32[]{:S(2)}, u32[]{:S(2)}) collective-permute-start(bf16[64,2048]{1,0:T(8,128)(2,1)S(1)} %get-tuple-element.83), channel_id=1, source_target_pairs={{0,2},{1,1},{2,0},{3,3},{4,6},{5,5},{6,4},{7,7},{8,10},{9,9},{10,8... | collective-permute-start | bytes 786440 | tf_op jit(solution)/shard_map/ppermute | solution.py:383
  14.5 11.9 %collective-permute-start.8 = (bf16[64,2048]{1,0:T(8,128)(2,1)S(1)}, bf16[64,2048]{1,0:T(8,128)(2,1)S(1)}, u32[]{:S(2)}, u32[]{:S(2)}) collective-permute-start(bf16[64,2048]{1,0:T(8,128)(2,1)S(1)} %get-tuple-element.82), channel_id=1, source_target_pairs={{0,1},{1,0},{2,3},{3,2},{4,5},{5,4},{6,7},{7,6},{8,9},{9,8},{10,11... | collective-permute-start | bytes 786440 | tf_op jit(solution)/shard_map/ppermute | solution.py:383
  14.6 11.8 %collective-permute-start.7 = (bf16[64,2048]{1,0:T(8,128)(2,1)S(1)}, bf16[64,2048]{1,0:T(8,128)(2,1)}, u32[]{:S(2)}, u32[]{:S(2)}) collective-permute-start(bf16[64,2048]{1,0:T(8,128)(2,1)S(1)} %get-tuple-element.81), channel_id=1, source_target_pairs={{0,0},{1,3},{2,2},{3,1},{4,4},{5,7},{6,6},{7,5},{8,8},{9,11},{10,1... | collective-permute-start | bytes 786440 | tf_op jit(solution)/shard_map/ppermute | solution.py:383
  28.6 235.9 %all-gather.8.cloned.1.call-start = ((), (), s32[]{:S(2)}) async-start(), calls=%async_computation.2 | async-start | bytes 9437184 | tf_op jit(solution)/shard_map/all_gather | solution.py:395
  37.0 12.8 %collective-permute-start.10 = (bf16[64,2560]{1,0:T(8,128)(2,1)}, bf16[64,2560]{1,0:T(8,128)(2,1)}, u32[]{:S(2)}, u32[]{:S(2)}) collective-permute-start(bf16[64,2560]{1,0:T(8,128)(2,1)} %bitcast.255), channel_id=1, source_target_pairs={{0,1},{1,2},{2,3},{3,0},{4,5},{5,6},{6,7},{7,4},{8,9},{9,10},{10,1... | collective-permute-start | bytes 983048 | tf_op jit(solution)/shard_map/ppermute | solution.py:172
  39.7 23.3 %collective-permute-start.11 = (bf16[64,2560]{1,0:T(8,128)(2,1)}, bf16[64,2560]{1,0:T(8,128)(2,1)}, u32[]{:S(2)}, u32[]{:S(2)}) collective-permute-start(bf16[64,2560]{1,0:T(8,128)(2,1)} %bitcast.254), channel_id=1, source_target_pairs={{0,2},{1,3},{2,0},{3,1},{4,6},{5,7},{6,4},{7,5},{8,10},{9,11},{10,... | collective-permute-start | bytes 983048 | tf_op jit(solution)/shard_map/ppermute | solution.py:172
  42.8 21.2 %collective-permute-start.12 = (bf16[64,2560]{1,0:T(8,128)(2,1)}, bf16[64,2560]{1,0:T(8,128)(2,1)}, u32[]{:S(2)}, u32[]{:S(2)}) collective-permute-start(bf16[64,2560]{1,0:T(8,128)(2,1)} %bitcast.253), channel_id=1, source_target_pairs={{0,3},{1,0},{2,1},{3,2},{4,7},{5,4},{6,5},{7,6},{8,11},{9,8},{10,9... | collective-permute-start | bytes 983048 | tf_op jit(solution)/shard_map/ppermute | solution.py:172
  66.2 213.1 %all-gather.10.cloned.1.call-start = ((), (), s32[]{:S(2)}) async-start(), calls=%async_computation.3 | async-start | bytes 2359296 | tf_op jit(solution)/shard_map/all_gather | solution.py:396
  67.2 22.2 %collective-permute-start = (bf16[3584]{0:T(1024)(128)(2,1)S(1)}, bf16[3584]{0:T(1024)(128)(2,1)S(1)}, u32[]{:S(2)}, u32[]{:S(2)}) collective-permute-start(bf16[3584]{0:T(1024)(128)(2,1)S(1)} %constant_dynamic-update-slice_fusion.9), channel_id=1, source_target_pairs={{0,1},{1,2},{2,3},{3,0},{4,5},{5,6},{6,7},{7,4},{8,9},{9,10},{10,1... | collective-permute-start | bytes 21512 | tf_op jit(solution)/shard_map/ppermute | solution.py:172
  73.7 15.8 %collective-permute-start.1 = (bf16[3584]{0:T(1024)(128)(2,1)S(1)}, bf16[3584]{0:T(1024)(128)(2,1)S(1)}, u32[]{:S(2)}, u32[]{:S(2)}) collective-permute-start(bf16[3584]{0:T(1024)(128)(2,1)S(1)} %constant_dynamic-update-slice_fusion.9), channel_id=1, source_target_pairs={{0,2},{1,3},{2,0},{3,1},{4,6},{5,7},{6,4},{7,5},{8,10},{9,11},{10,... | collective-permute-start | bytes 21512 | tf_op jit(solution)/shard_map/ppermute | solution.py:172
  74.3 15.4 %collective-permute-start.2 = (bf16[3584]{0:T(1024)(128)(2,1)S(1)}, bf16[3584]{0:T(1024)(128)(2,1)S(1)}, u32[]{:S(2)}, u32[]{:S(2)}) collective-permute-start(bf16[3584]{0:T(1024)(128)(2,1)S(1)} %constant_dynamic-update-slice_fusion.9), channel_id=1, source_target_pairs={{0,3},{1,0},{2,1},{3,2},{4,7},{5,4},{6,5},{7,6},{8,11},{9,8},{10,9... | collective-permute-start | bytes 21512 | tf_op jit(solution)/shard_map/ppermute | solution.py:172
  76.1 27.9 %collective-permute-start.16 = (bf16[256,2048]{1,0:T(8,128)(2,1)S(1)}, bf16[256,2048]{1,0:T(8,128)(2,1)}, u32[]{:S(2)}, u32[]{:S(2)}) collective-permute-start(bf16[256,2048]{1,0:T(8,128)(2,1)S(1)} %bitcast.266), channel_id=1, source_target_pairs={{0,1},{1,2},{2,3},{3,0},{4,5},{5,6},{6,7},{7,4},{8,9},{9,10},{10,1... | collective-permute-start | bytes 3145736 | tf_op jit(solution)/shard_map/ppermute | solution.py:172
  76.3 49.9 %collective-permute-start.17 = (bf16[256,2048]{1,0:T(8,128)(2,1)S(1)}, bf16[256,2048]{1,0:T(8,128)(2,1)}, u32[]{:S(2)}, u32[]{:S(2)}) collective-permute-start(bf16[256,2048]{1,0:T(8,128)(2,1)S(1)} %bitcast.267), channel_id=1, source_target_pairs={{0,3},{1,0},{2,1},{3,2},{4,7},{5,4},{6,5},{7,6},{8,11},{9,8},{10,9... | collective-permute-start | bytes 3145736 | tf_op jit(solution)/shard_map/ppermute | solution.py:172
  91.4 57.7 %collective-permute-start.3 = (bf16[256,2048]{1,0:T(8,128)(2,1)}, bf16[256,2048]{1,0:T(8,128)(2,1)}, u32[]{:S(2)}, u32[]{:S(2)}) collective-permute-start(bf16[256,2048]{1,0:T(8,128)(2,1)} %fusion.10), channel_id=1, source_target_pairs={{0,1},{1,2},{2,3},{3,0},{4,5},{5,6},{6,7},{7,4},{8,9},{9,10},{10,1... | collective-permute-start | bytes 3145736 | tf_op jit(solution)/shard_map/ppermute | solution.py:172
  91.4 79.8 %collective-permute-start.4 = (bf16[256,2048]{1,0:T(8,128)(2,1)}, bf16[256,2048]{1,0:T(8,128)(2,1)}, u32[]{:S(2)}, u32[]{:S(2)}) collective-permute-start(bf16[256,2048]{1,0:T(8,128)(2,1)} %fusion.10), channel_id=1, source_target_pairs={{0,3},{1,0},{2,1},{3,2},{4,7},{5,4},{6,5},{7,6},{8,11},{9,8},{10,9... | collective-permute-start | bytes 3145736 | tf_op jit(solution)/shard_map/ppermute | solution.py:172
  99.0 415.4 %reduce-scatter.2.cloned.1.call-start = ((), (), s32[]{:S(2)}) async-start(), calls=%async_computation.4 | async-start | bytes 2359296 | tf_op jit(solution)/shard_map/reduce_scatter | solution.py:466
  105.2 77.5 %collective-permute-start.18 = (bf16[128,2048]{1,0:T(8,128)(2,1)S(1)}, bf16[128,2048]{1,0:T(8,128)(2,1)S(1)}, u32[]{:S(2)}, u32[]{:S(2)}) collective-permute-start(bf16[128,2048]{1,0:T(8,128)(2,1)S(1)} %slice.197), channel_id=1, source_target_pairs={{0,1},{1,2},{2,3},{3,0},{4,5},{5,6},{6,7},{7,4},{8,9},{9,10},{10,1... | collective-permute-start | bytes 1572872 | tf_op jit(solution)/shard_map/ppermute | solution.py:172
  127.3 66.1 %collective-permute-start.19 = (bf16[128,2048]{1,0:T(8,128)(2,1)S(1)}, bf16[128,2048]{1,0:T(8,128)(2,1)S(1)}, u32[]{:S(2)}, u32[]{:S(2)}) collective-permute-start(bf16[128,2048]{1,0:T(8,128)(2,1)S(1)} %slice.198), channel_id=1, source_target_pairs={{0,3},{1,0},{2,1},{3,2},{4,7},{5,4},{6,5},{7,6},{8,11},{9,8},{10,9... | collective-permute-start | bytes 1572872 | tf_op jit(solution)/shard_map/ppermute | solution.py:172
  150.1 55.1 %collective-permute-start.5 = (bf16[128,2048]{1,0:T(8,128)(2,1)S(1)}, bf16[128,2048]{1,0:T(8,128)(2,1)S(1)}, u32[]{:S(2)}, u32[]{:S(2)}) collective-permute-start(bf16[128,2048]{1,0:T(8,128)(2,1)S(1)} %slice.190), channel_id=1, source_target_pairs={{0,1},{1,2},{2,3},{3,0},{4,5},{5,6},{6,7},{7,4},{8,9},{9,10},{10,1... | collective-permute-start | bytes 1572872 | tf_op jit(solution)/shard_map/ppermute | solution.py:172
  172.2 40.8 %collective-permute-start.6 = (bf16[128,2048]{1,0:T(8,128)(2,1)S(1)}, bf16[128,2048]{1,0:T(8,128)(2,1)S(1)}, u32[]{:S(2)}, u32[]{:S(2)}) collective-permute-start(bf16[128,2048]{1,0:T(8,128)(2,1)S(1)} %slice.191), channel_id=1, source_target_pairs={{0,3},{1,0},{2,1},{3,2},{4,7},{5,4},{6,5},{7,6},{8,11},{9,8},{10,9... | collective-permute-start | bytes 1572872 | tf_op jit(solution)/shard_map/ppermute | solution.py:172
  296.1 18.1 %collective-permute-start.20 = (bf16[2048,1024]{1,0:T(8,128)(2,1)}, bf16[2048,1024]{1,0:T(8,128)(2,1)}, u32[]{:S(2)}, u32[]{:S(2)}) collective-permute-start(bf16[2048,1024]{1,0:T(8,128)(2,1)} %convolution_convert_fusion.2), channel_id=1, source_target_pairs={{0,4},{4,0},{8,12},{12,8},{16,20},{20,16},{24,28},{28,24},{1,5},{5... | collective-permute-start | bytes 12582920 | tf_op jit(solution)/shard_map/ppermute | solution.py:247
  331.1 56.5 %collective-permute-start.21 = (bf16[2048,1024]{1,0:T(8,128)(2,1)}, bf16[2048,1024]{1,0:T(8,128)(2,1)}, u32[]{:S(2)}, u32[]{:S(2)}) collective-permute-start(bf16[2048,1024]{1,0:T(8,128)(2,1)} %convolution_convert_fusion.1), channel_id=1, source_target_pairs={{0,4},{4,0},{8,12},{12,8},{16,20},{20,16},{24,28},{28,24},{1,5},{5... | collective-permute-start | bytes 12582920 | tf_op jit(solution)/shard_map/ppermute | solution.py:247
  335.1 27.2 %collective-permute-start.24 = (bf16[4,128,1024]{2,1,0:T(8,128)(2,1)}, bf16[4,128,1024]{2,1,0:T(8,128)(2,1)S(1)}, u32[]{:S(2)}, u32[]{:S(2)}) collective-permute-start(bf16[4,128,1024]{2,1,0:T(8,128)(2,1)} %get-tuple-element.94), channel_id=1, source_target_pairs={{0,24},{4,28},{8,16},{12,20},{16,8},{20,12},{24,0},{28,4},{1,25},{... | collective-permute-start | bytes 3145736 | tf_op jit(solution)/shard_map/ppermute | solution.py:247
  337.6 46.2 %collective-permute-start.23 = (bf16[4,128,1024]{2,1,0:T(8,128)(2,1)}, bf16[4,128,1024]{2,1,0:T(8,128)(2,1)S(1)}, u32[]{:S(2)}, u32[]{:S(2)}) collective-permute-start(bf16[4,128,1024]{2,1,0:T(8,128)(2,1)} %get-tuple-element.95), channel_id=1, source_target_pairs={{0,16},{4,20},{8,24},{12,28},{16,0},{20,4},{24,8},{28,12},{1,17},{... | collective-permute-start | bytes 3145736 | tf_op jit(solution)/shard_map/ppermute | solution.py:247
  338.1 46.7 %collective-permute-start.22 = (bf16[4,128,1024]{2,1,0:T(8,128)(2,1)S(1)}, bf16[4,128,1024]{2,1,0:T(8,128)(2,1)}, u32[]{:S(2)}, u32[]{:S(2)}) collective-permute-start(bf16[4,128,1024]{2,1,0:T(8,128)(2,1)S(1)} %get-tuple-element.93), channel_id=1, source_target_pairs={{0,8},{4,12},{8,0},{12,4},{16,24},{20,28},{24,16},{28,20},{1,9},{5... | collective-permute-start | bytes 3145736 | tf_op jit(solution)/shard_map/ppermute | solution.py:247
  446.0 62.0 %collective-permute-start.25 = (bf16[1536,1024]{1,0:T(8,128)(2,1)}, bf16[1536,1024]{1,0:T(8,128)(2,1)}, u32[]{:S(2)}, u32[]{:S(2)}) collective-permute-start(bf16[1536,1024]{1,0:T(8,128)(2,1)} %convolution_convert_fusion), channel_id=1, source_target_pairs={{0,4},{4,0},{8,12},{12,8},{16,20},{20,16},{24,28},{28,24},{1,5},{5... | collective-permute-start | bytes 9437192 | tf_op jit(solution)/shard_map/ppermute | solution.py:247
  446.2 406.4 %all-gather.12.cloned.1.call-start = ((), (), s32[]{:S(2)}) async-start(), calls=%async_computation.5 | async-start | bytes 2359296 | tf_op jit(solution)/shard_map/all_gather | solution.py:503
  448.5 32.7 %collective-permute-start.28 = (bf16[4,128,1024]{2,1,0:T(8,128)(2,1)S(1)}, bf16[4,128,1024]{2,1,0:T(8,128)(2,1)S(1)}, u32[]{:S(2)}, u32[]{:S(2)}) collective-permute-start(bf16[4,128,1024]{2,1,0:T(8,128)(2,1)S(1)} %get-tuple-element.91), channel_id=1, source_target_pairs={{0,24},{4,28},{8,16},{12,20},{16,8},{20,12},{24,0},{28,4},{1,25},{... | collective-permute-start | bytes 3145736 | tf_op jit(solution)/shard_map/ppermute | solution.py:247
  450.2 55.6 %collective-permute-start.27 = (bf16[4,128,1024]{2,1,0:T(8,128)(2,1)S(1)}, bf16[4,128,1024]{2,1,0:T(8,128)(2,1)S(1)}, u32[]{:S(2)}, u32[]{:S(2)}) collective-permute-start(bf16[4,128,1024]{2,1,0:T(8,128)(2,1)S(1)} %get-tuple-element.92), channel_id=1, source_target_pairs={{0,16},{4,20},{8,24},{12,28},{16,0},{20,4},{24,8},{28,12},{1,17},{... | collective-permute-start | bytes 3145736 | tf_op jit(solution)/shard_map/ppermute | solution.py:247
  451.5 54.4 %collective-permute-start.26 = (bf16[4,128,1024]{2,1,0:T(8,128)(2,1)S(1)}, bf16[4,128,1024]{2,1,0:T(8,128)(2,1)S(1)}, u32[]{:S(2)}, u32[]{:S(2)}) collective-permute-start(bf16[4,128,1024]{2,1,0:T(8,128)(2,1)S(1)} %get-tuple-element.90), channel_id=1, source_target_pairs={{0,8},{4,12},{8,0},{12,4},{16,24},{20,28},{24,16},{28,20},{1,9},{5... | collective-permute-start | bytes 3145736 | tf_op jit(solution)/shard_map/ppermute | solution.py:247
  528.9 327.8 %all-gather.14.cloned.1.call-start = ((), (), s32[]{:S(2)}) async-start(), calls=%async_computation.6 | async-start | bytes 9437184 | tf_op jit(solution)/shard_map/all_gather | solution.py:474
  529.0 11.1 %collective-permute-start.65 = (bf16[128,1024]{1,0:T(8,128)(2,1)S(1)}, bf16[128,1024]{1,0:T(8,128)(2,1)S(1)}, u32[]{:S(2)}, u32[]{:S(2)}) collective-permute-start(bf16[128,1024]{1,0:T(8,128)(2,1)S(1)} %get-tuple-element.108), channel_id=1, source_target_pairs={{0,1},{1,2},{2,3},{3,0},{4,5},{5,6},{6,7},{7,4},{8,9},{9,10},{10,1... | collective-permute-start | bytes 786440 | tf_op jit(solution)/shard_map/ppermute | solution.py:172
  530.4 18.6 %collective-permute-start.66 = (bf16[128,1024]{1,0:T(8,128)(2,1)S(1)}, bf16[128,1024]{1,0:T(8,128)(2,1)S(1)}, u32[]{:S(2)}, u32[]{:S(2)}) collective-permute-start(bf16[128,1024]{1,0:T(8,128)(2,1)S(1)} %get-tuple-element.107), channel_id=1, source_target_pairs={{0,2},{1,3},{2,0},{3,1},{4,6},{5,7},{6,4},{7,5},{8,10},{9,11},{10,... | collective-permute-start | bytes 786440 | tf_op jit(solution)/shard_map/ppermute | solution.py:172
  533.0 16.0 %collective-permute-start.67 = (bf16[128,1024]{1,0:T(8,128)(2,1)S(1)}, bf16[128,1024]{1,0:T(8,128)(2,1)S(1)}, u32[]{:S(2)}, u32[]{:S(2)}) collective-permute-start(bf16[128,1024]{1,0:T(8,128)(2,1)S(1)} %get-tuple-element.106), channel_id=1, source_target_pairs={{0,3},{1,0},{2,1},{3,2},{4,7},{5,4},{6,5},{7,6},{8,11},{9,8},{10,9... | collective-permute-start | bytes 786440 | tf_op jit(solution)/shard_map/ppermute | solution.py:172
  553.9 33.4 %collective-permute-start.15 = (bf16[256,2048]{1,0:T(8,128)(2,1)}, bf16[256,2048]{1,0:T(8,128)(2,1)}, u32[]{:S(2)}, u32[]{:S(2)}) collective-permute-start(bf16[256,2048]{1,0:T(8,128)(2,1)} %get-tuple-element.97), channel_id=1, source_target_pairs={{0,3},{1,0},{2,1},{3,2},{4,7},{5,4},{6,5},{7,6},{8,11},{9,8},{10,9... | collective-permute-start | bytes 3145736 | tf_op jit(solution)/shard_map/ppermute | solution.py:172
  576.4 10.7 %collective-permute-start.35 = (f32[2,512]{1,0:T(2,128)S(1)}, f32[2,512]{1,0:T(2,128)S(1)}, u32[]{:S(2)}, u32[]{:S(2)}) collective-permute-start(f32[2,512]{1,0:T(2,128)S(1)} %bitcast.302), channel_id=1, source_target_pairs={{0,3},{1,0},{2,1},{3,2},{4,7},{5,4},{6,5},{7,6},{8,11},{9,8},{10,9... | collective-permute-start | bytes 12296 | tf_op jit(solution)/shard_map/ppermute | solution.py:172
  582.4 46.0 %collective-permute-start.58 = (bf16[4,128,1024]{2,1,0:T(8,128)(2,1)S(1)}, bf16[4,128,1024]{2,1,0:T(8,128)(2,1)S(1)}, u32[]{:S(2)}, u32[]{:S(2)}) collective-permute-start(bf16[4,128,1024]{2,1,0:T(8,128)(2,1)S(1)} %fusion.26.refs_0_), channel_id=1, source_target_pairs={{0,8},{4,12},{8,0},{12,4},{16,24},{20,28},{24,16},{28,20},{1,9},{5... | collective-permute-start | bytes 3145736 | tf_op jit(solution)/shard_map/ppermute | solution.py:247
  583.9 67.7 %collective-permute-start.59 = (bf16[4,128,1024]{2,1,0:T(8,128)(2,1)S(1)}, bf16[4,128,1024]{2,1,0:T(8,128)(2,1)S(1)}, u32[]{:S(2)}, u32[]{:S(2)}) collective-permute-start(bf16[4,128,1024]{2,1,0:T(8,128)(2,1)S(1)} %fusion.26.refs_0_), channel_id=1, source_target_pairs={{0,16},{4,20},{8,24},{12,28},{16,0},{20,4},{24,8},{28,12},{1,17},{... | collective-permute-start | bytes 3145736 | tf_op jit(solution)/shard_map/ppermute | solution.py:247
  585.5 79.1 %collective-permute-start.60 = (bf16[4,128,1024]{2,1,0:T(8,128)(2,1)S(1)}, bf16[4,128,1024]{2,1,0:T(8,128)(2,1)}, u32[]{:S(2)}, u32[]{:S(2)}) collective-permute-start(bf16[4,128,1024]{2,1,0:T(8,128)(2,1)S(1)} %fusion.26.refs_0_), channel_id=1, source_target_pairs={{0,24},{4,28},{8,16},{12,20},{16,8},{20,12},{24,0},{28,4},{1,25},{... | collective-permute-start | bytes 3145736 | tf_op jit(solution)/shard_map/ppermute | solution.py:247
  587.1 81.8 %collective-permute-start.61 = (bf16[4,128,1024]{2,1,0:T(8,128)(2,1)S(1)}, bf16[4,128,1024]{2,1,0:T(8,128)(2,1)}, u32[]{:S(2)}, u32[]{:S(2)}) collective-permute-start(bf16[4,128,1024]{2,1,0:T(8,128)(2,1)S(1)} %fusion.26.refs_0_), channel_id=1, source_target_pairs={{0,4},{4,0},{8,12},{12,8},{16,20},{20,16},{24,28},{28,24},{1,5},{5... | collective-permute-start | bytes 3145736 | tf_op jit(solution)/shard_map/ppermute | solution.py:247
  587.4 41.1 %collective-permute-start.36 = (f32[5120]{0:T(1024)S(1)}, f32[5120]{0:T(1024)S(1)}, u32[]{:S(2)}, u32[]{:S(2)}) collective-permute-start(f32[5120]{0:T(1024)S(1)} %constant_dynamic-update-slice_fusion.10), channel_id=1, source_target_pairs={{0,4},{4,0},{8,12},{12,8},{16,20},{20,16},{24,28},{28,24},{1,5},{5... | collective-permute-start | bytes 61448 | tf_op jit(solution)/shard_map/ppermute | solution.py:247
  628.4 36.3 %collective-permute-start.29 = (bf16[128,2048]{1,0:T(8,128)(2,1)}, bf16[128,2048]{1,0:T(8,128)(2,1)}, u32[]{:S(2)}, u32[]{:S(2)}) collective-permute-start(bf16[128,2048]{1,0:T(8,128)(2,1)} %get-tuple-element.86), channel_id=1, source_target_pairs={{0,1},{1,2},{2,3},{3,0},{4,5},{5,6},{6,7},{7,4},{8,9},{9,10},{10,1... | collective-permute-start | bytes 1572872 | tf_op jit(solution)/shard_map/ppermute | solution.py:172
  628.5 37.0 %collective-permute-start.31 = (bf16[128,2048]{1,0:T(8,128)(2,1)}, bf16[128,2048]{1,0:T(8,128)(2,1)}, u32[]{:S(2)}, u32[]{:S(2)}) collective-permute-start(bf16[128,2048]{1,0:T(8,128)(2,1)} %get-tuple-element.88), channel_id=1, source_target_pairs={{0,3},{1,0},{2,1},{3,2},{4,7},{5,4},{6,5},{7,6},{8,11},{9,8},{10,9... | collective-permute-start | bytes 1572872 | tf_op jit(solution)/shard_map/ppermute | solution.py:172
  655.6 15.3 %collective-permute-start.41 = (bf16[3,128,1024]{2,1,0:T(8,128)(2,1)}, bf16[3,128,1024]{2,1,0:T(8,128)(2,1)}, u32[]{:S(2)}, u32[]{:S(2)}) collective-permute-start(bf16[3,128,1024]{2,1,0:T(8,128)(2,1)} %get-tuple-element.100), channel_id=1, source_target_pairs={{0,24},{4,28},{8,16},{12,20},{16,8},{20,12},{24,0},{28,4},{1,25},{... | collective-permute-start | bytes 2359304 | tf_op jit(solution)/shard_map/ppermute | solution.py:247
  664.7 31.8 %collective-permute-start.62 = (bf16[4,128,1024]{2,1,0:T(8,128)(2,1)S(1)}, bf16[4,128,1024]{2,1,0:T(8,128)(2,1)S(1)}, u32[]{:S(2)}, u32[]{:S(2)}) collective-permute-start(bf16[4,128,1024]{2,1,0:T(8,128)(2,1)S(1)} %collective-permute-done.58.refs_1_), channel_id=1, source_target_pairs={{0,4},{4,0},{8,12},{12,8},{16,20},{20,16},{24,28},{28,24},{1,5},{5... | collective-permute-start | bytes 3145736 | tf_op jit(solution)/shard_map/ppermute | solution.py:247
  664.8 22.2 %collective-permute-start.40 = (bf16[3,128,1024]{2,1,0:T(8,128)(2,1)}, bf16[3,128,1024]{2,1,0:T(8,128)(2,1)S(1)}, u32[]{:S(2)}, u32[]{:S(2)}) collective-permute-start(bf16[3,128,1024]{2,1,0:T(8,128)(2,1)} %get-tuple-element.101), channel_id=1, source_target_pairs={{0,16},{4,20},{8,24},{12,28},{16,0},{20,4},{24,8},{28,12},{1,17},{... | collective-permute-start | bytes 2359304 | tf_op jit(solution)/shard_map/ppermute | solution.py:247
  665.4 22.2 %collective-permute-start.39 = (bf16[3,128,1024]{2,1,0:T(8,128)(2,1)}, bf16[3,128,1024]{2,1,0:T(8,128)(2,1)S(1)}, u32[]{:S(2)}, u32[]{:S(2)}) collective-permute-start(bf16[3,128,1024]{2,1,0:T(8,128)(2,1)} %get-tuple-element.99), channel_id=1, source_target_pairs={{0,8},{4,12},{8,0},{12,4},{16,24},{20,28},{24,16},{28,20},{1,9},{5... | collective-permute-start | bytes 2359304 | tf_op jit(solution)/shard_map/ppermute | solution.py:247
  668.9 34.3 %collective-permute-start.63 = (bf16[4,128,1024]{2,1,0:T(8,128)(2,1)S(1)}, bf16[4,128,1024]{2,1,0:T(8,128)(2,1)}, u32[]{:S(2)}, u32[]{:S(2)}) collective-permute-start(bf16[4,128,1024]{2,1,0:T(8,128)(2,1)S(1)} %collective-permute-done.59.refs_2_), channel_id=1, source_target_pairs={{0,4},{4,0},{8,12},{12,8},{16,20},{20,16},{24,28},{28,24},{1,5},{5... | collective-permute-start | bytes 3145736 | tf_op jit(solution)/shard_map/ppermute | solution.py:247
  670.9 36.2 %collective-permute-start.64 = (bf16[4,128,1024]{2,1,0:T(8,128)(2,1)}, bf16[4,128,1024]{2,1,0:T(8,128)(2,1)}, u32[]{:S(2)}, u32[]{:S(2)}) collective-permute-start(bf16[4,128,1024]{2,1,0:T(8,128)(2,1)} %collective-permute-done.60.refs_3_), channel_id=1, source_target_pairs={{0,4},{4,0},{8,12},{12,8},{16,20},{20,16},{24,28},{28,24},{1,5},{5... | collective-permute-start | bytes 3145736 | tf_op jit(solution)/shard_map/ppermute | solution.py:247
  687.0 114.3 %collective-permute-start.32 = (bf16[256,2048]{1,0:T(8,128)(2,1)}, bf16[256,2048]{1,0:T(8,128)(2,1)}, u32[]{:S(2)}, u32[]{:S(2)}) collective-permute-start(bf16[256,2048]{1,0:T(8,128)(2,1)} %pad_maximum_fusion.1), channel_id=1, source_target_pairs={{0,3},{1,0},{2,1},{3,2},{4,7},{5,4},{6,5},{7,6},{8,11},{9,8},{10,9... | collective-permute-start | bytes 3145736 | tf_op jit(solution)/shard_map/ppermute | solution.py:172
  687.6 115.9 %collective-permute-start.30 = (bf16[256,2048]{1,0:T(8,128)(2,1)}, bf16[256,2048]{1,0:T(8,128)(2,1)}, u32[]{:S(2)}, u32[]{:S(2)}) collective-permute-start(bf16[256,2048]{1,0:T(8,128)(2,1)} %pad_maximum_fusion), channel_id=1, source_target_pairs={{0,1},{1,2},{2,3},{3,0},{4,5},{5,6},{6,7},{7,4},{8,9},{9,10},{10,1... | collective-permute-start | bytes 3145736 | tf_op jit(solution)/shard_map/ppermute | solution.py:172
  700.3 75.7 %collective-permute-start.44 = (bf16[128,1024]{1,0:T(8,128)(2,1)}, bf16[128,1024]{1,0:T(8,128)(2,1)}, u32[]{:S(2)}, u32[]{:S(2)}) collective-permute-start(bf16[128,1024]{1,0:T(8,128)(2,1)} %get-tuple-element.112), channel_id=1, source_target_pairs={{2,0},{1,1},{0,2},{3,3},{6,4},{5,5},{4,6},{7,7},{10,8},{9,9},{8,10... | collective-permute-start | bytes 786440 | tf_op jit(solution)/shard_map/ppermute | solution.py:496
  703.2 71.4 %collective-permute-start.54 = (f32[512]{0:T(512)S(1)}, f32[512]{0:T(512)S(1)}, u32[]{:S(2)}, u32[]{:S(2)}) collective-permute-start(f32[512]{0:T(512)S(1)} %bitcast.307), channel_id=1, source_target_pairs={{2,0},{1,1},{0,2},{3,3},{6,4},{5,5},{4,6},{7,7},{10,8},{9,9},{8,10... | collective-permute-start | bytes 6152 | tf_op jit(solution)/shard_map/ppermute | solution.py:521
  707.1 80.7 %collective-permute-start.43 = (bf16[128,1024]{1,0:T(8,128)(2,1)}, bf16[128,1024]{1,0:T(8,128)(2,1)}, u32[]{:S(2)}, u32[]{:S(2)}) collective-permute-start(bf16[128,1024]{1,0:T(8,128)(2,1)} %get-tuple-element.113), channel_id=1, source_target_pairs={{1,0},{0,1},{3,2},{2,3},{5,4},{4,5},{7,6},{6,7},{9,8},{8,9},{11,10... | collective-permute-start | bytes 786440 | tf_op jit(solution)/shard_map/ppermute | solution.py:496
  774.6 13.3 %collective-permute-start.42 = (bf16[128,1024]{1,0:T(8,128)(2,1)S(1)}, bf16[128,1024]{1,0:T(8,128)(2,1)}, u32[]{:S(2)}, u32[]{:S(2)}) collective-permute-start(bf16[128,1024]{1,0:T(8,128)(2,1)S(1)} %get-tuple-element.111), channel_id=1, source_target_pairs={{0,0},{3,1},{2,2},{1,3},{4,4},{7,5},{6,6},{5,7},{8,8},{11,9},{10,1... | collective-permute-start | bytes 786440 | tf_op jit(solution)/shard_map/ppermute | solution.py:496
  776.1 33.2 %collective-permute-start.14 = (bf16[256,2048]{1,0:T(8,128)(2,1)}, bf16[256,2048]{1,0:T(8,128)(2,1)S(1)}, u32[]{:S(2)}, u32[]{:S(2)}) collective-permute-start(bf16[256,2048]{1,0:T(8,128)(2,1)} %get-tuple-element.98), channel_id=1, source_target_pairs={{0,2},{1,3},{2,0},{3,1},{4,6},{5,7},{6,4},{7,5},{8,10},{9,11},{10,... | collective-permute-start | bytes 3145736 | tf_op jit(solution)/shard_map/ppermute | solution.py:172
  787.9 13.2 %collective-permute-start.52 = (f32[512]{0:T(512)S(1)}, f32[512]{0:T(512)S(1)}, u32[]{:S(2)}, u32[]{:S(2)}) collective-permute-start(f32[512]{0:T(512)S(1)} %bitcast.305), channel_id=1, source_target_pairs={{0,0},{3,1},{2,2},{1,3},{4,4},{7,5},{6,6},{5,7},{8,8},{11,9},{10,1... | collective-permute-start | bytes 6152 | tf_op jit(solution)/shard_map/ppermute | solution.py:521
  798.5 38.8 %collective-permute-start.13 = (bf16[256,2048]{1,0:T(8,128)(2,1)S(1)}, bf16[256,2048]{1,0:T(8,128)(2,1)S(1)}, u32[]{:S(2)}, u32[]{:S(2)}) collective-permute-start(bf16[256,2048]{1,0:T(8,128)(2,1)S(1)} %copy-done.24), channel_id=1, source_target_pairs={{0,1},{1,2},{2,3},{3,0},{4,5},{5,6},{6,7},{7,4},{8,9},{9,10},{10,1... | collective-permute-start | bytes 3145736 | tf_op jit(solution)/shard_map/ppermute | solution.py:172
  801.1 20.4 %collective-permute-start.45 = (bf16[3,128,1024]{2,1,0:T(8,128)(2,1)S(1)}, bf16[3,128,1024]{2,1,0:T(8,128)(2,1)S(1)}, u32[]{:S(2)}, u32[]{:S(2)}) collective-permute-start(bf16[3,128,1024]{2,1,0:T(8,128)(2,1)S(1)} %pad_maximum_fusion.4.refs_0_), channel_id=1, source_target_pairs={{0,8},{4,12},{8,0},{12,4},{16,24},{20,28},{24,16},{28,20},{1,9},{5... | collective-permute-start | bytes 2359304 | tf_op jit(solution)/shard_map/ppermute | solution.py:247
  801.3 34.1 %collective-permute-start.46 = (bf16[3,128,1024]{2,1,0:T(8,128)(2,1)S(1)}, bf16[3,128,1024]{2,1,0:T(8,128)(2,1)S(1)}, u32[]{:S(2)}, u32[]{:S(2)}) collective-permute-start(bf16[3,128,1024]{2,1,0:T(8,128)(2,1)S(1)} %pad_maximum_fusion.4.refs_0_), channel_id=1, source_target_pairs={{0,16},{4,20},{8,24},{12,28},{16,0},{20,4},{24,8},{28,12},{1,17},{... | collective-permute-start | bytes 2359304 | tf_op jit(solution)/shard_map/ppermute | solution.py:247
  803.5 33.7 %collective-permute-start.47 = (bf16[3,128,1024]{2,1,0:T(8,128)(2,1)S(1)}, bf16[3,128,1024]{2,1,0:T(8,128)(2,1)S(1)}, u32[]{:S(2)}, u32[]{:S(2)}) collective-permute-start(bf16[3,128,1024]{2,1,0:T(8,128)(2,1)S(1)} %pad_maximum_fusion.4.refs_0_), channel_id=1, source_target_pairs={{0,24},{4,28},{8,16},{12,20},{16,8},{20,12},{24,0},{28,4},{1,25},{... | collective-permute-start | bytes 2359304 | tf_op jit(solution)/shard_map/ppermute | solution.py:247
  809.3 34.3 %collective-permute-start.48 = (bf16[3,128,1024]{2,1,0:T(8,128)(2,1)S(1)}, bf16[3,128,1024]{2,1,0:T(8,128)(2,1)S(1)}, u32[]{:S(2)}, u32[]{:S(2)}) collective-permute-start(bf16[3,128,1024]{2,1,0:T(8,128)(2,1)S(1)} %pad_maximum_fusion.4.refs_0_), channel_id=1, source_target_pairs={{0,4},{4,0},{8,12},{12,8},{16,20},{20,16},{24,28},{28,24},{1,5},{5... | collective-permute-start | bytes 2359304 | tf_op jit(solution)/shard_map/ppermute | solution.py:247
  821.5 22.1 %collective-permute-start.49 = (bf16[3,128,1024]{2,1,0:T(8,128)(2,1)S(1)}, bf16[3,128,1024]{2,1,0:T(8,128)(2,1)S(1)}, u32[]{:S(2)}, u32[]{:S(2)}) collective-permute-start(bf16[3,128,1024]{2,1,0:T(8,128)(2,1)S(1)} %collective-permute-done.45.refs_1_), channel_id=1, source_target_pairs={{0,4},{4,0},{8,12},{12,8},{16,20},{20,16},{24,28},{28,24},{1,5},{5... | collective-permute-start | bytes 2359304 | tf_op jit(solution)/shard_map/ppermute | solution.py:247
  (60 other events, 1278.7 us)
Sparse Core Ops, SparseCore 0:
  28.7 46.6 all-gather.5
  77.9 54.2 all-gather.7
  134.1 27.7 all-gather.9
  446.3 54.6 reduce-scatter.1
  529.0 27.7 all-gather.11
  558.6 95.8 all-gather.13

commit v5 on v4

--- a/solution.py
+++ b/solution.py
@@ -263,50 +263,70 @@
     return total
 
 
+def step_bits(reps):
+    bits = list(range((reps // 2).bit_length() - 1))
+    return bits, bits[::-1]
+
+
 def spread(x, reps):
-    own = [x] + [flip(x, 2 * mask, reps) for mask in range(1, reps // 2)]
+    half = x.shape[1] // 2
+    own = []
+    parts = [x[None, :, :half], x[None, :, half:]]
+    steps = step_bits(reps)
+    for step in range(len(steps[0])):
+        last = step == len(steps[0]) - 1
+        got = [flip(parts[i], 2 << steps[i][step], reps) for i in range(2)]
+        if last:
+            own = [parts[0], got[0], parts[1], got[1]]
+        else:
+            parts = [jnp.concatenate(pair, 0) for pair in zip(parts, got)]
     return own + [flip(piece, 1, reps) for piece in own]
 
 
 def assemble(pieces, rep, wide):
-    chips = len(pieces) // 2
-    lead, rows, cols = pieces[0].shape
-    tile = max(8, rows // 2)
-    tiles = rows // tile
+    some, lead, tile, cols = pieces[0].shape
+    chips = 2 * some
     groups, width = (1, 2 * cols * lead) if wide else (lead, 2 * cols)
-
-    def kernel(place_ref, *refs):
+    table = []
+    for order in step_bits(2 * chips):
+        masks = [0]
+        for bit in order:
+            masks += [m ^ (1 << bit) for m in masks]
+        table += masks
+
+    def kernel(table_ref, *refs):
         out = refs[-1]
-        for i in range(chips):
+        core = table_ref[2 * chips]
+        for i in range(4):
 
             @pl.when(pl.program_id(0) == i)
             def _(i=i):
-                for side, ref in ((place_ref[1], refs[i]), (1 - place_ref[1], refs[chips + i])):
+                for side, ref in ((core, refs[i]), (1 - core, refs[4 + i])):
                     for l in range(lead):
                         at = pl.multiple_of(side * cols + (l * 2 * cols if wide else 0), 128)
-                        out[0 if wide else l, 0, :, pl.ds(at, cols)] = ref[l].astype(F32)
+                        out[0 if wide else l, 0, :, pl.ds(at, cols)] = ref[0, l].astype(F32)
 
     def source(i):
         return pl.BlockSpec(
-            (lead, tile, cols),
-            lambda p, t, place: (0, jnp.where(p == i, t, jnp.where(p < i, 0, tiles - 1)), 0),
+            (1, lead, tile, cols),
+            lambda p, j, t: (jnp.where(p == i, j, jnp.where(p < i, 0, some - 1)), 0, 0, 0),
         )
 
     out = pl.pallas_call(
         kernel,
         grid_spec=pltpu.PrefetchScalarGridSpec(
             num_scalar_prefetch=1,
-            grid=(chips, tiles),
-            in_specs=[source(i) for i in range(chips)] * 2,
+            grid=(4, some),
+            in_specs=[source(i) for i in range(4)] * 2,
             out_specs=pl.BlockSpec(
-                (groups, 1, tile, width), lambda p, t, place: (0, place[0] ^ p, t, 0)
+                (groups, 1, tile, width), lambda p, j, t: (0, t[p * some + j], p // 2, 0)
             ),
         ),
-        out_shape=jax.ShapeDtypeStruct((groups, chips, rows, width), F32),
+        out_shape=jax.ShapeDtypeStruct((groups, chips, 2 * tile, width), F32),
         compiler_params=pltpu.CompilerParams(vmem_limit_bytes=48 << 20),
         name="assemble",
-    )(jnp.stack([rep >> 1, rep & 1]), *pieces)
-    return out.reshape(groups * chips * rows, width)
+    )(jnp.concatenate([jnp.asarray(table, jnp.int32) ^ (rep >> 1), (rep & 1)[None]]), *pieces)
+    return out.reshape(groups * chips * 2 * tile, width)
 
 
 def lay_out(x, wide):
@@ -445,6 +465,11 @@
 
     grads, branches = hold(grads, branches)
     blocks = inner // part
+    g_out = tn(grads, attended).astype(BF16)
+    g_out_1 = lax.psum_scatter(
+        g_out.reshape(count, part, part), "rep", scatter_dimension=1, tiled=True
+    )
+    grads, g_out = hold(grads, g_out)
     shr_send = low_term(grads, hidden_other)
     shr_arrived = flip(shr_send, 1, reps)
     grads_1, shr_send = hold(grads, shr_send)
@@ -461,12 +486,8 @@
     exp_sum = low_term(d_up_1, normed_mine, exp_arrived)
     exp_total = reduce_chips(exp_sum.reshape(blocks, part, width // 2), rep, reps)
 
-    grads_4, exp_sum = hold(grads_3, exp_sum)
-    g_out = tn(grads_4, attended).astype(BF16)
-    g_out_1 = lax.psum_scatter(
-        g_out.reshape(count, part, part), "rep", scatter_dimension=1, tiled=True
-    )
-    d_up_2, g_out = hold(d_up_1, g_out)
+    d_up_2, exp_sum, g_out_1 = hold(d_up_1, exp_sum, g_out_1)
+    g_out = jnp.transpose(swap_blocks(g_out_1, 0, count, me), (1, 0, 2)).reshape(sub, width)
     d_normed = nn(d_up_2, expand_weight)
     g_shr = shr_total()
     d_att, d_normed, g_shr = hold(d_att, d_normed, g_shr)
@@ -486,7 +507,7 @@
     d_mixed_2, in_sum = hold(d_mixed_1, in_sum)
     g_exp = exp_total()
     exp_pieces = spread(g_exp, reps)
-    d_mixed_2, g_exp, g_out_1 = hold(d_mixed_2, g_exp, g_out_1)
+    d_mixed_2, g_exp = hold(d_mixed_2, g_exp)
     d_normed = d_normed + nn(d_mixed_2, in_w)
     both = jnp.stack([jnp.sum(d_normed * normed.astype(F32), 0), jnp.sum(d_normed, 0)])
     d_normed = d_normed.astype(BF16)
@@ -499,7 +520,6 @@
     both = jnp.sum(swap_blocks(both.reshape(2, count, part), 1, count, me), 1)
     sums = jnp.concatenate([both[0], both[1], b_out, b_exp, b_in])
 
-    g_out = jnp.transpose(swap_blocks(g_out_1, 0, count, me), (1, 0, 2)).reshape(sub, width)
     g_out = lax.all_gather(g_out, "rep", axis=0, tiled=True).astype(F32)
     g_shr = lay_out(g_shr, True)
     g_exp = assemble(exp_pieces, rep, False)

time: 885 us -> 864 us (0.976)
  waiting for transfers between devices: 371 us -> 320 us
  starting transfers between devices: 134 us -> 173 us
    ppermute x29 -> x31, waiting for transfers between devices: 193 us -> 106 us  [flip(): return lax.ppermute(x, 'rep', [(i, i ^ mask) for i in range(reps)])]
    ppermute x3, waiting for transfers between devices: 76 us -> 3.9 us  [local(): lax.ppermute(pick(b_in, kinds[j]), 'shard', back[j])]
    ppermute x30, waiting for transfers between devices: 98.5 us -> 165 us  [shift(): lax.ppermute(x, 'shard', [(i, (i + offset) % count) for i in range(count)])]
    reduce_scatter x1, waiting for transfers between devices: 0.01 us -> 41.6 us  [local(): lax.psum_scatter(g_out.reshape(count, part, part), 'rep', scatter_dimensi...]
    ppermute x30, starting transfers between devices: 94.4 us -> 133 us  [shift(): lax.ppermute(x, 'shard', [(i, (i + offset) % count) for i in range(count)])]
    ppermute x29 -> x31, starting transfers between devices: 22.7 us -> 24.9 us  [flip(): return lax.ppermute(x, 'rep', [(i, i ^ mask) for i in range(reps)])]
  transfers between devices with their start and end apart: 74 -> 76, of which waited for: 31 -> 30; matrix products, arithmetic and copies ran while one was open for 21% -> 24% of each run, Pallas kernels for 5% -> 8%
where the time goes in v5:
time: 864 us; the launch traced here: 854 us
  waiting for transfers between devices  320 us (37%)
  starting transfers between devices  173 us (20%)
  matrix products  151 us (17%)
  Pallas kernels  77.1 us (9%)
  local copies, waits for them, and re-layouts  65.1 us (8%)
  other arithmetic  40.5 us (5%)
  between operations  27.6 us (3%)
    ppermute x30, waiting for transfers between devices, shift(): lax.ppermute(x, 'shard', [(i, (i + offset) % count) for i in range(count)])  165 us
    ppermute x30, starting transfers between devices, shift(): lax.ppermute(x, 'shard', [(i, (i + offset) % count) for i in range(count)])  133 us
    ppermute x31, waiting for transfers between devices, flip(): return lax.ppermute(x, 'rep', [(i, i ^ mask) for i in range(reps)])  106 us
    dot_general x4, matrix products, nt(): lax.dot_general(a, b, (((1,), (1,)), ((), ())), preferred_element_type=F32)  52 us
    dot_general x7, matrix products, tn(): lax.dot_general(a, b, (((0,), (0,)), ((), ())), preferred_element_type=F32)  50.8 us
    dot_general x4, matrix products, nn(): lax.dot_general(a, b, (((1,), (0,)), ((), ())), preferred_element_type=F32)  48.3 us
    reduce_scatter x1, waiting for transfers between devices, local(): lax.psum_scatter(g_out.reshape(count, part, part), 'rep', scatter_dimensi...  41.6 us
    pallas_call x1, Pallas kernels, attend_back(): pl.pallas_call(functools.partial(attend_back_kernel, blk), grid=(pairs,),...  25.4 us
  transfers between devices with their start and end apart: 76, of which 30 were waited for; matrix products, arithmetic and copies ran while one was open for 24% of the time, Pallas kernels for 8%

profile of v5, /device:TPU:0, one launch (start us, length us, event | category | flops | bytes accessed | tf_op | source)
XLA Modules:
  0.0 853.8 jit_solution(14362797980388309065)
XLA Ops:
  8.6 6.0 collective-permute-start.9
  23.1 3.4 collective-permute-done.8
  33.5 2.7 constant_dynamic-slice_fusion.8
  43.1 6.7 collective-permute-done.10
  50.8 12.2 %collective-permute-done.11 = bf16[64,2560]{1,0:T(8,128)(2,1)} collective-permute-done((bf16[64,2560]{1,0:T(8,128)(2,1)}, bf16[64,2560]{1,0:T(8,128)(2,1)}, u32[]{:S(2)}, u32[]{:S(2)}) %collective-permute-start.11) | collective-permute-done | bytes 327712 | tf_op jit(solution)/shard_map/ppermute | solution.py:172
  66.2 6.4 collective-permute-start
  75.3 3.5 collective-permute-start.17
  80.2 2.5 broadcast.129.clone.1
  85.0 3.2 fusion.49
  91.5 3.8 collective-permute-start.4
  99.2 3.9 collective-permute-done.16
  104.3 18.2 %collective-permute-start.18 = (bf16[128,2048]{1,0:T(8,128)(2,1)S(1)}, bf16[128,2048]{1,0:T(8,128)(2,1)S(1)}, u32[]{:S(2)}, u32[]{:S(2)}) collective-permute-start(bf16[128,2048]{1,0:T(8,128)(2,1)S(1)} %slice.213), channel_id=1, source_target_pairs={{0,1},{1,2},{2,3},{3,0},{4,5},{5,6},{6,7},{7,4},{8,9},{9,10},{10,1... | collective-permute-start | bytes 1572872 | tf_op jit(solution)/shard_map/ppermute | solution.py:172
  122.5 2.9 collective-permute-done.17
  132.9 15.3 %collective-permute-done.3 = bf16[256,2048]{1,0:T(8,128)(2,1)} collective-permute-done((bf16[256,2048]{1,0:T(8,128)(2,1)}, bf16[256,2048]{1,0:T(8,128)(2,1)}, u32[]{:S(2)}, u32[]{:S(2)}) %collective-permute-start.3) | collective-permute-done | bytes 1048608 | tf_op jit(solution)/shard_map/ppermute | solution.py:172
  149.3 18.1 %collective-permute-start.5 = (bf16[128,2048]{1,0:T(8,128)(2,1)S(1)}, bf16[128,2048]{1,0:T(8,128)(2,1)S(1)}, u32[]{:S(2)}, u32[]{:S(2)}) collective-permute-start(bf16[128,2048]{1,0:T(8,128)(2,1)S(1)} %slice.206), channel_id=1, source_target_pairs={{0,1},{1,2},{2,3},{3,0},{4,5},{5,6},{6,7},{7,4},{8,9},{9,10},{10,1... | collective-permute-start | bytes 1572872 | tf_op jit(solution)/shard_map/ppermute | solution.py:172
  167.4 2.9 collective-permute-done.4
  175.5 6.4 collective-permute-done.18
  182.7 9.9 %collective-permute-done.19 = bf16[128,2048]{1,0:T(8,128)(2,1)S(1)} collective-permute-done((bf16[128,2048]{1,0:T(8,128)(2,1)S(1)}, bf16[128,2048]{1,0:T(8,128)(2,1)S(1)}, u32[]{:S(2)}, u32[]{:S(2)}) %collective-permute-start.19) | collective-permute-done | bytes 524320 | tf_op jit(solution)/shard_map/ppermute | solution.py:172
  193.4 10.9 %collective-permute-done.5 = bf16[128,2048]{1,0:T(8,128)(2,1)S(1)} collective-permute-done((bf16[128,2048]{1,0:T(8,128)(2,1)S(1)}, bf16[128,2048]{1,0:T(8,128)(2,1)S(1)}, u32[]{:S(2)}, u32[]{:S(2)}) %collective-permute-start.5) | collective-permute-done | bytes 524320 | tf_op jit(solution)/shard_map/ppermute | solution.py:172
  204.4 7.8 collective-permute-done.6
  212.3 17.1 %multiply_convert_fusion.1 = (bf16[1024,2048]{1,0:T(8,128)(2,1)}, f32[1024,2048]{1,0:T(8,128)}) fusion(f32[2048]{0:T(1024)S(1)} %convert_element_type.258, bf16[1024,2048]{1,0:T(8,128)(2,1)S(1)} %bitcast.277, bf16[2048,2048]{1,0:T(8,128)(2,1)} %param.26), kind=kOutput, calls=%fused_computation.10 | convolution fusion | flops 8610906112 | bytes 25174016 | tf_op jit(solution)/shard_map/dot_general | solution.py:22
  229.4 11.7 %convolution_add_fusion.q_ref.k_ref.v_ref = f32[1024,1536]{1,0:T(8,128)} fusion(bf16[1024,2048]{1,0:T(8,128)(2,1)} %bitcast.278, bf16[1536,2048]{1,0:T(8,128)(2,1)} %bitcast.320, f32[1536]{0:T(1024)S(1)} %reshape.282), kind=kOutput, calls=%fused_computation.14 | convolution fusion | flops 6444023808 | bytes 16783360 | tf_op jit(solution)/shard_map/dot_general | solution.py:22
  241.1 22.5 %attend.1 = (bf16[1024,512]{1,0:T(8,128)(2,1)}, bf16[1024,512]{1,0:T(8,128)(2,1)}, bf16[1024,512]{1,0:T(8,128)(2,1)}, bf16[1024,512]{1,0:T(8,128)(2,1)}, f32[4,2,1024]{2,1,0:T(2,128)}) custom-call(f32[1024,1536]{1,0:T(8,128)} %convolution_add_fusion.q_ref.k_ref.v_ref, f32[1024,1536]{1,0:T(8,128)} %convolution_add_fusion.q_ref.k_ref.v_ref, ...), custom_call_target="tpu_custom_call" | custom-call | tf_op jit(solution)/shard_map/attend/pallas_call | solution.py:92
  263.6 14.8 %fusion.72 = f32[1024,2048]{1,0:T(8,128)} fusion(bf16[1024,2048]{1,0:T(8,128)(2,1)} %get-tuple-element.46, bf16[2048,2048]{1,0:T(8,128)(2,1)} %bitcast.318), kind=kOutput, calls=%fused_computation.221 | convolution fusion | flops 8589934592 | bytes 20971520 | tf_op jit(solution)/shard_map/dot_general | solution.py:22
  278.5 8.3 add_convert_fusion.3
  286.8 6.0 convolution_convert_fusion.3
  292.9 8.4 convolution_convert_fusion.2
  301.2 18.0 %multiply_convert_fusion = bf16[1024,2048]{1,0:T(8,128)(2,1)S(1)} fusion(f32[1024,2048]{1,0:T(8,128)} %get-tuple-element.147, f32[2048]{0:T(1024)S(1)} %convert_element_type.258, bf16[1024,2048]{1,0:T(8,128)(2,1)} %bitcast.35, bf16[2048,2048]{1,0:T(8,128)(2,1)} %bitcast.319), kind=kOutput, calls=%fused_computation.7 | convolution fusion | flops 8633974784 | bytes 25174016 | tf_op jit(solution)/shard_map/dot_general | solution.py:26
  319.3 10.6 %add_convert_fusion.1 = bf16[2048,1024]{1,0:T(8,128)(2,1)} fusion(bf16[2048,1024]{1,0:T(8,128)(2,1)} %collective-permute-done.20, bf16[1024,2048]{1,0:T(8,128)(2,1)} %bitcast.35, bf16[1024,2048]{1,0:T(8,128)(2,1)S(1)} %copy-done.59, s32[]{:T(128)S(6)} %select_n.296), kind=kOutput, calls=%fused_computation.6 | convolution fusion | flops 4301258752 | bytes 14680068 | tf_op jit(solution)/shard_map/dot_general | solution.py:30
  330.0 6.2 convolution_convert_fusion.1
  336.9 5.6 convolution_convert_fusion.4.g_ref
  344.2 2.5 collective-permute-start.24
  347.7 8.1 add_convert_fusion
  355.8 41.6 %reduce-scatter.2.cloned.1.call-done = bf16[4,64,512]{2,1,0:T(8,128)(2,1)} async-done(((bf16[4,512,512]{2,1,0:T(8,128)(2,1)}), bf16[4,64,512]{2,1,0:T(8,128)(2,1)}) %reduce-scatter.2.cloned.1.call-update) | async-done | bytes 262160 | tf_op jit(solution)/shard_map/reduce_scatter | solution.py:469
  402.3 2.7 collective-permute-done.56
  413.7 2.9 fusion.29
  416.8 13.2 %fusion.73 = f32[1024,2048]{1,0:T(8,128)} fusion(bf16[1024,2048]{1,0:T(8,128)(2,1)S(1)} %copy-done.17, bf16[2048,2048]{1,0:T(8,128)(2,1)} %param.26), kind=kOutput, calls=%fused_computation.222 | convolution fusion | flops 8589934592 | bytes 20971520 | tf_op jit(solution)/shard_map/dot_general | solution.py:26
  430.1 3.8 collective-permute-start.68
  434.9 6.3 collective-permute-done.67
  441.2 8.4 collective-permute-done.68
  450.7 25.4 %attend_back.1 = (bf16[1024,512]{1,0:T(8,128)(2,1)}, bf16[1024,512]{1,0:T(8,128)(2,1)}, bf16[1024,512]{1,0:T(8,128)(2,1)}) custom-call(bf16[1024,512]{1,0:T(8,128)(2,1)} %get-tuple-element.59.q_ref, bf16[1024,512]{1,0:T(8,128)(2,1)} %get-tuple-element.60.k_ref, bf16[1024,512]{1,0:T(8,128)(2,1)} %get-tuple-element.61.v_ref, ...), custom_call_target="tpu_custom_call" | custom-call | tf_op jit(solution)/shard_map/attend_back/pallas_call | solution.py:152
  480.3 4.9 convolution_convert_fusion
  495.1 33.7 %collective-permute-done.28 = bf16[4,128,1024]{2,1,0:T(8,128)(2,1)S(1)} collective-permute-done((bf16[4,128,1024]{2,1,0:T(8,128)(2,1)}, bf16[4,128,1024]{2,1,0:T(8,128)(2,1)S(1)}, u32[]{:S(2)}, u32[]{:S(2)}) %collective-permute-start.28) | collective-permute-done | bytes 1048608 | tf_op jit(solution)/shard_map/ppermute | solution.py:247
  528.8 21.4 %collective-permute-done.27 = bf16[4,128,1024]{2,1,0:T(8,128)(2,1)S(1)} collective-permute-done((bf16[4,128,1024]{2,1,0:T(8,128)(2,1)}, bf16[4,128,1024]{2,1,0:T(8,128)(2,1)S(1)}, u32[]{:S(2)}, u32[]{:S(2)}) %collective-permute-start.27) | collective-permute-done | bytes 1048608 | tf_op jit(solution)/shard_map/ppermute | solution.py:247
  555.0 6.7 add_convert_fusion.4
  561.7 11.4 %fusion.68 = (f32[2048]{0:T(1024)S(1)}, f32[2048]{0:T(1024)S(1)}, bf16[1024,2048]{1,0:T(8,128)(2,1)}) fusion(bf16[4,256,2048]{2,1,0:T(8,128)(2,1)S(1)} %copy-done.25, f32[1024,2048]{1,0:T(8,128)} %fusion.73, bf16[1024,1536]{1,0:T(8,128)(2,1)S(1)} %copy-done.8, bf16[1536,2048]{1,0:T(8,128)(2,1)S(1)} %bitcast.323), kind=kOutput, calls=%fused_computation.217 | convolution fusion | flops 6455029760 | bytes 26230784 | tf_op jit(solution)/shard_map/dot_general | solution.py:26
  580.9 3.1 dynamic-slice_bitcast_fusion.16
  584.5 3.3 collective-permute-start.31
  596.0 23.3 %collective-permute-done.60.refs_1_ = bf16[2,4,64,1024]{3,2,1,0:T(8,128)(2,1)S(1)} collective-permute-done((bf16[2,4,64,1024]{3,2,1,0:T(8,128)(2,1)S(1)}, bf16[2,4,64,1024]{3,2,1,0:T(8,128)(2,1)S(1)}, u32[]{:S(2)}, u32[]{:S(2)}) %collective-permute-start.60) | collective-permute-done | bytes 1048608 | tf_op jit(solution)/shard_map/ppermute | solution.py:247
  632.6 4.0 collective-permute-done.40
  636.5 5.1 collective-permute-done.39
  641.7 2.5 fusion.44
  644.3 2.7 collective-permute-start.44
  647.0 13.4 %collective-permute-done.62.refs_3_ = bf16[2,4,64,1024]{3,2,1,0:T(8,128)(2,1)S(1)} collective-permute-done((bf16[2,4,64,1024]{3,2,1,0:T(8,128)(2,1)S(1)}, bf16[2,4,64,1024]{3,2,1,0:T(8,128)(2,1)S(1)}, u32[]{:S(2)}, u32[]{:S(2)}) %collective-permute-start.62) | collective-permute-done | bytes 1048608 | tf_op jit(solution)/shard_map/ppermute | solution.py:247
  664.3 3.9 collective-permute-done.55
  668.2 4.2 collective-permute-start.32
  679.0 4.0 collective-permute-done.45
  683.0 47.6 %collective-permute-start.15 = (bf16[256,2048]{1,0:T(8,128)(2,1)}, bf16[256,2048]{1,0:T(8,128)(2,1)}, u32[]{:S(2)}, u32[]{:S(2)}) collective-permute-start(bf16[256,2048]{1,0:T(8,128)(2,1)} %get-tuple-element.97), channel_id=1, source_target_pairs={{0,3},{1,0},{2,1},{3,2},{4,7},{5,4},{6,5},{7,6},{8,11},{9,8},{10,9... | collective-permute-start | bytes 3145736 | tf_op jit(solution)/shard_map/ppermute | solution.py:172
  736.6 9.9 %assemble.3 = f32[4,4,128,2048]{3,2,1,0:T(8,128)} custom-call(s32[9]{0:T(128)S(1)} %pad_add_fusion.table_ref, bf16[2,4,64,1024]{3,2,1,0:T(8,128)(2,1)S(1)} %pad_maximum_fusion.2.refs_0_, bf16[2,4,64,1024]{3,2,1,0:T(8,128)(2,1)S(1)} %copy-done.3, bf16[2,4,64,1024]{3,2,1,0:T(8,128)(2,1)S(1)} %pad_maximum_fusion.3.refs_2_, ...), custom_call_target="tpu_custom_call" | custom-call | tf_op jit(solution)/shard_map/assemble/pallas_call | solution.py:315
  746.6 4.4 convert_element_type.320
  754.5 64.5 %collective-permute-done.14 = bf16[256,2048]{1,0:T(8,128)(2,1)} collective-permute-done((bf16[256,2048]{1,0:T(8,128)(2,1)}, bf16[256,2048]{1,0:T(8,128)(2,1)}, u32[]{:S(2)}, u32[]{:S(2)}) %collective-permute-start.14) | collective-permute-done | bytes 1048608 | tf_op jit(solution)/shard_map/ppermute | solution.py:172
  819.6 6.3 fusion.15
  826.8 8.9 %assemble.2 = f32[3,4,128,2048]{3,2,1,0:T(8,128)} custom-call(s32[9]{0:T(128)S(1)} %pad_add_fusion.table_ref, bf16[2,3,64,1024]{3,2,1,0:T(8,128)(2,1)S(1)} %pad_maximum_fusion.7.refs_0_, bf16[2,3,64,1024]{3,2,1,0:T(8,128)(2,1)} %collective-permute-done.46.refs_1_, bf16[2,3,64,1024]{3,2,1,0:T(8,128)(2,1)} %pad_maximum_fusion.8.refs_2_, ...), custom_call_target="tpu_custom_call" | custom-call | tf_op jit(solution)/shard_map/assemble/pallas_call | solution.py:315
  835.7 10.5 %place.1 = f32[1,4,128,8192]{3,2,1,0:T(8,128)} custom-call(bf16[8,4,128,1024]{3,2,1,0:T(8,128)(2,1)} %all-gather.14.cloned.1.call-done.x_ref), custom_call_target="tpu_custom_call" | custom-call | tf_op jit(solution)/shard_map/place/pallas_call | solution.py:343
  (399 shorter events, 135.7 us)
Async XLA Ops:
  7.2 222.2 %all-gather.6.cloned.1.call-start = ((), (), s32[]{:S(2)}) async-start(), calls=%async_computation.1 | async-start | bytes 7077888 | tf_op jit(solution)/shard_map/all_gather | solution.py:406
  8.6 14.5 %collective-permute-start.9 = (bf16[64,2048]{1,0:T(8,128)(2,1)S(1)}, bf16[64,2048]{1,0:T(8,128)(2,1)S(1)}, u32[]{:S(2)}, u32[]{:S(2)}) collective-permute-start(bf16[64,2048]{1,0:T(8,128)(2,1)S(1)} %get-tuple-element.83), channel_id=1, source_target_pairs={{0,2},{1,1},{2,0},{3,3},{4,6},{5,5},{6,4},{7,7},{8,10},{9,9},{10,8... | collective-permute-start | bytes 786440 | tf_op jit(solution)/shard_map/ppermute | solution.py:403
  14.5 11.9 %collective-permute-start.8 = (bf16[64,2048]{1,0:T(8,128)(2,1)S(1)}, bf16[64,2048]{1,0:T(8,128)(2,1)S(1)}, u32[]{:S(2)}, u32[]{:S(2)}) collective-permute-start(bf16[64,2048]{1,0:T(8,128)(2,1)S(1)} %get-tuple-element.82), channel_id=1, source_target_pairs={{0,1},{1,0},{2,3},{3,2},{4,5},{5,4},{6,7},{7,6},{8,9},{9,8},{10,11... | collective-permute-start | bytes 786440 | tf_op jit(solution)/shard_map/ppermute | solution.py:403
  14.6 11.8 %collective-permute-start.7 = (bf16[64,2048]{1,0:T(8,128)(2,1)S(1)}, bf16[64,2048]{1,0:T(8,128)(2,1)}, u32[]{:S(2)}, u32[]{:S(2)}) collective-permute-start(bf16[64,2048]{1,0:T(8,128)(2,1)S(1)} %get-tuple-element.81), channel_id=1, source_target_pairs={{0,0},{1,3},{2,2},{3,1},{4,4},{5,7},{6,6},{7,5},{8,8},{9,11},{10,1... | collective-permute-start | bytes 786440 | tf_op jit(solution)/shard_map/ppermute | solution.py:403
  28.6 235.0 %all-gather.8.cloned.1.call-start = ((), (), s32[]{:S(2)}) async-start(), calls=%async_computation.2 | async-start | bytes 9437184 | tf_op jit(solution)/shard_map/all_gather | solution.py:415
  37.0 12.8 %collective-permute-start.10 = (bf16[64,2560]{1,0:T(8,128)(2,1)}, bf16[64,2560]{1,0:T(8,128)(2,1)}, u32[]{:S(2)}, u32[]{:S(2)}) collective-permute-start(bf16[64,2560]{1,0:T(8,128)(2,1)} %bitcast.262), channel_id=1, source_target_pairs={{0,1},{1,2},{2,3},{3,0},{4,5},{5,6},{6,7},{7,4},{8,9},{9,10},{10,1... | collective-permute-start | bytes 983048 | tf_op jit(solution)/shard_map/ppermute | solution.py:172
  39.7 23.3 %collective-permute-start.11 = (bf16[64,2560]{1,0:T(8,128)(2,1)}, bf16[64,2560]{1,0:T(8,128)(2,1)}, u32[]{:S(2)}, u32[]{:S(2)}) collective-permute-start(bf16[64,2560]{1,0:T(8,128)(2,1)} %bitcast.261), channel_id=1, source_target_pairs={{0,2},{1,3},{2,0},{3,1},{4,6},{5,7},{6,4},{7,5},{8,10},{9,11},{10,... | collective-permute-start | bytes 983048 | tf_op jit(solution)/shard_map/ppermute | solution.py:172
  42.8 21.2 %collective-permute-start.12 = (bf16[64,2560]{1,0:T(8,128)(2,1)}, bf16[64,2560]{1,0:T(8,128)(2,1)S(1)}, u32[]{:S(2)}, u32[]{:S(2)}) collective-permute-start(bf16[64,2560]{1,0:T(8,128)(2,1)} %bitcast.260), channel_id=1, source_target_pairs={{0,3},{1,0},{2,1},{3,2},{4,7},{5,4},{6,5},{7,6},{8,11},{9,8},{10,9... | collective-permute-start | bytes 983048 | tf_op jit(solution)/shard_map/ppermute | solution.py:172
  65.2 213.3 %all-gather.10.cloned.1.call-start = ((), (), s32[]{:S(2)}) async-start(), calls=%async_computation.3 | async-start | bytes 2359296 | tf_op jit(solution)/shard_map/all_gather | solution.py:416
  66.2 23.3 %collective-permute-start = (bf16[3584]{0:T(1024)(128)(2,1)S(1)}, bf16[3584]{0:T(1024)(128)(2,1)S(1)}, u32[]{:S(2)}, u32[]{:S(2)}) collective-permute-start(bf16[3584]{0:T(1024)(128)(2,1)S(1)} %constant_dynamic-update-slice_fusion.9), channel_id=1, source_target_pairs={{0,1},{1,2},{2,3},{3,0},{4,5},{5,6},{6,7},{7,4},{8,9},{9,10},{10,1... | collective-permute-start | bytes 21512 | tf_op jit(solution)/shard_map/ppermute | solution.py:172
  72.6 17.0 %collective-permute-start.1 = (bf16[3584]{0:T(1024)(128)(2,1)S(1)}, bf16[3584]{0:T(1024)(128)(2,1)S(1)}, u32[]{:S(2)}, u32[]{:S(2)}) collective-permute-start(bf16[3584]{0:T(1024)(128)(2,1)S(1)} %constant_dynamic-update-slice_fusion.9), channel_id=1, source_target_pairs={{0,2},{1,3},{2,0},{3,1},{4,6},{5,7},{6,4},{7,5},{8,10},{9,11},{10,... | collective-permute-start | bytes 21512 | tf_op jit(solution)/shard_map/ppermute | solution.py:172
  73.3 16.5 %collective-permute-start.2 = (bf16[3584]{0:T(1024)(128)(2,1)S(1)}, bf16[3584]{0:T(1024)(128)(2,1)S(1)}, u32[]{:S(2)}, u32[]{:S(2)}) collective-permute-start(bf16[3584]{0:T(1024)(128)(2,1)S(1)} %constant_dynamic-update-slice_fusion.9), channel_id=1, source_target_pairs={{0,3},{1,0},{2,1},{3,2},{4,7},{5,4},{6,5},{7,6},{8,11},{9,8},{10,9... | collective-permute-start | bytes 21512 | tf_op jit(solution)/shard_map/ppermute | solution.py:172
  75.0 28.1 %collective-permute-start.16 = (bf16[256,2048]{1,0:T(8,128)(2,1)}, bf16[256,2048]{1,0:T(8,128)(2,1)}, u32[]{:S(2)}, u32[]{:S(2)}) collective-permute-start(bf16[256,2048]{1,0:T(8,128)(2,1)} %bitcast.273), channel_id=1, source_target_pairs={{0,1},{1,2},{2,3},{3,0},{4,5},{5,6},{6,7},{7,4},{8,9},{9,10},{10,1... | collective-permute-start | bytes 3145736 | tf_op jit(solution)/shard_map/ppermute | solution.py:172
  75.3 50.0 %collective-permute-start.17 = (bf16[256,2048]{1,0:T(8,128)(2,1)}, bf16[256,2048]{1,0:T(8,128)(2,1)}, u32[]{:S(2)}, u32[]{:S(2)}) collective-permute-start(bf16[256,2048]{1,0:T(8,128)(2,1)} %bitcast.274), channel_id=1, source_target_pairs={{0,3},{1,0},{2,1},{3,2},{4,7},{5,4},{6,5},{7,6},{8,11},{9,8},{10,9... | collective-permute-start | bytes 3145736 | tf_op jit(solution)/shard_map/ppermute | solution.py:172
  91.5 56.7 %collective-permute-start.3 = (bf16[256,2048]{1,0:T(8,128)(2,1)}, bf16[256,2048]{1,0:T(8,128)(2,1)}, u32[]{:S(2)}, u32[]{:S(2)}) collective-permute-start(bf16[256,2048]{1,0:T(8,128)(2,1)} %fusion.10), channel_id=1, source_target_pairs={{0,1},{1,2},{2,3},{3,0},{4,5},{5,6},{6,7},{7,4},{8,9},{9,10},{10,1... | collective-permute-start | bytes 3145736 | tf_op jit(solution)/shard_map/ppermute | solution.py:172
  91.5 78.8 %collective-permute-start.4 = (bf16[256,2048]{1,0:T(8,128)(2,1)}, bf16[256,2048]{1,0:T(8,128)(2,1)}, u32[]{:S(2)}, u32[]{:S(2)}) collective-permute-start(bf16[256,2048]{1,0:T(8,128)(2,1)} %fusion.10), channel_id=1, source_target_pairs={{0,3},{1,0},{2,1},{3,2},{4,7},{5,4},{6,5},{7,6},{8,11},{9,8},{10,9... | collective-permute-start | bytes 3145736 | tf_op jit(solution)/shard_map/ppermute | solution.py:172
  99.2 298.2 %reduce-scatter.2.cloned.1.call-start = ((), (), s32[]{:S(2)}) async-start(), calls=%async_computation.4 | async-start | bytes 2359296 | tf_op jit(solution)/shard_map/reduce_scatter | solution.py:469
  104.3 77.5 %collective-permute-start.18 = (bf16[128,2048]{1,0:T(8,128)(2,1)S(1)}, bf16[128,2048]{1,0:T(8,128)(2,1)S(1)}, u32[]{:S(2)}, u32[]{:S(2)}) collective-permute-start(bf16[128,2048]{1,0:T(8,128)(2,1)S(1)} %slice.213), channel_id=1, source_target_pairs={{0,1},{1,2},{2,3},{3,0},{4,5},{5,6},{6,7},{7,4},{8,9},{9,10},{10,1... | collective-permute-start | bytes 1572872 | tf_op jit(solution)/shard_map/ppermute | solution.py:172
  126.5 66.0 %collective-permute-start.19 = (bf16[128,2048]{1,0:T(8,128)(2,1)S(1)}, bf16[128,2048]{1,0:T(8,128)(2,1)S(1)}, u32[]{:S(2)}, u32[]{:S(2)}) collective-permute-start(bf16[128,2048]{1,0:T(8,128)(2,1)S(1)} %slice.214), channel_id=1, source_target_pairs={{0,3},{1,0},{2,1},{3,2},{4,7},{5,4},{6,5},{7,6},{8,11},{9,8},{10,9... | collective-permute-start | bytes 1572872 | tf_op jit(solution)/shard_map/ppermute | solution.py:172
  149.3 55.1 %collective-permute-start.5 = (bf16[128,2048]{1,0:T(8,128)(2,1)S(1)}, bf16[128,2048]{1,0:T(8,128)(2,1)S(1)}, u32[]{:S(2)}, u32[]{:S(2)}) collective-permute-start(bf16[128,2048]{1,0:T(8,128)(2,1)S(1)} %slice.206), channel_id=1, source_target_pairs={{0,1},{1,2},{2,3},{3,0},{4,5},{5,6},{6,7},{7,4},{8,9},{9,10},{10,1... | collective-permute-start | bytes 1572872 | tf_op jit(solution)/shard_map/ppermute | solution.py:172
  171.3 40.9 %collective-permute-start.6 = (bf16[128,2048]{1,0:T(8,128)(2,1)S(1)}, bf16[128,2048]{1,0:T(8,128)(2,1)S(1)}, u32[]{:S(2)}, u32[]{:S(2)}) collective-permute-start(bf16[128,2048]{1,0:T(8,128)(2,1)S(1)} %slice.207), channel_id=1, source_target_pairs={{0,3},{1,0},{2,1},{3,2},{4,7},{5,4},{6,5},{7,6},{8,11},{9,8},{10,9... | collective-permute-start | bytes 1572872 | tf_op jit(solution)/shard_map/ppermute | solution.py:172
  301.2 18.1 %collective-permute-start.20 = (bf16[2048,1024]{1,0:T(8,128)(2,1)}, bf16[2048,1024]{1,0:T(8,128)(2,1)}, u32[]{:S(2)}, u32[]{:S(2)}) collective-permute-start(bf16[2048,1024]{1,0:T(8,128)(2,1)} %convolution_convert_fusion.2), channel_id=1, source_target_pairs={{0,4},{4,0},{8,12},{12,8},{16,20},{20,16},{24,28},{28,24},{1,5},{5... | collective-permute-start | bytes 12582920 | tf_op jit(solution)/shard_map/ppermute | solution.py:247
  336.1 11.6 %collective-permute-start.21 = (bf16[2048,1024]{1,0:T(8,128)(2,1)}, bf16[2048,1024]{1,0:T(8,128)(2,1)}, u32[]{:S(2)}, u32[]{:S(2)}) collective-permute-start(bf16[2048,1024]{1,0:T(8,128)(2,1)} %convolution_convert_fusion.1), channel_id=1, source_target_pairs={{0,4},{4,0},{8,12},{12,8},{16,20},{20,16},{24,28},{28,24},{1,5},{5... | collective-permute-start | bytes 12582920 | tf_op jit(solution)/shard_map/ppermute | solution.py:247
  336.6 409.9 %all-gather.12.cloned.1.call-start = ((), (), s32[]{:S(2)}) async-start(), calls=%async_computation.5 | async-start | bytes 2359296 | tf_op jit(solution)/shard_map/all_gather | solution.py:523
  344.2 69.4 %collective-permute-start.24 = (bf16[4,128,1024]{2,1,0:T(8,128)(2,1)}, bf16[4,128,1024]{2,1,0:T(8,128)(2,1)S(1)}, u32[]{:S(2)}, u32[]{:S(2)}) collective-permute-start(bf16[4,128,1024]{2,1,0:T(8,128)(2,1)} %get-tuple-element.94), channel_id=1, source_target_pairs={{0,24},{4,28},{8,16},{12,20},{16,8},{20,12},{24,0},{28,4},{1,25},{... | collective-permute-start | bytes 3145736 | tf_op jit(solution)/shard_map/ppermute | solution.py:247
  346.7 67.0 %collective-permute-start.23 = (bf16[4,128,1024]{2,1,0:T(8,128)(2,1)}, bf16[4,128,1024]{2,1,0:T(8,128)(2,1)}, u32[]{:S(2)}, u32[]{:S(2)}) collective-permute-start(bf16[4,128,1024]{2,1,0:T(8,128)(2,1)} %get-tuple-element.95), channel_id=1, source_target_pairs={{0,16},{4,20},{8,24},{12,28},{16,0},{20,4},{24,8},{28,12},{1,17},{... | collective-permute-start | bytes 3145736 | tf_op jit(solution)/shard_map/ppermute | solution.py:247
  347.2 66.5 %collective-permute-start.22 = (bf16[4,128,1024]{2,1,0:T(8,128)(2,1)S(1)}, bf16[4,128,1024]{2,1,0:T(8,128)(2,1)}, u32[]{:S(2)}, u32[]{:S(2)}) collective-permute-start(bf16[4,128,1024]{2,1,0:T(8,128)(2,1)S(1)} %get-tuple-element.93), channel_id=1, source_target_pairs={{0,8},{4,12},{8,0},{12,4},{16,24},{20,28},{24,16},{28,20},{1,9},{5... | collective-permute-start | bytes 3145736 | tf_op jit(solution)/shard_map/ppermute | solution.py:247
  399.9 7.4 collective-permute-start.57
  413.6 422.1 %all-gather.14.cloned.1.call-start = ((), (), s32[]{:S(2)}) async-start(), calls=%async_computation.6 | async-start | bytes 9437184 | tf_op jit(solution)/shard_map/all_gather | solution.py:495
  430.1 11.1 %collective-permute-start.67 = (bf16[128,1024]{1,0:T(8,128)(2,1)S(1)}, bf16[128,1024]{1,0:T(8,128)(2,1)S(1)}, u32[]{:S(2)}, u32[]{:S(2)}) collective-permute-start(bf16[128,1024]{1,0:T(8,128)(2,1)S(1)} %get-tuple-element.108), channel_id=1, source_target_pairs={{0,1},{1,2},{2,3},{3,0},{4,5},{5,6},{6,7},{7,4},{8,9},{9,10},{10,1... | collective-permute-start | bytes 786440 | tf_op jit(solution)/shard_map/ppermute | solution.py:172
  430.1 19.4 %collective-permute-start.68 = (bf16[128,1024]{1,0:T(8,128)(2,1)S(1)}, bf16[128,1024]{1,0:T(8,128)(2,1)S(1)}, u32[]{:S(2)}, u32[]{:S(2)}) collective-permute-start(bf16[128,1024]{1,0:T(8,128)(2,1)S(1)} %get-tuple-element.107), channel_id=1, source_target_pairs={{0,2},{1,3},{2,0},{3,1},{4,6},{5,7},{6,4},{7,5},{8,10},{9,11},{10,... | collective-permute-start | bytes 786440 | tf_op jit(solution)/shard_map/ppermute | solution.py:172
  434.1 15.5 %collective-permute-start.69 = (bf16[128,1024]{1,0:T(8,128)(2,1)S(1)}, bf16[128,1024]{1,0:T(8,128)(2,1)S(1)}, u32[]{:S(2)}, u32[]{:S(2)}) collective-permute-start(bf16[128,1024]{1,0:T(8,128)(2,1)S(1)} %get-tuple-element.106), channel_id=1, source_target_pairs={{0,3},{1,0},{2,1},{3,2},{4,7},{5,4},{6,5},{7,6},{8,11},{9,8},{10,9... | collective-permute-start | bytes 786440 | tf_op jit(solution)/shard_map/ppermute | solution.py:172
  485.3 69.7 %collective-permute-start.25 = (bf16[1536,1024]{1,0:T(8,128)(2,1)}, bf16[1536,1024]{1,0:T(8,128)(2,1)}, u32[]{:S(2)}, u32[]{:S(2)}) collective-permute-start(bf16[1536,1024]{1,0:T(8,128)(2,1)} %convolution_convert_fusion), channel_id=1, source_target_pairs={{0,4},{4,0},{8,12},{12,8},{16,20},{20,16},{24,28},{28,24},{1,5},{5... | collective-permute-start | bytes 9437192 | tf_op jit(solution)/shard_map/ppermute | solution.py:247
  486.9 41.8 %collective-permute-start.28 = (bf16[4,128,1024]{2,1,0:T(8,128)(2,1)}, bf16[4,128,1024]{2,1,0:T(8,128)(2,1)S(1)}, u32[]{:S(2)}, u32[]{:S(2)}) collective-permute-start(bf16[4,128,1024]{2,1,0:T(8,128)(2,1)} %get-tuple-element.91), channel_id=1, source_target_pairs={{0,24},{4,28},{8,16},{12,20},{16,8},{20,12},{24,0},{28,4},{1,25},{... | collective-permute-start | bytes 3145736 | tf_op jit(solution)/shard_map/ppermute | solution.py:247
  488.4 61.8 %collective-permute-start.27 = (bf16[4,128,1024]{2,1,0:T(8,128)(2,1)}, bf16[4,128,1024]{2,1,0:T(8,128)(2,1)S(1)}, u32[]{:S(2)}, u32[]{:S(2)}) collective-permute-start(bf16[4,128,1024]{2,1,0:T(8,128)(2,1)} %get-tuple-element.92), channel_id=1, source_target_pairs={{0,16},{4,20},{8,24},{12,28},{16,0},{20,4},{24,8},{28,12},{1,17},{... | collective-permute-start | bytes 3145736 | tf_op jit(solution)/shard_map/ppermute | solution.py:247
  489.8 60.5 %collective-permute-start.26 = (bf16[4,128,1024]{2,1,0:T(8,128)(2,1)S(1)}, bf16[4,128,1024]{2,1,0:T(8,128)(2,1)}, u32[]{:S(2)}, u32[]{:S(2)}) collective-permute-start(bf16[4,128,1024]{2,1,0:T(8,128)(2,1)S(1)} %get-tuple-element.90), channel_id=1, source_target_pairs={{0,8},{4,12},{8,0},{12,4},{16,24},{20,28},{24,16},{28,20},{1,9},{5... | collective-permute-start | bytes 3145736 | tf_op jit(solution)/shard_map/ppermute | solution.py:247
  552.9 25.6 %collective-permute-start.59 = (bf16[1,4,64,1024]{3,2,1,0:T(8,128)(2,1)S(1)}, bf16[1,4,64,1024]{3,2,1,0:T(8,128)(2,1)S(1)}, u32[]{:S(2)}, u32[]{:S(2)}) collective-permute-start(bf16[1,4,64,1024]{3,2,1,0:T(8,128)(2,1)S(1)} %get-tuple-element.110), channel_id=1, source_target_pairs={{0,8},{4,12},{8,0},{12,4},{16,24},{20,28},{24,16},{28,20},{1,9},{5... | collective-permute-start | bytes 1572872 | tf_op jit(solution)/shard_map/ppermute | solution.py:247
  554.3 39.5 %collective-permute-start.61 = (bf16[1,4,64,1024]{3,2,1,0:T(8,128)(2,1)S(1)}, bf16[1,4,64,1024]{3,2,1,0:T(8,128)(2,1)S(1)}, u32[]{:S(2)}, u32[]{:S(2)}) collective-permute-start(bf16[1,4,64,1024]{3,2,1,0:T(8,128)(2,1)S(1)} %get-tuple-element.109), channel_id=1, source_target_pairs={{0,16},{4,20},{8,24},{12,28},{16,0},{20,4},{24,8},{28,12},{1,17},{... | collective-permute-start | bytes 1572872 | tf_op jit(solution)/shard_map/ppermute | solution.py:247
  573.1 7.1 collective-permute-start.33
  578.6 40.7 %collective-permute-start.60 = (bf16[2,4,64,1024]{3,2,1,0:T(8,128)(2,1)S(1)}, bf16[2,4,64,1024]{3,2,1,0:T(8,128)(2,1)S(1)}, u32[]{:S(2)}, u32[]{:S(2)}) collective-permute-start(bf16[2,4,64,1024]{3,2,1,0:T(8,128)(2,1)S(1)} %pad_maximum_fusion.2.refs_0_), channel_id=1, source_target_pairs={{0,16},{4,20},{8,24},{12,28},{16,0},{20,4},{24,8},{28,12},{1,17},{... | collective-permute-start | bytes 3145736 | tf_op jit(solution)/shard_map/ppermute | solution.py:247
  584.0 44.6 %collective-permute-start.29 = (bf16[128,2048]{1,0:T(8,128)(2,1)}, bf16[128,2048]{1,0:T(8,128)(2,1)}, u32[]{:S(2)}, u32[]{:S(2)}) collective-permute-start(bf16[128,2048]{1,0:T(8,128)(2,1)} %get-tuple-element.86), channel_id=1, source_target_pairs={{0,1},{1,2},{2,3},{3,0},{4,5},{5,6},{6,7},{7,4},{8,9},{9,10},{10,1... | collective-permute-start | bytes 1572872 | tf_op jit(solution)/shard_map/ppermute | solution.py:172
  584.5 44.2 %collective-permute-start.31 = (bf16[128,2048]{1,0:T(8,128)(2,1)}, bf16[128,2048]{1,0:T(8,128)(2,1)}, u32[]{:S(2)}, u32[]{:S(2)}) collective-permute-start(bf16[128,2048]{1,0:T(8,128)(2,1)} %get-tuple-element.88), channel_id=1, source_target_pairs={{0,3},{1,0},{2,1},{3,2},{4,7},{5,4},{6,5},{7,6},{8,11},{9,8},{10,9... | collective-permute-start | bytes 1572872 | tf_op jit(solution)/shard_map/ppermute | solution.py:172
  591.7 38.8 %collective-permute-start.41 = (bf16[3,128,1024]{2,1,0:T(8,128)(2,1)}, bf16[3,128,1024]{2,1,0:T(8,128)(2,1)}, u32[]{:S(2)}, u32[]{:S(2)}) collective-permute-start(bf16[3,128,1024]{2,1,0:T(8,128)(2,1)} %get-tuple-element.100), channel_id=1, source_target_pairs={{0,24},{4,28},{8,16},{12,20},{16,8},{20,12},{24,0},{28,4},{1,25},{... | collective-permute-start | bytes 2359304 | tf_op jit(solution)/shard_map/ppermute | solution.py:247
  593.8 27.2 %collective-permute-start.38 = (f32[5120]{0:T(1024)S(1)}, f32[5120]{0:T(1024)S(1)}, u32[]{:S(2)}, u32[]{:S(2)}) collective-permute-start(f32[5120]{0:T(1024)S(1)} %add.472), channel_id=1, source_target_pairs={{0,16},{4,20},{8,24},{12,28},{16,0},{20,4},{24,8},{28,12},{1,17},{... | collective-permute-start | bytes 61448 | tf_op jit(solution)/shard_map/ppermute | solution.py:247
  619.2 17.3 %collective-permute-start.40 = (bf16[3,128,1024]{2,1,0:T(8,128)(2,1)}, bf16[3,128,1024]{2,1,0:T(8,128)(2,1)}, u32[]{:S(2)}, u32[]{:S(2)}) collective-permute-start(bf16[3,128,1024]{2,1,0:T(8,128)(2,1)} %get-tuple-element.101), channel_id=1, source_target_pairs={{0,16},{4,20},{8,24},{12,28},{16,0},{20,4},{24,8},{28,12},{1,17},{... | collective-permute-start | bytes 2359304 | tf_op jit(solution)/shard_map/ppermute | solution.py:247
  620.9 20.7 %collective-permute-start.39 = (bf16[3,128,1024]{2,1,0:T(8,128)(2,1)}, bf16[3,128,1024]{2,1,0:T(8,128)(2,1)}, u32[]{:S(2)}, u32[]{:S(2)}) collective-permute-start(bf16[3,128,1024]{2,1,0:T(8,128)(2,1)} %get-tuple-element.99), channel_id=1, source_target_pairs={{0,8},{4,12},{8,0},{12,4},{16,24},{20,28},{24,16},{28,20},{1,9},{5... | collective-permute-start | bytes 2359304 | tf_op jit(solution)/shard_map/ppermute | solution.py:247
  628.6 32.4 %collective-permute-start.63 = (bf16[2,4,64,1024]{3,2,1,0:T(8,128)(2,1)S(1)}, bf16[2,4,64,1024]{3,2,1,0:T(8,128)(2,1)S(1)}, u32[]{:S(2)}, u32[]{:S(2)}) collective-permute-start(bf16[2,4,64,1024]{3,2,1,0:T(8,128)(2,1)S(1)} %pad_maximum_fusion.2.refs_0_), channel_id=1, source_target_pairs={{0,4},{4,0},{8,12},{12,8},{16,20},{20,16},{24,28},{28,24},{1,5},{5... | collective-permute-start | bytes 3145736 | tf_op jit(solution)/shard_map/ppermute | solution.py:247
  628.7 31.7 %collective-permute-start.62 = (bf16[2,4,64,1024]{3,2,1,0:T(8,128)(2,1)S(1)}, bf16[2,4,64,1024]{3,2,1,0:T(8,128)(2,1)S(1)}, u32[]{:S(2)}, u32[]{:S(2)}) collective-permute-start(bf16[2,4,64,1024]{3,2,1,0:T(8,128)(2,1)S(1)} %pad_maximum_fusion.3.refs_2_), channel_id=1, source_target_pairs={{0,8},{4,12},{8,0},{12,4},{16,24},{20,28},{24,16},{28,20},{1,9},{5... | collective-permute-start | bytes 3145736 | tf_op jit(solution)/shard_map/ppermute | solution.py:247
  630.4 31.4 %collective-permute-start.65 = (bf16[2,4,64,1024]{3,2,1,0:T(8,128)(2,1)S(1)}, bf16[2,4,64,1024]{3,2,1,0:T(8,128)(2,1)S(1)}, u32[]{:S(2)}, u32[]{:S(2)}) collective-permute-start(bf16[2,4,64,1024]{3,2,1,0:T(8,128)(2,1)S(1)} %pad_maximum_fusion.3.refs_2_), channel_id=1, source_target_pairs={{0,4},{4,0},{8,12},{12,8},{16,20},{20,16},{24,28},{28,24},{1,5},{5... | collective-permute-start | bytes 3145736 | tf_op jit(solution)/shard_map/ppermute | solution.py:247
  636.5 39.3 %collective-permute-start.64 = (bf16[2,4,64,1024]{3,2,1,0:T(8,128)(2,1)S(1)}, bf16[2,4,64,1024]{3,2,1,0:T(8,128)(2,1)S(1)}, u32[]{:S(2)}, u32[]{:S(2)}) collective-permute-start(bf16[2,4,64,1024]{3,2,1,0:T(8,128)(2,1)S(1)} %collective-permute-done.60.refs_1_), channel_id=1, source_target_pairs={{0,4},{4,0},{8,12},{12,8},{16,20},{20,16},{24,28},{28,24},{1,5},{5... | collective-permute-start | bytes 3145736 | tf_op jit(solution)/shard_map/ppermute | solution.py:247
  644.3 23.9 %collective-permute-start.44 = (bf16[128,1024]{1,0:T(8,128)(2,1)S(1)}, bf16[128,1024]{1,0:T(8,128)(2,1)S(1)}, u32[]{:S(2)}, u32[]{:S(2)}) collective-permute-start(bf16[128,1024]{1,0:T(8,128)(2,1)S(1)} %get-tuple-element.116), channel_id=1, source_target_pairs={{2,0},{1,1},{0,2},{3,3},{6,4},{5,5},{4,6},{7,7},{10,8},{9,9},{8,10... | collective-permute-start | bytes 786440 | tf_op jit(solution)/shard_map/ppermute | solution.py:517
  660.4 7.8 collective-permute-start.43
  661.0 11.4 %collective-permute-start.42 = (bf16[128,1024]{1,0:T(8,128)(2,1)S(1)}, bf16[128,1024]{1,0:T(8,128)(2,1)S(1)}, u32[]{:S(2)}, u32[]{:S(2)}) collective-permute-start(bf16[128,1024]{1,0:T(8,128)(2,1)S(1)} %get-tuple-element.115), channel_id=1, source_target_pairs={{0,0},{3,1},{2,2},{1,3},{4,4},{7,5},{6,6},{5,7},{8,8},{11,9},{10,1... | collective-permute-start | bytes 786440 | tf_op jit(solution)/shard_map/ppermute | solution.py:517
  668.2 63.5 %collective-permute-start.66 = (bf16[2,4,64,1024]{3,2,1,0:T(8,128)(2,1)S(1)}, bf16[2,4,64,1024]{3,2,1,0:T(8,128)(2,1)S(1)}, u32[]{:S(2)}, u32[]{:S(2)}) collective-permute-start(bf16[2,4,64,1024]{3,2,1,0:T(8,128)(2,1)S(1)} %collective-permute-done.62.refs_3_), channel_id=1, source_target_pairs={{0,4},{4,0},{8,12},{12,8},{16,20},{20,16},{24,28},{28,24},{1,5},{5... | collective-permute-start | bytes 3145736 | tf_op jit(solution)/shard_map/ppermute | solution.py:247
  668.2 64.8 %collective-permute-start.32 = (bf16[256,2048]{1,0:T(8,128)(2,1)S(1)}, bf16[256,2048]{1,0:T(8,128)(2,1)S(1)}, u32[]{:S(2)}, u32[]{:S(2)}) collective-permute-start(bf16[256,2048]{1,0:T(8,128)(2,1)S(1)} %pad_maximum_fusion.1), channel_id=1, source_target_pairs={{0,3},{1,0},{2,1},{3,2},{4,7},{5,4},{6,5},{7,6},{8,11},{9,8},{10,9... | collective-permute-start | bytes 3145736 | tf_op jit(solution)/shard_map/ppermute | solution.py:172
  672.4 61.9 %collective-permute-start.30 = (bf16[256,2048]{1,0:T(8,128)(2,1)S(1)}, bf16[256,2048]{1,0:T(8,128)(2,1)S(1)}, u32[]{:S(2)}, u32[]{:S(2)}) collective-permute-start(bf16[256,2048]{1,0:T(8,128)(2,1)S(1)} %pad_maximum_fusion), channel_id=1, source_target_pairs={{0,1},{1,2},{2,3},{3,0},{4,5},{5,6},{6,7},{7,4},{8,9},{9,10},{10,1... | collective-permute-start | bytes 3145736 | tf_op jit(solution)/shard_map/ppermute | solution.py:172
  673.7 9.2 %collective-permute-start.45 = (bf16[1,3,64,1024]{3,2,1,0:T(8,128)(2,1)S(1)}, bf16[1,3,64,1024]{3,2,1,0:T(8,128)(2,1)S(1)}, u32[]{:S(2)}, u32[]{:S(2)}) collective-permute-start(bf16[1,3,64,1024]{3,2,1,0:T(8,128)(2,1)S(1)} %get-tuple-element.114), channel_id=1, source_target_pairs={{0,8},{4,12},{8,0},{12,4},{16,24},{20,28},{24,16},{28,20},{1,9},{5... | collective-permute-start | bytes 1179656 | tf_op jit(solution)/shard_map/ppermute | solution.py:247
  675.8 54.7 %collective-permute-start.47 = (bf16[1,3,64,1024]{3,2,1,0:T(8,128)(2,1)S(1)}, bf16[1,3,64,1024]{3,2,1,0:T(8,128)(2,1)S(1)}, u32[]{:S(2)}, u32[]{:S(2)}) collective-permute-start(bf16[1,3,64,1024]{3,2,1,0:T(8,128)(2,1)S(1)} %get-tuple-element.113), channel_id=1, source_target_pairs={{0,16},{4,20},{8,24},{12,28},{16,0},{20,4},{24,8},{28,12},{1,17},{... | collective-permute-start | bytes 1179656 | tf_op jit(solution)/shard_map/ppermute | solution.py:247
  683.0 71.5 %collective-permute-start.15 = (bf16[256,2048]{1,0:T(8,128)(2,1)}, bf16[256,2048]{1,0:T(8,128)(2,1)}, u32[]{:S(2)}, u32[]{:S(2)}) collective-permute-start(bf16[256,2048]{1,0:T(8,128)(2,1)} %get-tuple-element.97), channel_id=1, source_target_pairs={{0,3},{1,0},{2,1},{3,2},{4,7},{5,4},{6,5},{7,6},{8,11},{9,8},{10,9... | collective-permute-start | bytes 3145736 | tf_op jit(solution)/shard_map/ppermute | solution.py:172
  730.6 88.4 %collective-permute-start.14 = (bf16[256,2048]{1,0:T(8,128)(2,1)}, bf16[256,2048]{1,0:T(8,128)(2,1)}, u32[]{:S(2)}, u32[]{:S(2)}) collective-permute-start(bf16[256,2048]{1,0:T(8,128)(2,1)} %get-tuple-element.98), channel_id=1, source_target_pairs={{0,2},{1,3},{2,0},{3,1},{4,6},{5,7},{6,4},{7,5},{8,10},{9,11},{10,... | collective-permute-start | bytes 3145736 | tf_op jit(solution)/shard_map/ppermute | solution.py:172
  731.7 87.9 %collective-permute-start.13 = (bf16[256,2048]{1,0:T(8,128)(2,1)}, bf16[256,2048]{1,0:T(8,128)(2,1)}, u32[]{:S(2)}, u32[]{:S(2)}) collective-permute-start(bf16[256,2048]{1,0:T(8,128)(2,1)} %get-tuple-element.96), channel_id=1, source_target_pairs={{0,1},{1,2},{2,3},{3,0},{4,5},{5,6},{6,7},{7,4},{8,9},{9,10},{10,1... | collective-permute-start | bytes 3145736 | tf_op jit(solution)/shard_map/ppermute | solution.py:172
  733.0 85.9 %collective-permute-start.46 = (bf16[2,3,64,1024]{3,2,1,0:T(8,128)(2,1)S(1)}, bf16[2,3,64,1024]{3,2,1,0:T(8,128)(2,1)}, u32[]{:S(2)}, u32[]{:S(2)}) collective-permute-start(bf16[2,3,64,1024]{3,2,1,0:T(8,128)(2,1)S(1)} %pad_maximum_fusion.7.refs_0_), channel_id=1, source_target_pairs={{0,16},{4,20},{8,24},{12,28},{16,0},{20,4},{24,8},{28,12},{1,17},{... | collective-permute-start | bytes 2359304 | tf_op jit(solution)/shard_map/ppermute | solution.py:247
  734.3 85.1 %collective-permute-start.48 = (bf16[2,3,64,1024]{3,2,1,0:T(8,128)(2,1)}, bf16[2,3,64,1024]{3,2,1,0:T(8,128)(2,1)}, u32[]{:S(2)}, u32[]{:S(2)}) collective-permute-start(bf16[2,3,64,1024]{3,2,1,0:T(8,128)(2,1)} %pad_maximum_fusion.8.refs_2_), channel_id=1, source_target_pairs={{0,8},{4,12},{8,0},{12,4},{16,24},{20,28},{24,16},{28,20},{1,9},{5... | collective-permute-start | bytes 2359304 | tf_op jit(solution)/shard_map/ppermute | solution.py:247
  754.5 71.4 %collective-permute-start.49 = (bf16[2,3,64,1024]{3,2,1,0:T(8,128)(2,1)S(1)}, bf16[2,3,64,1024]{3,2,1,0:T(8,128)(2,1)S(1)}, u32[]{:S(2)}, u32[]{:S(2)}) collective-permute-start(bf16[2,3,64,1024]{3,2,1,0:T(8,128)(2,1)S(1)} %pad_maximum_fusion.7.refs_0_), channel_id=1, source_target_pairs={{0,4},{4,0},{8,12},{12,8},{16,20},{20,16},{24,28},{28,24},{1,5},{5... | collective-permute-start | bytes 2359304 | tf_op jit(solution)/shard_map/ppermute | solution.py:247
  (74 other events, 1429.0 us)
Sparse Core Ops, SparseCore 0:
  28.7 46.6 all-gather.5
  77.9 54.2 all-gather.7
  134.1 27.7 all-gather.9
  336.7 60.5 reduce-scatter.1
  413.7 27.7 all-gather.11
  450.8 92.8 all-gather.13
